TPU v7x, 256 devices: a whole 4x4x8 slice. The times are simulated.
256 devices in a mesh: dp: 16 (over z, core), seq: 16 (over y, x).
Axes of the slice: x: 4, y: 4, z: 8, core: 2. Of those that a mesh axis runs over, the one named last changes fastest.
Arguments:
- patches: bfloat16 [12288, 6144], P(('dp', 'seq')), may hold values from -12 to 12
- destination: int32 [12288, 1], P(('dp', 'seq')), may hold values from 0 to 15; in each aligned block of 48 rows (0 to 47, 48 to 95, ...) at most 4 rows name the same one
- segments: int32 [16, 1024], P('dp'), may hold values from 0 to 7, never falling along the last dimension, each value on 1 to 256 neighbouring positions
- qkv_weight: bfloat16 [6144, 3, 4096], P(None, None, 'seq'), may hold values from -2 to 2
- cotangent: bfloat16 [16, 1024, 4096], P('dp', None, 'seq'), may hold values from -6 to 6
Outputs:
- attended: bfloat16 [16, 1024, 4096], P('dp', None, 'seq')
- dproj: bfloat16 [16, 1024, 3, 4096], P('dp', None, None, 'seq')
Inputs may be any that keep to these rules, and one draw needn't show every extreme that they name: `destination`: the rows of one loader device name one pack at most 4 times. `segments`: image ids never fall along a pack; one image holds 1 to 256 slots.
All inputs are finite; a program needn't handle non-finite values.
Results may differ from a plain program's by a relative error of at most 0.009.
The roundings to bfloat16 on the way count: a program that leaves them out, or rounds other values in their place, can miss the bound.
Values may be sent and summed in bfloat16 or wider, within the bound.
No kernel may reach another device: no remote copies, remote signals or barrier semaphores. Data moves between devices by JAX's collectives and lax.ppermute only.
A program may use at most 128 MiB of HBM per device.

v0:
```python
import jax
import jax.numpy as jnp
from jax import lax
from jax.sharding import PartitionSpec as P

HD = 128


mask_fill = -1000000000.0


def send_buffers(patches, destination, owners, capacity):
    target = destination[:, 0]
    onehot = (target[:, None] == jnp.arange(owners, dtype=jnp.int32)[None, :]).astype(jnp.int32)
    before = jnp.cumsum(onehot, axis=0) - onehot
    rank_row = jnp.sum(before * onehot, axis=1)
    slot_row = target * capacity + rank_row
    select = (jnp.arange(owners * capacity, dtype=jnp.int32)[:, None] == slot_row[None, :]).astype(
        jnp.bfloat16
    )
    buffer = jnp.dot(select, patches, preferred_element_type=jnp.float32).astype(jnp.bfloat16)
    filled = jnp.sum(select.astype(jnp.float32), axis=1).astype(jnp.bfloat16)
    return (buffer.reshape(owners, capacity, patches.shape[1]), filled.reshape(owners, capacity))


def per_device(patches, destination, segments, qkv_weight, cotangent):
    owners = lax.axis_size("dp")
    width_in = patches.shape[1]
    capacity = patches.shape[0] * 4 // 3 // owners
    buffer, filled = send_buffers(patches, destination, owners, capacity)
    own_rows, own_live = (
        lax.all_to_all(buffer, "dp", split_axis=0, concat_axis=0, tiled=True),
        lax.all_to_all(filled, "dp", split_axis=0, concat_axis=0, tiled=True),
    )
    packed, live = (
        lax.all_gather(own_rows.reshape(-1, width_in), "seq", axis=0, tiled=True),
        lax.all_gather(own_live.reshape(-1), "seq", axis=0, tiled=True),
    )
    pack_len = packed.shape[0]
    head_cols = qkv_weight.shape[2]
    heads_here = head_cols // HD
    flat_weight = qkv_weight.reshape(width_in, 3 * head_cols)
    projected = jnp.dot(packed, flat_weight, preferred_element_type=jnp.float32).astype(
        jnp.bfloat16
    )
    projected = projected.reshape(pack_len, 3, heads_here, HD)
    queries = projected[:, 0]
    keys_all = projected[:, 1]
    values = projected[:, 2]
    seg_row = segments[0]
    grad_out = (cotangent[0] * live[:, None]).reshape(pack_len, heads_here, HD)
    block = min(512, pack_len)
    scale = HD ** (-0.5)

    def attend(carry, index):
        key_grad, value_grad = carry
        q_start = index * block
        query_blk = lax.dynamic_slice_in_dim(queries, q_start, block, 0)
        seg_query = lax.dynamic_slice_in_dim(seg_row, q_start, block, 0)
        live_query = lax.dynamic_slice_in_dim(live, q_start, block, 0)
        scores = (
            jnp.einsum("qhd,khd->hqk", query_blk, keys_all, preferred_element_type=jnp.float32)
            * scale
        )
        allowed = (seg_query[:, None] == seg_row[None, :]) & (live[None, :] > 0)
        scores = jnp.where(allowed[None], scores, mask_fill)
        top = jnp.max(scores, axis=2, keepdims=True)
        expo = jnp.exp(scores - top)
        probs = expo / jnp.sum(expo, axis=2, keepdims=True)
        probs_low = probs.astype(jnp.bfloat16)
        context = jnp.einsum("hqk,khd->qhd", probs_low, values, preferred_element_type=jnp.float32)
        out_blk = (context * live_query.astype(jnp.float32)[:, None, None]).astype(jnp.bfloat16)
        grad_blk = lax.dynamic_slice_in_dim(grad_out, q_start, block, 0)
        row_delta = jnp.sum(grad_blk.astype(jnp.float32) * context, axis=2)
        prob_grad = jnp.einsum("qhd,khd->hqk", grad_blk, values, preferred_element_type=jnp.float32)
        score_grad = (probs * (prob_grad - row_delta.T[:, :, None])).astype(jnp.bfloat16)
        query_grad = (
            jnp.einsum("hqk,khd->qhd", score_grad, keys_all, preferred_element_type=jnp.float32)
            * scale
        ).astype(jnp.bfloat16)
        key_part = jnp.einsum(
            "hqk,qhd->khd", score_grad, query_blk, preferred_element_type=jnp.float32
        )
        value_part = jnp.einsum(
            "hqk,qhd->khd", probs_low, grad_blk, preferred_element_type=jnp.float32
        )
        key_grad = key_grad + key_part
        value_grad = value_grad + value_part
        return ((key_grad, value_grad), (out_blk, query_grad))

    zeros_grad = jnp.zeros((pack_len, heads_here, HD), jnp.float32)
    steps_count = jnp.arange(pack_len // block, dtype=jnp.int32)
    (key_grad, value_grad), (outputs, query_grads) = lax.scan(
        attend, (zeros_grad, zeros_grad), steps_count
    )
    key_low = (key_grad * scale).astype(jnp.bfloat16)
    value_low = value_grad.astype(jnp.bfloat16)
    query_low = query_grads.reshape(pack_len, heads_here, HD)
    grad_proj = jnp.stack([query_low, key_low, value_low], axis=1).reshape(
        1, pack_len, 3, head_cols
    )
    attended_all = outputs.reshape(1, pack_len, head_cols)
    return (attended_all, grad_proj)


def solution(mesh):
    in_specs = (
        P(("dp", "seq"), None),
        P(("dp", "seq"), None),
        P("dp", None),
        P(None, None, "seq"),
        P("dp", None, "seq"),
    )
    out_specs = (P("dp", None, "seq"), P("dp", None, None, "seq"))
    return jax.shard_map(
        per_device, mesh=mesh, in_specs=in_specs, out_specs=out_specs, check_vma=False
    )
```

profile of v0, /device:TPU:1, one launch (start us, length us, event | category | flops | bytes accessed | tf_op | source)
XLA Modules:
  0.0 217.8 jit_solution(10197379233664856477)
XLA Ops:
  7.2 0.0 all-gather.2.cloned.1.call-start
  7.2 0.8 fusion.28
  8.0 0.1 reduce_window_sum.11
  8.1 0.8 select_reduce_fusion
  8.9 0.7 multiply_add_fusion
  9.6 0.5 convolution_convert_fusion
  10.1 0.3 reshape.103
  10.4 32.7 %all_to_all.15 = bf16[16,4,6144]{2,1,0:T(4,128)(2,1)S(1)} all-to-all(bf16[16,4,6144]{2,1,0:T(4,128)(2,1)S(1)} %reshape.103), channel_id=1, replica_groups=mesh['dp'=16,'seq'=16] {'dp'}, dimensions={0} | all-to-all | bytes 1572864 | tf_op jit(solution)/shard_map/all_to_all | solution.py:32
  43.1 1.1 reshape.104
  44.1 0.0 all-gather.2.cloned.1.call-update
  44.2 0.1 fusion.30
  44.3 0.7 all_to_all.12
  45.0 3.4 %all-to-all-start.1 = ((bf16[16,1,4]{2,1,0:T(2,128)(2,1)}), bf16[16,1,4]{2,1,0:T(2,128)(2,1)S(1)}, u32[]{:S(2)}, u32[]{:S(2)}) async-start(bf16[16,1,4]{2,1,0:T(2,128)(2,1)} %all_to_all.12), calls=%async_computation.1 | async-start | bytes 16384 | tf_op jit(solution)/shard_map/all_to_all | solution.py:33
  48.4 12.6 %copy.46 = bf16[6144,3,256]{0,2,1:T(8,128)(2,1)} copy(bf16[6144,3,256]{2,0,1:T(8,128)(2,1)} %param.10) | data formatting | bytes 18874368 | tf_op args[3]
  61.0 0.2 copy.50
  61.2 0.6 dynamic-slice
  62.5 0.1 reshape.109
  62.6 0.2 dynamic-update-slice
  62.9 34.0 %all-reduce = bf16[1024]{0:T(1024)(128)(2,1)S(1)} all-reduce(bf16[1024]{0:T(1024)(128)(2,1)S(1)} %dynamic-update-slice), channel_id=1, replica_groups=mesh['dp'=16,'seq'=16] {'seq'}, use_global_device_ids=true, to_apply=%add | all-reduce | flops 1024 | bytes 4096
  96.9 39.5 %all-gather.2.cloned.1.call-done = bf16[1024,6144]{1,0:T(8,128)(2,1)} async-done(((bf16[64,6144]{1,0:T(8,128)(2,1)}), bf16[1024,6144]{1,0:T(8,128)(2,1)}) %all-gather.2.cloned.1.call-update) | async-done | bytes 12582928 | tf_op jit(solution)/shard_map/all_gather | solution.py:36
  136.5 14.5 %convolution_convert_fusion.1 = bf16[1024,768]{0,1:T(8,128)(2,1)S(1)} fusion(bf16[1024,6144]{1,0:T(8,128)(2,1)} %all-gather.2.cloned.1.call-done, bf16[6144,768]{0,1:T(8,128)(2,1)} %bitcast.84), kind=kOutput, calls=%fused_computation.38 | convolution fusion | flops 9664462848 | bytes 23592960 | tf_op jit(solution)/shard_map/dot_general | solution.py:43
  151.0 1.0 slice_bitcast_fusion
  152.0 1.0 copy.67
  153.0 1.0 copy.68
  154.0 51.0 %while.17 = (s32[]{:T(128)}, f32[1024,2,128]{0,2,1:T(8,128)}, f32[1024,2,128]{0,2,1:T(8,128)}, bf16[2,512,2,128]{3,2,1,0:T(2,128)(2,1)}, bf16[2,512,2,128]{3,2,1...) while((s32[]{:T(128)}, f32[1024,2,128]{0,2,1:T(8,128)}, ...), condition=%wide.region_7.8_spmd.clone, body=%wide.region_3.7_spmd.clone.sunk | while | flops 1624114688 | bytes 57449916 | solution.py:93
  154.1 0.7 dynamic_slice.47
  155.4 0.1 dynamic_slice.48
  155.5 0.4 compare_and_fusion.2
  155.9 4.7 %fusion.81 = (f32[2,512]{1,0:T(2,128)S(1)}, f32[2,512,1024]{2,1,0:T(8,128)}) fusion(pred[512,1024]{1,0:T(8,128)(4,1)S(1)} %compare_and_fusion.2, bf16[1024,2,128]{2,0,1:T(8,128)(2,1)} %get-tuple-element.327, bf16[1024,2,128]{2,0,1:T(8,128)(2,1)} %get-tuple-element.323, s32[]{:T(128)S(6)} %select_n.25), kind=kOutput, calls=%fused_computation.51.clone.1 | convolution fusion | flops 272630784 | bytes 5509124 | tf_op jit(solution)/shard_map/while/body/eval_jaxpr/sub | solution.py:68
  160.6 2.7 %fusion.82 = bf16[2,512,1024]{2,1,0:T(8,128)(2,1)S(1)} fusion(f32[2,512,1024]{2,1,0:T(8,128)} %get-tuple-element.277, f32[2,512]{1,0:T(2,128)S(1)} %get-tuple-element.278), kind=kLoop, calls=%fused_computation.10.clone.1 | loop fusion | flops 2097152 | bytes 6295552 | tf_op jit(solution)/shard_map/while/body/eval_jaxpr/convert_element_type | solution.py:70
  163.4 0.2 copy.75
  163.6 0.1 dynamic-slice_convert_fusion.2
  163.6 1.9 fusion.83
  165.5 3.3 %multiply_convert_fusion.4 = bf16[2,512,1024]{2,1,0:T(8,128)(2,1)S(1)} fusion(bf16[512,2,128]{0,2,1:T(8,128)(2,1)S(1)} %constant_dynamic-slice_fusion.2, bf16[1024,2,128]{0,2,1:T(8,128)(2,1)} %get-tuple-element.329, f32[2,512]{1,0:T(2,128)S(1)} %bitcast.95, f32[2,512,1024]{2,1,0:T(8,128)} %get-tuple-element.277, f32[2,512]{1,0:T(2,128)S(1)} %get-tuple-element.278), kind=kOutput, calls=%fused_computation.1.clone.1 | convolution fusion | flops 272629760 | bytes 7086080 | tf_op jit(solution)/shard_map/while/body/eval_jaxpr/qhd,khd->hqk/dot_general | solution.py:75
  168.8 1.3 copy-done.1
  170.2 1.8 fusion.86
  171.9 0.6 copy_dynamic-update-slice_fusion.3
  172.5 0.8 copy-done.6
  173.3 0.8 copy-done.9
  174.1 3.2 %fusion.84 = f32[1024,2,128]{0,2,1:T(8,128)} fusion(bf16[2,512,1024]{2,1,0:T(8,128)(2,1)} %copy-done.1, f32[1024,2,128]{0,2,1:T(8,128)} %get-tuple-element.301, pred[]{:T(512)S(6)} %compare.3, bf16[1024,2,128]{2,0,1:T(8,128)(2,1)} %get-tuple-element.323, s32[]{:T(128)S(6)} %select_n.25), kind=kOutput, calls=%fused_computation.13.clone.1 | convolution fusion | flops 268959744 | bytes 4456453 | tf_op jit(solution)/shard_map/while/body/eval_jaxpr/hqk,qhd->khd/dot_general | solution.py:81
  177.3 1.5 fusion.85
  178.8 0.7 dynamic_slice.47
  180.2 0.1 dynamic_slice.48
  180.3 0.4 compare_and_fusion.2
  180.7 4.7 %fusion.81 = (f32[2,512]{1,0:T(2,128)S(1)}, f32[2,512,1024]{2,1,0:T(8,128)}) fusion(pred[512,1024]{1,0:T(8,128)(4,1)S(1)} %compare_and_fusion.2, bf16[1024,2,128]{2,0,1:T(8,128)(2,1)} %get-tuple-element.327, bf16[1024,2,128]{2,0,1:T(8,128)(2,1)} %get-tuple-element.323, s32[]{:T(128)S(6)} %select_n.25), kind=kOutput, calls=%fused_computation.51.clone.1 | convolution fusion | flops 272630784 | bytes 5509124 | tf_op jit(solution)/shard_map/while/body/eval_jaxpr/sub | solution.py:68
  185.4 2.7 %fusion.82 = bf16[2,512,1024]{2,1,0:T(8,128)(2,1)S(1)} fusion(f32[2,512,1024]{2,1,0:T(8,128)} %get-tuple-element.277, f32[2,512]{1,0:T(2,128)S(1)} %get-tuple-element.278), kind=kLoop, calls=%fused_computation.10.clone.1 | loop fusion | flops 2097152 | bytes 6295552 | tf_op jit(solution)/shard_map/while/body/eval_jaxpr/convert_element_type | solution.py:70
  188.1 0.2 copy.75
  188.3 0.1 dynamic-slice_convert_fusion.2
  188.4 1.9 fusion.83
  190.3 3.3 %multiply_convert_fusion.4 = bf16[2,512,1024]{2,1,0:T(8,128)(2,1)S(1)} fusion(bf16[512,2,128]{0,2,1:T(8,128)(2,1)S(1)} %constant_dynamic-slice_fusion.2, bf16[1024,2,128]{0,2,1:T(8,128)(2,1)} %get-tuple-element.329, f32[2,512]{1,0:T(2,128)S(1)} %bitcast.95, f32[2,512,1024]{2,1,0:T(8,128)} %get-tuple-element.277, f32[2,512]{1,0:T(2,128)S(1)} %get-tuple-element.278), kind=kOutput, calls=%fused_computation.1.clone.1 | convolution fusion | flops 272629760 | bytes 7086080 | tf_op jit(solution)/shard_map/while/body/eval_jaxpr/qhd,khd->hqk/dot_general | solution.py:75
  193.6 1.3 copy-done.1
  194.9 1.8 fusion.86
  196.7 0.6 copy_dynamic-update-slice_fusion.3
  197.3 0.8 copy-done.6
  198.1 0.8 copy-done.9
  198.9 3.5 %fusion.84 = f32[1024,2,128]{0,2,1:T(8,128)} fusion(bf16[2,512,1024]{2,1,0:T(8,128)(2,1)} %copy-done.1, f32[1024,2,128]{0,2,1:T(8,128)} %get-tuple-element.301, pred[]{:T(512)S(6)} %compare.3, bf16[1024,2,128]{2,0,1:T(8,128)(2,1)} %get-tuple-element.323, s32[]{:T(128)S(6)} %select_n.25), kind=kOutput, calls=%fused_computation.13.clone.1 | convolution fusion | flops 268959744 | bytes 4456453 | tf_op jit(solution)/shard_map/while/body/eval_jaxpr/hqk,qhd->khd/dot_general | solution.py:81
  202.3 2.7 %fusion.85 = f32[1024,2,128]{0,2,1:T(8,128)} fusion(bf16[512,2,128]{0,2,1:T(8,128)(2,1)S(1)} %constant_dynamic-slice_fusion.2, bf16[2,512,1024]{2,1,0:T(8,128)(2,1)S(1)} %fusion.82, f32[1024,2,128]{0,2,1:T(8,128)} %get-tuple-element.302, pred[]{:T(512)S(6)} %compare.3), kind=kOutput, calls=%fused_computation.14.clone.1 | convolution fusion | flops 268959744 | bytes 4456449 | tf_op jit(solution)/shard_map/while/body/eval_jaxpr/hqk,qhd->khd/dot_general | solution.py:84
  205.0 1.4 multiply_convert_fusion.2
  206.4 0.2 copy.60
  206.7 1.3 convert_element_type.46
  208.0 0.2 copy.61
  208.2 0.3 stack.11
  208.5 1.1 reshape.108
  209.6 1.3 pad_maximum_fusion
  (47 shorter events, 0.2 us)
Async XLA Ops:
  7.2 2.4 %copy-start = (bf16[48,6144]{1,0:T(8,128)(2,1)S(1)}, bf16[48,6144]{1,0:T(8,128)(2,1)}, u32[]{:S(2)}) copy-start(bf16[48,6144]{1,0:T(8,128)(2,1)} %param.7) | copy-start | bytes 1769476
  7.2 129.3 %all-gather.2.cloned.1.call-start = ((), (), s32[]{:S(2)}) async-start(), calls=%async_computation.2 | async-start | bytes 13369344 | tf_op jit(solution)/shard_map/all_gather | solution.py:36
  45.0 17.5 %all-to-all-start.1 = ((bf16[16,1,4]{2,1,0:T(2,128)(2,1)}), bf16[16,1,4]{2,1,0:T(2,128)(2,1)S(1)}, u32[]{:S(2)}, u32[]{:S(2)}) async-start(bf16[16,1,4]{2,1,0:T(2,128)(2,1)} %all_to_all.12), calls=%async_computation.1 | async-start | bytes 16384 | tf_op jit(solution)/shard_map/all_to_all | solution.py:33
  48.4 12.6 %copy-start.4 = (bf16[1,1024,256]{2,1,0:T(8,128)(2,1)S(1)}, bf16[1,1024,256]{2,1,0:T(8,128)(2,1)}, u32[]{:S(2)}) copy-start(bf16[1,1024,256]{2,1,0:T(8,128)(2,1)} %param.11) | copy-start | bytes 1572868
  48.4 12.8 %copy-start.12 = (u32[256]{0:T(256)S(1)}, u32[256]{0:T(256)}, u32[]{:S(2)}) copy-start(u32[256]{0:T(256)} %constant.47) | copy-start | bytes 3076
  151.0 3.0 %copy-start.11 = (s32[1,1024]{1,0:T(1,128)S(1)}, s32[1,1024]{1,0:T(1,128)}, u32[]{:S(2)}) copy-start(s32[1,1024]{1,0:T(1,128)} %param.9) | copy-start | bytes 12292
  154.1 9.3 %copy-start.2 = (bf16[1024,2,128]{0,2,1:T(8,128)(2,1)}, bf16[1024,2,128]{0,2,1:T(8,128)(2,1)S(1)}, u32[]{:S(2)}) copy-start(bf16[1024,2,128]{0,2,1:T(8,128)(2,1)S(1)} %get-tuple-element.328) | copy-start | bytes 1572868 | tf_op jit(solution)/shard_map/while
  165.5 6.4 %copy-start.5 = (bf16[2,512,2,128]{3,2,1,0:T(2,128)(2,1)S(1)}, bf16[2,512,2,128]{3,2,1,0:T(2,128)(2,1)}, u32[]{:S(2)}) copy-start(bf16[2,512,2,128]{3,2,1,0:T(2,128)(2,1)} %get-tuple-element.303) | copy-start | bytes 1572868 | tf_op jit(solution)/shard_map/while
  165.5 6.4 %copy-start.8 = (bf16[2,512,2,128]{3,2,1,0:T(2,128)(2,1)S(1)}, bf16[2,512,2,128]{3,2,1,0:T(2,128)(2,1)}, u32[]{:S(2)}) copy-start(bf16[2,512,2,128]{3,2,1,0:T(2,128)(2,1)} %get-tuple-element.304) | copy-start | bytes 1572868 | tf_op jit(solution)/shard_map/while
  168.8 1.4 copy-start.1
  172.5 0.8 copy-start.6
  173.3 0.8 copy-start.9
  174.1 4.7 %copy-start.3 = (bf16[1024,2,128]{0,2,1:T(8,128)(2,1)S(1)}, bf16[1024,2,128]{0,2,1:T(8,128)(2,1)}, u32[]{:S(2)}) copy-start(bf16[1024,2,128]{0,2,1:T(8,128)(2,1)} %copy-done.2) | copy-start | bytes 1572868 | tf_op jit(solution)/shard_map/while
  178.8 9.3 %copy-start.2 = (bf16[1024,2,128]{0,2,1:T(8,128)(2,1)}, bf16[1024,2,128]{0,2,1:T(8,128)(2,1)S(1)}, u32[]{:S(2)}) copy-start(bf16[1024,2,128]{0,2,1:T(8,128)(2,1)S(1)} %get-tuple-element.328) | copy-start | bytes 1572868 | tf_op jit(solution)/shard_map/while
  190.3 6.4 %copy-start.5 = (bf16[2,512,2,128]{3,2,1,0:T(2,128)(2,1)S(1)}, bf16[2,512,2,128]{3,2,1,0:T(2,128)(2,1)}, u32[]{:S(2)}) copy-start(bf16[2,512,2,128]{3,2,1,0:T(2,128)(2,1)} %get-tuple-element.303) | copy-start | bytes 1572868 | tf_op jit(solution)/shard_map/while
  190.3 6.4 %copy-start.8 = (bf16[2,512,2,128]{3,2,1,0:T(2,128)(2,1)S(1)}, bf16[2,512,2,128]{3,2,1,0:T(2,128)(2,1)}, u32[]{:S(2)}) copy-start(bf16[2,512,2,128]{3,2,1,0:T(2,128)(2,1)} %get-tuple-element.304) | copy-start | bytes 1572868 | tf_op jit(solution)/shard_map/while
  193.5 1.4 copy-start.1
  197.3 0.8 copy-start.6
  198.1 0.8 copy-start.9
  198.9 6.2 %copy-start.3 = (bf16[1024,2,128]{0,2,1:T(8,128)(2,1)S(1)}, bf16[1024,2,128]{0,2,1:T(8,128)(2,1)}, u32[]{:S(2)}) copy-start(bf16[1024,2,128]{0,2,1:T(8,128)(2,1)} %copy-done.2) | copy-start | bytes 1572868 | tf_op jit(solution)/shard_map/while
  205.0 3.1 %copy-start.10 = (bf16[2,512,2,128]{3,2,1,0:T(2,128)(2,1)S(1)}, bf16[2,512,2,128]{3,2,1,0:T(2,128)(2,1)}, u32[]{:S(2)}) copy-start(bf16[2,512,2,128]{3,2,1,0:T(2,128)(2,1)} %get-tuple-element.73) | copy-start | bytes 1572868
  205.0 3.5 %copy-start.7 = (bf16[2,512,2,128]{3,2,1,0:T(2,128)(2,1)S(1)}, bf16[2,512,2,128]{3,2,1,0:T(2,128)(2,1)}, u32[]{:S(2)}) copy-start(bf16[2,512,2,128]{3,2,1,0:T(2,128)(2,1)} %get-tuple-element.72) | copy-start | bytes 1572868
Sparse Core Ops, SparseCore 0:
  44.3 92.1 all-gather.1
where the time goes:
time: 219 us; the launch traced here: 218 us
  blocking collectives  66.7 us (30%)
  matrix products  49 us (22%)
  waiting for transfers between devices  39.5 us (18%)
  local copies, waits for them, and re-layouts  29.8 us (14%)
  between operations  14.9 us (7%)
  other arithmetic  13 us (6%)
  starting transfers between devices  3.41 us (2%)
    all_gather x1, waiting for transfers between devices, per_device(): lax.all_gather(own_rows.reshape(-1, width_in), 'seq', axis=0, tiled=True)  39.5 us
    unnamed x1, blocking collectives  34 us
    all_to_all x1, blocking collectives, per_device(): lax.all_to_all(buffer, 'dp', split_axis=0, concat_axis=0, tiled=True)  32.7 us
    unnamed x19, local copies, waits for them, and re-layouts  15.7 us
    dot_general x1, matrix products, per_device(): jnp.dot(packed, flat_weight, preferred_element_type=jnp.float32)  14.5 us
    sub x2, matrix products, attend(): expo = jnp.exp(scores - top)  9.41 us
    dot_general x2, matrix products, attend(): jnp.einsum('hqk,qhd->khd', score_grad, query_blk, preferred_element_type=...  6.68 us
    dot_general x2, matrix products, attend(): jnp.einsum('qhd,khd->hqk', grad_blk, values, preferred_element_type=jnp.f...  6.54 us
  transfers between devices with their start and end apart: 2, of which 1 were waited for; matrix products, arithmetic and copies ran while one was open for 6% of the time, Pallas kernels for 0%

commit v1 on v0

v1 whole, which is shorter than its diff:
```python
import jax
import jax.numpy as jnp
from jax import lax
from jax.experimental import pallas as pl
from jax.experimental.pallas import tpu as pltpu
from jax.sharding import PartitionSpec as P

HD = 128
SIDE = 4
CAP = 4
FILL = -1000000000.0
EMPTY = 1.0e15
EDGE = 128

ROUNDS = (
    (((1, 0), (1, 0)), ((3, 0), (3, 0)), ((0, 1), (0, 1)), ((0, 3), (0, 3))),
    (((1, 1), (1, 0)), ((3, 1), (0, 1)), ((3, 3), (3, 0)), ((1, 3), (0, 3))),
    (((2, 1), (1, 0)), ((2, 3), (3, 0)), ((3, 2), (0, 1)), ((1, 2), (0, 3))),
    (((2, 0), (1, 0)), ((0, 2), (0, 1)), ((2, 2), (3, 0))),
)


def mark_rows(patches, destination):
    rows, width = patches.shape

    def body(x_ref, t_ref, o_ref):
        o_ref[:, :width] = x_ref[...]
        target = t_ref[...]
        owner = lax.broadcasted_iota(jnp.int32, (rows, EDGE), 1)
        onehot = (target == owner).astype(jnp.float32)
        r = lax.broadcasted_iota(jnp.int32, (rows, rows), 0)
        c = lax.broadcasted_iota(jnp.int32, (rows, rows), 1)
        lower = (c < r).astype(jnp.bfloat16)
        before = jnp.dot(lower, onehot.astype(jnp.bfloat16), preferred_element_type=jnp.float32)
        rank = jnp.sum(before * onehot, axis=1, keepdims=True)
        slot = target.astype(jnp.float32) * CAP + rank
        o_ref[:, width:] = jnp.broadcast_to(slot, (rows, EDGE)).astype(jnp.bfloat16)

    return pl.pallas_call(
        body,
        out_shape=jax.ShapeDtypeStruct((rows, width + EDGE), jnp.bfloat16),
        name="mark_rows",
    )(patches, destination)


def project(blocks, weight, owners):
    count = len(blocks)
    rows = blocks[0].shape[0]
    width, cols = weight.shape
    step = 1024
    steps = width // step
    slots = owners * CAP * count

    def body(*refs):
        x_refs = refs[:count]
        w_ref, o_ref, all_x, acc = refs[count:]
        k = pl.program_id(0)

        @pl.when(k == 0)
        def _():
            for i in range(count):
                for j in range(steps):
                    all_x[j, i * rows : (i + 1) * rows, :] = x_refs[i][:, j * step : (j + 1) * step]

        part = jnp.dot(all_x[k], w_ref[...], preferred_element_type=jnp.float32)

        @pl.when(k == 0)
        def _():
            acc[...] = part

        @pl.when(k > 0)
        def _():
            acc[...] += part

        @pl.when(k == steps - 1)
        def _():
            done = acc[...].astype(jnp.bfloat16)
            picks = []
            for i in range(count):
                code = x_refs[i][:, width:].astype(jnp.float32)[:, :1].astype(jnp.int32)
                slot = (code // CAP) * (CAP * count) + i * CAP + code % CAP
                place = lax.broadcasted_iota(jnp.int32, (rows, slots), 1)
                picks.append((slot == place).astype(jnp.bfloat16))
            pick = jnp.concatenate(picks, axis=0)
            down = (((0,), (0,)), ((), ()))
            placed = lax.dot_general(pick, done, down, preferred_element_type=jnp.float32)
            ones = jnp.ones((count * rows, EDGE), jnp.bfloat16)
            filled = lax.dot_general(pick, ones, down, preferred_element_type=jnp.float32)
            placed = jnp.where(filled[:, :1] > 0, placed, EMPTY)
            o_ref[...] = placed.astype(jnp.bfloat16).reshape(owners, CAP * count, cols)

    full = pl.BlockSpec((rows, width + EDGE), lambda k: (0, 0))
    return pl.pallas_call(
        body,
        grid=(steps,),
        in_specs=[full] * count + [pl.BlockSpec((step, cols), lambda k: (k, 0))],
        out_specs=pl.BlockSpec((owners, CAP * count, cols), lambda k: (0, 0, 0)),
        out_shape=jax.ShapeDtypeStruct((owners, CAP * count, cols), jnp.bfloat16),
        scratch_shapes=[
            pltpu.VMEM((steps, count * rows, step), jnp.bfloat16),
            pltpu.VMEM((count * rows, cols), jnp.float32),
        ],
        compiler_params=pltpu.CompilerParams(vmem_limit_bytes=40 << 20),
        cost_estimate=pl.CostEstimate(
            flops=2 * count * rows * width * cols,
            transcendentals=0,
            bytes_accessed=2 * width * cols + 2 * count * rows * width,
        ),
        name="project",
    )(*blocks, weight)


def attention(parts, where_to, segments, cotangent):
    owners, per_owner, cols = parts[0].shape
    sources = per_owner // CAP
    pack_len = cotangent.shape[0]
    third = cols // 3
    heads = third // HD
    chunk = owners * per_owner
    span = owners * CAP
    block = 256
    blocks = pack_len // block
    scale = HD ** (-0.5)
    nt = (((1,), (1,)), ((), ()))
    tn = (((0,), (0,)), ((), ()))
    f32 = jnp.float32

    def body(*refs):
        part_refs = refs[: len(parts)]
        to_ref, segk_ref, segq_ref, cot_ref, out_ref, grad_ref, qkv, keep, codes, dk, dv, low = refs[len(parts) :]
        new = lax.broadcasted_iota(jnp.int32, (chunk, chunk), 0)
        old = lax.broadcasted_iota(jnp.int32, (chunk, chunk), 1)
        source, rest = new // span, new % span
        move = ((rest // CAP) * per_owner + source * CAP + rest % CAP == old).astype(jnp.bfloat16)
        for c in range(len(parts)):
            flat = part_refs[c][...].reshape(chunk, cols)
            moved = jnp.dot(move, flat, preferred_element_type=f32).astype(jnp.bfloat16)
            for i in range(sources):
                at = pl.multiple_of(to_ref[c * sources + i] * span, span)
                qkv[pl.ds(at, span), :] = moved[i * span : (i + 1) * span, :]
        for b in range(blocks):
            at = b * block
            lead = qkv[at : at + block, :HD].astype(f32)
            live = (lead < 0.5 * EMPTY).astype(f32)
            keep[at : at + block, :] = live
            held = qkv[at : at + block, :]
            qkv[at : at + block, :] = jnp.where(live[:, :1] > 0, held, jnp.zeros_like(held))
            live_row = (lead.T[:1, :] < 0.5 * EMPTY)
            seg = segk_ref[:, at : at + block]
            codes[:, at : at + block] = jnp.where(live_row, seg, -1)

        def clear():
            dk[...] = jnp.zeros_like(dk)
            dv[...] = jnp.zeros_like(dv)
            low[...] = jnp.zeros_like(low)

        def work(at, start, size):
            rows = pl.ds(at, block)
            win = pl.ds(start, size)
            live = keep[rows, :]
            allowed = segq_ref[rows, :] == codes[:, win]
            for h in range(heads):
                lanes = slice(h * HD, (h + 1) * HD)
                q = qkv[rows, h * HD : (h + 1) * HD]
                k = qkv[win, third + h * HD : third + (h + 1) * HD]
                v = qkv[win, 2 * third + h * HD : 2 * third + (h + 1) * HD]
                s = lax.dot_general(q, k, nt, preferred_element_type=f32) * scale
                s = jnp.where(allowed, s, FILL)
                top = jnp.max(s, axis=1, keepdims=True)
                e = jnp.exp(s - top)
                p = e * (1.0 / jnp.sum(e, axis=1, keepdims=True))
                p_low = p.astype(jnp.bfloat16)
                context = jnp.dot(p_low, v, preferred_element_type=f32)
                out_ref[rows, lanes] = (context * live).astype(jnp.bfloat16)
                g32 = cot_ref[rows, lanes].astype(f32) * live
                g = g32.astype(jnp.bfloat16)
                delta = jnp.sum(g32 * context, axis=1, keepdims=True)
                dp = lax.dot_general(g, v, nt, preferred_element_type=f32)
                ds = (p * (dp - delta)).astype(jnp.bfloat16)
                dq = jnp.dot(ds, k, preferred_element_type=f32) * scale
                grad_ref[rows, lanes] = dq.astype(jnp.bfloat16)
                dk[win, lanes] += lax.dot_general(ds, q, tn, preferred_element_type=f32)
                dv[win, lanes] += lax.dot_general(p_low, g, tn, preferred_element_type=f32)
                low[...] = jnp.minimum(low[...], jnp.min(jnp.where(live > 0, top, 0.0), axis=0, keepdims=True))

        clear()
        for b in range(blocks):
            first, last = max(b - 1, 0), min(b + 2, blocks)
            work(b * block, first * block, (last - first) * block)

        @pl.when(jnp.min(low[...]) < 0.5 * FILL)
        def _():
            clear()

            def again(b, carry):
                work(pl.multiple_of(b * block, block), 0, pack_len)
                return carry

            lax.fori_loop(0, blocks, again, 0)

        grad_ref[:, third : 2 * third] = (dk[...] * scale).astype(jnp.bfloat16)
        grad_ref[:, 2 * third :] = dv[...].astype(jnp.bfloat16)

    vmem = pl.BlockSpec(memory_space=pltpu.VMEM)
    return pl.pallas_call(
        body,
        in_specs=[vmem] * len(parts) + [pl.BlockSpec(memory_space=pltpu.SMEM)] + [vmem] * 3,
        out_specs=[vmem, vmem],
        out_shape=[
            jax.ShapeDtypeStruct((pack_len, third), jnp.bfloat16),
            jax.ShapeDtypeStruct((pack_len, cols), jnp.bfloat16),
        ],
        scratch_shapes=[
            pltpu.VMEM((pack_len, cols), jnp.bfloat16),
            pltpu.VMEM((pack_len, HD), f32),
            pltpu.VMEM((1, pack_len), jnp.int32),
            pltpu.VMEM((pack_len, third), f32),
            pltpu.VMEM((pack_len, third), f32),
            pltpu.VMEM((8, HD), f32),
        ],
        compiler_params=pltpu.CompilerParams(vmem_limit_bytes=50 << 20),
        cost_estimate=pl.CostEstimate(
            flops=12 * pack_len * pack_len * third, transcendentals=pack_len * pack_len * heads, bytes_accessed=1 << 23
        ),
        name="attention",
    )(*parts, where_to, segments, segments.reshape(pack_len, 1), cotangent)


def receive(block, link):
    pairs = [
        (((y + link[1]) % SIDE) * SIDE + (x + link[0]) % SIDE, y * SIDE + x)
        for y in range(SIDE)
        for x in range(SIDE)
    ]
    return lax.ppermute(block, "seq", pairs)


def per_device(patches, destination, segments, qkv_weight, cotangent):
    owners = lax.axis_size("dp")
    width = patches.shape[1]
    cols = 3 * qkv_weight.shape[2]
    pack_len = segments.shape[1]
    weight = qkv_weight.reshape(width, cols)

    held = {(0, 0): mark_rows(patches, destination)}
    groups = []
    for turn in ROUNDS:
        for (dx, dy), (lx, ly) in turn:
            held[dx, dy] = receive(held[(dx - lx) % SIDE, (dy - ly) % SIDE], (lx, ly))
        groups.append([offset for offset, _ in turn])
    groups[-1].append((0, 0))

    here = lax.axis_index("seq")
    hx, hy = here % SIDE, here // SIDE
    where_to = jnp.stack([((hy + dy) % SIDE) * SIDE + (hx + dx) % SIDE for group in groups for dx, dy in group])

    parts = []
    for group in groups:
        placed = project([held[offset] for offset in group], weight, owners)
        parts.append(lax.all_to_all(placed, "dp", split_axis=0, concat_axis=0, tiled=True))
    attended, grads = attention(parts, where_to, segments, cotangent[0])
    return attended[None], grads.reshape(1, pack_len, 3, cols // 3)


def solution(mesh):
    in_specs = (
        P(("dp", "seq"), None),
        P(("dp", "seq"), None),
        P("dp", None),
        P(None, None, "seq"),
        P("dp", None, "seq"),
    )
    out_specs = (P("dp", None, "seq"), P("dp", None, None, "seq"))
    return jax.shard_map(per_device, mesh=mesh, in_specs=in_specs, out_specs=out_specs, check_vma=False)
```

time: 219 us -> 156 us (0.71)
  blocking collectives: 66.7 us -> 0 us
  matrix products: 49 us -> 0 us
  starting transfers between devices: 3.41 us -> 52.2 us
  Pallas kernels: 0 us -> 37.6 us
  waiting for transfers between devices: 39.5 us -> 18.4 us
  local copies, waits for them, and re-layouts: 29.8 us -> 45.1 us
  between operations: 14.9 us -> 0.9 us
  other arithmetic: 13 us -> 0 us
    dot_general x12 -> x0, matrix products: 39.6 us -> none  [the longest x1 14.5 us: per_device(): jnp.dot(packed, flat_weight, preferred_element_type=jnp.float32)]
    all_gather x1 -> x0, waiting for transfers between devices: 39.5 us -> none  [per_device(): lax.all_gather(own_rows.reshape(-1, width_in), 'seq', axis=0, tiled=True)]
    pallas_call x0 -> x6, Pallas kernels: none -> 37.6 us  [the longest x4 24.1 us: project(): pl.pallas_call(body, grid=(steps,), in_specs=[full] * count + [pl.BlockSp...]
    unnamed x1 -> x0, blocking collectives: 34 us -> none
    all_to_all x1 -> x0, blocking collectives: 32.7 us -> none  [per_device(): lax.all_to_all(buffer, 'dp', split_axis=0, concat_axis=0, tiled=True)]
    all_to_all x1 -> x4, starting transfers between devices: 3.37 us -> 30.4 us  [per_device(): lax.all_to_all(placed, 'dp', split_axis=0, concat_axis=0, tiled=True)]
    ppermute x0 -> x15, starting transfers between devices: none -> 21.8 us  [receive(): return lax.ppermute(block, 'seq', pairs)]
    all_to_all x1 -> x4, waiting for transfers between devices: 0.01 us -> 18.3 us  [per_device(): lax.all_to_all(placed, 'dp', split_axis=0, concat_axis=0, tiled=True)]
  transfers between devices with their start and end apart: 2 -> 19, of which waited for: 1 -> 2; matrix products, arithmetic and copies ran while one was open for 6% -> 17% of each run, Pallas kernels for 0% -> 16%
where the time goes in v1:
time: 156 us; the launch traced here: 154 us
  starting transfers between devices  52.2 us (33%)
  local copies, waits for them, and re-layouts  45.1 us (29%)
  Pallas kernels  37.6 us (24%)
  waiting for transfers between devices  18.4 us (12%)
    unnamed x17, local copies, waits for them, and re-layouts  30.4 us
    all_to_all x4, starting transfers between devices, per_device(): lax.all_to_all(placed, 'dp', split_axis=0, concat_axis=0, tiled=True)  30.4 us
    pallas_call x4, Pallas kernels, project(): pl.pallas_call(body, grid=(steps,), in_specs=[full] * count + [pl.BlockSp...  24.1 us
    ppermute x15, starting transfers between devices, receive(): return lax.ppermute(block, 'seq', pairs)  21.8 us
    all_to_all x4, waiting for transfers between devices, per_device(): lax.all_to_all(placed, 'dp', split_axis=0, concat_axis=0, tiled=True)  18.3 us
    reshape x1, local copies, waits for them, and re-layouts, per_device(): weight = qkv_weight.reshape(width, cols)  12.6 us
    pallas_call x1, Pallas kernels, attention(): pl.pallas_call(body, in_specs=[vmem] * len(parts) + [pl.BlockSpec(memory_...  11.3 us
  transfers between devices with their start and end apart: 19, of which 2 were waited for; matrix products, arithmetic and copies ran while one was open for 17% of the time, Pallas kernels for 16%

profile of v1, /device:TPU:1, one launch (start us, length us, event | category | flops | bytes accessed | tf_op | source)
XLA Modules:
  0.0 154.1 jit_solution(10856574492715710023)
XLA Ops:
  0.6 1.3 copy.10.t_ref
  2.0 2.2 %mark_rows.1.refs_3_ = bf16[48,6272]{1,0:T(8,128)(2,1)} custom-call(bf16[48,6144]{1,0:T(8,128)(2,1)} %x_ref.1, s32[48,1]{1,0:T(8,128)} %copy.10.t_ref), custom_call_target="tpu_custom_call" | custom-call | tf_op jit(solution)/shard_map/mark_rows/pallas_call | solution.py:39
  4.2 3.6 %collective-permute-start.2 = (bf16[48,6272]{1,0:T(8,128)(2,1)}, bf16[48,6272]{1,0:T(8,128)(2,1)S(1)}, u32[]{:S(2)}, u32[]{:S(2)}) collective-permute-start(bf16[48,6272]{1,0:T(8,128)(2,1)} %mark_rows.1.refs_3_), channel_id=1, source_target_pairs={{4,0},{5,1},{6,2},{7,3},{8,4},{9,5},{10,6},{11,7},{12,8},{13,9},{1... | collective-permute-start | bytes 1806344 | tf_op jit(solution)/shard_map/ppermute | solution.py:235
  7.8 1.2 collective-permute-start.1
  9.0 0.0 collective-permute-start.3
  9.0 1.5 collective-permute-start
  10.5 12.8 %copy.11 = bf16[6144,3,256]{0,2,1:T(8,128)(2,1)} copy(bf16[6144,3,256]{2,0,1:T(8,128)(2,1)} %param.8) | data formatting | bytes 18874368 | tf_op args[3]
  23.2 12.6 %copy.12.refs_4_ = bf16[6144,768]{1,0:T(8,128)(2,1)} copy(bf16[6144,768]{0,1:T(8,128)(2,1)} %bitcast.23) | data formatting | bytes 18874368 | tf_op jit(solution)/shard_map/reshape | solution.py:243
  35.8 0.0 collective-permute-done.2.refs_2_
  35.9 1.3 collective-permute-start.4
  37.1 0.0 collective-permute-done.1.refs_1_
  37.1 2.7 %collective-permute-start.5 = (bf16[48,6272]{1,0:T(8,128)(2,1)S(1)}, bf16[48,6272]{1,0:T(8,128)(2,1)S(1)}, u32[]{:S(2)}, u32[]{:S(2)}) collective-permute-start(bf16[48,6272]{1,0:T(8,128)(2,1)S(1)} %collective-permute-done.1.refs_1_), channel_id=1, source_target_pairs={{4,0},{5,1},{6,2},{7,3},{8,4},{9,5},{10,6},{11,7},{12,8},{13,9},{1... | collective-permute-start | bytes 1806344 | tf_op jit(solution)/shard_map/ppermute | solution.py:235
  39.8 0.0 collective-permute-done.3.refs_3_
  39.8 0.2 collective-permute-start.6
  40.0 0.0 collective-permute-done.refs_0_
  40.0 0.0 collective-permute-start.7
  40.0 0.0 copy-start
  40.0 3.7 %copy-done = bf16[6144,768]{1,0:T(8,128)(2,1)S(1)} copy-done((bf16[6144,768]{1,0:T(8,128)(2,1)S(1)}, bf16[6144,768]{1,0:T(8,128)(2,1)}, u32[]{:S(2)}) %copy-start) | copy-done | bytes 9437208
  43.7 5.8 %project.4 = bf16[16,16,768]{2,1,0:T(8,128)(2,1)} custom-call(bf16[48,6272]{1,0:T(8,128)(2,1)S(1)} %collective-permute-done.refs_0_, bf16[48,6272]{1,0:T(8,128)(2,1)S(1)} %collective-permute-done.1.refs_1_, bf16[48,6272]{1,0:T(8,128)(2,1)S(1)} %collective-permute-done.2.refs_2_, bf16[48,6272]{1,0:T(8,128)(2,1)} %collective-permute-done.3.refs_3_, ...), custom_call_target="tpu_custom_call" | custom-call | flops 1811939328 | bytes 11796480 | tf_op jit(solution)/shard_map/project/pallas_call | solution.py:93
  49.5 11.1 %all-to-all-start = ((bf16[16,16,768]{2,1,0:T(8,128)(2,1)}), bf16[16,16,768]{2,1,0:T(8,128)(2,1)S(1)}, u32[]{:S(2)}, u32[]{:S(2)}) async-start(bf16[16,16,768]{2,1,0:T(8,128)(2,1)} %project.4), calls=%async_computation | async-start | bytes 786432 | tf_op jit(solution)/shard_map/all_to_all | solution.py:260
  60.6 0.0 collective-permute-done.4.refs_0_
  60.6 2.6 %collective-permute-start.8 = (bf16[48,6272]{1,0:T(8,128)(2,1)}, bf16[48,6272]{1,0:T(8,128)(2,1)}, u32[]{:S(2)}, u32[]{:S(2)}) collective-permute-start(bf16[48,6272]{1,0:T(8,128)(2,1)} %collective-permute-done.4.refs_0_), channel_id=1, source_target_pairs={{1,0},{2,1},{3,2},{0,3},{5,4},{6,5},{7,6},{4,7},{9,8},{10,9},{11,1... | collective-permute-start | bytes 1806344 | tf_op jit(solution)/shard_map/ppermute | solution.py:235
  63.2 0.0 collective-permute-done.6.refs_2_
  63.2 0.0 collective-permute-start.9
  63.2 0.0 collective-permute-done.5.refs_1_
  63.2 3.0 %collective-permute-start.10 = (bf16[48,6272]{1,0:T(8,128)(2,1)S(1)}, bf16[48,6272]{1,0:T(8,128)(2,1)}, u32[]{:S(2)}, u32[]{:S(2)}) collective-permute-start(bf16[48,6272]{1,0:T(8,128)(2,1)S(1)} %collective-permute-done.5.refs_1_), channel_id=1, source_target_pairs={{4,0},{5,1},{6,2},{7,3},{8,4},{9,5},{10,6},{11,7},{12,8},{13,9},{1... | collective-permute-start | bytes 1806344 | tf_op jit(solution)/shard_map/ppermute | solution.py:235
  66.2 0.0 collective-permute-done.7.refs_3_
  66.2 0.0 collective-permute-start.11
  66.2 0.0 copy-start.1
  66.2 3.7 %copy-done.1 = bf16[6144,768]{1,0:T(8,128)(2,1)S(1)} copy-done((bf16[6144,768]{1,0:T(8,128)(2,1)S(1)}, bf16[6144,768]{1,0:T(8,128)(2,1)}, u32[]{:S(2)}) %copy-start.1) | copy-done | bytes 9437208
  69.9 6.0 %project.5 = bf16[16,16,768]{2,1,0:T(8,128)(2,1)} custom-call(bf16[48,6272]{1,0:T(8,128)(2,1)} %collective-permute-done.4.refs_0_, bf16[48,6272]{1,0:T(8,128)(2,1)S(1)} %collective-permute-done.5.refs_1_, bf16[48,6272]{1,0:T(8,128)(2,1)S(1)} %collective-permute-done.6.refs_2_, bf16[48,6272]{1,0:T(8,128)(2,1)} %collective-permute-done.7.refs_3_, ...), custom_call_target="tpu_custom_call" | custom-call | flops 1811939328 | bytes 11796480 | tf_op jit(solution)/shard_map/project/pallas_call | solution.py:93
  75.8 0.0 copy-start.4
  75.9 0.0 all-to-all-done.refs_0_
  75.9 7.9 %all-to-all-start.1 = ((bf16[16,16,768]{2,1,0:T(8,128)(2,1)}), bf16[16,16,768]{2,1,0:T(8,128)(2,1)}, u32[]{:S(2)}, u32[]{:S(2)}) async-start(bf16[16,16,768]{2,1,0:T(8,128)(2,1)} %project.5), calls=%async_computation.1 | async-start | bytes 786432 | tf_op jit(solution)/shard_map/all_to_all | solution.py:260
  83.7 2.9 %collective-permute-start.12 = (bf16[48,6272]{1,0:T(8,128)(2,1)S(1)}, bf16[48,6272]{1,0:T(8,128)(2,1)}, u32[]{:S(2)}, u32[]{:S(2)}) collective-permute-start(bf16[48,6272]{1,0:T(8,128)(2,1)S(1)} %collective-permute-done.refs_0_), channel_id=1, source_target_pairs={{1,0},{2,1},{3,2},{0,3},{5,4},{6,5},{7,6},{4,7},{9,8},{10,9},{11,1... | collective-permute-start | bytes 1806344 | tf_op jit(solution)/shard_map/ppermute | solution.py:235
  86.6 0.0 collective-permute-done.8.refs_0_
  86.6 3.0 %collective-permute-start.13 = (bf16[48,6272]{1,0:T(8,128)(2,1)S(1)}, bf16[48,6272]{1,0:T(8,128)(2,1)}, u32[]{:S(2)}, u32[]{:S(2)}) collective-permute-start(bf16[48,6272]{1,0:T(8,128)(2,1)S(1)} %collective-permute-done.2.refs_2_), channel_id=1, source_target_pairs={{4,0},{5,1},{6,2},{7,3},{8,4},{9,5},{10,6},{11,7},{12,8},{13,9},{1... | collective-permute-start | bytes 1806344 | tf_op jit(solution)/shard_map/ppermute | solution.py:235
  89.6 0.0 collective-permute-done.10.refs_2_
  89.6 0.0 collective-permute-start.14
  89.6 0.0 collective-permute-done.9.refs_1_
  89.6 0.0 collective-permute-done.11.refs_3_
  89.6 0.0 copy-start.2
  89.6 3.7 %copy-done.2 = bf16[6144,768]{1,0:T(8,128)(2,1)S(1)} copy-done((bf16[6144,768]{1,0:T(8,128)(2,1)S(1)}, bf16[6144,768]{1,0:T(8,128)(2,1)}, u32[]{:S(2)}) %copy-start.2) | copy-done | bytes 9437208
  93.3 6.3 %project.6 = bf16[16,16,768]{2,1,0:T(8,128)(2,1)} custom-call(bf16[48,6272]{1,0:T(8,128)(2,1)} %collective-permute-done.8.refs_0_, bf16[48,6272]{1,0:T(8,128)(2,1)} %collective-permute-done.9.refs_1_, bf16[48,6272]{1,0:T(8,128)(2,1)} %collective-permute-done.10.refs_2_, bf16[48,6272]{1,0:T(8,128)(2,1)} %collective-permute-done.11.refs_3_, ...), custom_call_target="tpu_custom_call" | custom-call | flops 1811939328 | bytes 11796480 | tf_op jit(solution)/shard_map/project/pallas_call | solution.py:93
  99.6 0.0 copy-start.5
  99.6 0.0 all-to-all-done.1.refs_1_
  99.6 7.9 %all-to-all-start.2 = ((bf16[16,16,768]{2,1,0:T(8,128)(2,1)}), bf16[16,16,768]{2,1,0:T(8,128)(2,1)S(1)}, u32[]{:S(2)}, u32[]{:S(2)}) async-start(bf16[16,16,768]{2,1,0:T(8,128)(2,1)} %project.6), calls=%async_computation.2 | async-start | bytes 786432 | tf_op jit(solution)/shard_map/all_to_all | solution.py:260
  107.5 0.0 collective-permute-done.12.refs_0_
  107.5 0.0 collective-permute-done.13.refs_1_
  107.6 0.0 collective-permute-done.14.refs_2_
  107.6 0.0 copy-done.4
  107.6 0.0 copy-start.3
  107.6 3.7 %copy-done.3 = bf16[6144,768]{1,0:T(8,128)(2,1)S(1)} copy-done((bf16[6144,768]{1,0:T(8,128)(2,1)S(1)}, bf16[6144,768]{1,0:T(8,128)(2,1)}, u32[]{:S(2)}) %copy-start.3) | copy-done | bytes 9437208
  111.3 6.0 %project.7 = bf16[16,16,768]{2,1,0:T(8,128)(2,1)} custom-call(bf16[48,6272]{1,0:T(8,128)(2,1)} %collective-permute-done.12.refs_0_, bf16[48,6272]{1,0:T(8,128)(2,1)} %collective-permute-done.13.refs_1_, bf16[48,6272]{1,0:T(8,128)(2,1)S(1)} %collective-permute-done.14.refs_2_, bf16[48,6272]{1,0:T(8,128)(2,1)S(1)} %copy-done.4, bf16[6144,768]{1,0:T(8,128)(2,1)S(1)} %copy-done.3), custom_call_target="tpu_custom_call" | custom-call | flops 1811939328 | bytes 11796480 | tf_op jit(solution)/shard_map/project/pallas_call | solution.py:93
  117.3 4.8 %all-to-all-done.2.refs_2_ = bf16[16,16,768]{2,1,0:T(8,128)(2,1)S(1)} async-done(((bf16[16,16,768]{2,1,0:T(8,128)(2,1)}), bf16[16,16,768]{2,1,0:T(8,128)(2,1)S(1)}, u32[]{:S(2)}, u32[]{:S(2)}) %all-to-all-start.2) | async-done | bytes 393248 | tf_op jit(solution)/shard_map/all_to_all | solution.py:260
  122.1 3.5 %all-to-all-start.3 = ((bf16[16,16,768]{2,1,0:T(8,128)(2,1)}), bf16[16,16,768]{2,1,0:T(8,128)(2,1)S(1)}, u32[]{:S(2)}, u32[]{:S(2)}) async-start(bf16[16,16,768]{2,1,0:T(8,128)(2,1)} %project.7), calls=%async_computation.3 | async-start | bytes 786432 | tf_op jit(solution)/shard_map/all_to_all | solution.py:260
  125.7 0.0 copy-done.5
  125.7 0.2 copy.16.refs_6_
  125.9 0.1 stack.67.refs_4_
  126.0 13.5 %all-to-all-done.3.refs_3_ = bf16[16,16,768]{2,1,0:T(8,128)(2,1)S(1)} async-done(((bf16[16,16,768]{2,1,0:T(8,128)(2,1)}), bf16[16,16,768]{2,1,0:T(8,128)(2,1)S(1)}, u32[]{:S(2)}, u32[]{:S(2)}) %all-to-all-start.3) | async-done | bytes 393248 | tf_op jit(solution)/shard_map/all_to_all | solution.py:260
  139.5 0.0 copy-done.6
  139.5 11.3 %attention.1 = (bf16[1024,256]{1,0:T(8,128)(2,1)}, bf16[1024,768]{1,0:T(8,128)(2,1)}) custom-call(bf16[16,16,768]{2,1,0:T(8,128)(2,1)S(1)} %all-to-all-done.refs_0_, bf16[16,16,768]{2,1,0:T(8,128)(2,1)} %all-to-all-done.1.refs_1_, bf16[16,16,768]{2,1,0:T(8,128)(2,1)S(1)} %all-to-all-done.2.refs_2_, bf16[16,16,768]{2,1,0:T(8,128)(2,1)S(1)} %all-to-all-done.3.refs_3_, ...), custom_call_target="tpu_custom_call" | custom-call | flops 3221225472 | bytes 8388608 | tf_op jit(solution)/shard_map/attention/pallas_call | solution.py:205
  150.8 1.7 %copy.17 = bf16[1024,768]{0,1:T(8,128)(2,1)S(1)} copy(bf16[1024,768]{1,0:T(8,128)(2,1)} %get-tuple-element.5) | data formatting | bytes 3145728 | tf_op jit(solution)/shard_map/attention/pallas_call | solution.py:205
  152.5 1.6 %copy.18 = bf16[1,1024,3,256]{3,1,2,0:T(8,128)(2,1)} copy(bf16[1,1024,3,256]{1,3,2,0:T(8,128)(2,1)S(1)} %bitcast.24) | data formatting | bytes 3145728
  (1 shorter events, 0.0 us)
Async XLA Ops:
  4.2 31.6 %collective-permute-start.2 = (bf16[48,6272]{1,0:T(8,128)(2,1)}, bf16[48,6272]{1,0:T(8,128)(2,1)S(1)}, u32[]{:S(2)}, u32[]{:S(2)}) collective-permute-start(bf16[48,6272]{1,0:T(8,128)(2,1)} %mark_rows.1.refs_3_), channel_id=1, source_target_pairs={{4,0},{5,1},{6,2},{7,3},{8,4},{9,5},{10,6},{11,7},{12,8},{13,9},{1... | collective-permute-start | bytes 1806344 | tf_op jit(solution)/shard_map/ppermute | solution.py:235
  7.8 29.4 %collective-permute-start.1 = (bf16[48,6272]{1,0:T(8,128)(2,1)}, bf16[48,6272]{1,0:T(8,128)(2,1)S(1)}, u32[]{:S(2)}, u32[]{:S(2)}) collective-permute-start(bf16[48,6272]{1,0:T(8,128)(2,1)} %mark_rows.1.refs_3_), channel_id=1, source_target_pairs={{3,0},{0,1},{1,2},{2,3},{7,4},{4,5},{5,6},{6,7},{11,8},{8,9},{9,10... | collective-permute-start | bytes 1806344 | tf_op jit(solution)/shard_map/ppermute | solution.py:235
  9.0 30.8 %collective-permute-start.3 = (bf16[48,6272]{1,0:T(8,128)(2,1)}, bf16[48,6272]{1,0:T(8,128)(2,1)}, u32[]{:S(2)}, u32[]{:S(2)}) collective-permute-start(bf16[48,6272]{1,0:T(8,128)(2,1)} %mark_rows.1.refs_3_), channel_id=1, source_target_pairs={{12,0},{13,1},{14,2},{15,3},{0,4},{1,5},{2,6},{3,7},{4,8},{5,9},{6... | collective-permute-start | bytes 1806344 | tf_op jit(solution)/shard_map/ppermute | solution.py:235
  9.0 31.0 %collective-permute-start = (bf16[48,6272]{1,0:T(8,128)(2,1)}, bf16[48,6272]{1,0:T(8,128)(2,1)S(1)}, u32[]{:S(2)}, u32[]{:S(2)}) collective-permute-start(bf16[48,6272]{1,0:T(8,128)(2,1)} %mark_rows.1.refs_3_), channel_id=1, source_target_pairs={{1,0},{2,1},{3,2},{0,3},{5,4},{6,5},{7,6},{4,7},{9,8},{10,9},{11,1... | collective-permute-start | bytes 1806344 | tf_op jit(solution)/shard_map/ppermute | solution.py:235
  35.9 24.7 %collective-permute-start.4 = (bf16[48,6272]{1,0:T(8,128)(2,1)S(1)}, bf16[48,6272]{1,0:T(8,128)(2,1)}, u32[]{:S(2)}, u32[]{:S(2)}) collective-permute-start(bf16[48,6272]{1,0:T(8,128)(2,1)S(1)} %collective-permute-done.2.refs_2_), channel_id=1, source_target_pairs={{1,0},{2,1},{3,2},{0,3},{5,4},{6,5},{7,6},{4,7},{9,8},{10,9},{11,1... | collective-permute-start | bytes 1806344 | tf_op jit(solution)/shard_map/ppermute | solution.py:235
  37.1 26.0 %collective-permute-start.5 = (bf16[48,6272]{1,0:T(8,128)(2,1)S(1)}, bf16[48,6272]{1,0:T(8,128)(2,1)S(1)}, u32[]{:S(2)}, u32[]{:S(2)}) collective-permute-start(bf16[48,6272]{1,0:T(8,128)(2,1)S(1)} %collective-permute-done.1.refs_1_), channel_id=1, source_target_pairs={{4,0},{5,1},{6,2},{7,3},{8,4},{9,5},{10,6},{11,7},{12,8},{13,9},{1... | collective-permute-start | bytes 1806344 | tf_op jit(solution)/shard_map/ppermute | solution.py:235
  39.8 23.4 %collective-permute-start.6 = (bf16[48,6272]{1,0:T(8,128)(2,1)}, bf16[48,6272]{1,0:T(8,128)(2,1)S(1)}, u32[]{:S(2)}, u32[]{:S(2)}) collective-permute-start(bf16[48,6272]{1,0:T(8,128)(2,1)} %collective-permute-done.3.refs_3_), channel_id=1, source_target_pairs={{3,0},{0,1},{1,2},{2,3},{7,4},{4,5},{5,6},{6,7},{11,8},{8,9},{9,10... | collective-permute-start | bytes 1806344 | tf_op jit(solution)/shard_map/ppermute | solution.py:235
  40.0 26.2 %collective-permute-start.7 = (bf16[48,6272]{1,0:T(8,128)(2,1)S(1)}, bf16[48,6272]{1,0:T(8,128)(2,1)}, u32[]{:S(2)}, u32[]{:S(2)}) collective-permute-start(bf16[48,6272]{1,0:T(8,128)(2,1)S(1)} %collective-permute-done.refs_0_), channel_id=1, source_target_pairs={{12,0},{13,1},{14,2},{15,3},{0,4},{1,5},{2,6},{3,7},{4,8},{5,9},{6... | collective-permute-start | bytes 1806344 | tf_op jit(solution)/shard_map/ppermute | solution.py:235
  40.0 3.7 %copy-start = (bf16[6144,768]{1,0:T(8,128)(2,1)S(1)}, bf16[6144,768]{1,0:T(8,128)(2,1)}, u32[]{:S(2)}) copy-start(bf16[6144,768]{1,0:T(8,128)(2,1)} %copy.12.refs_4_) | copy-start | bytes 28311556
  49.5 26.4 %all-to-all-start = ((bf16[16,16,768]{2,1,0:T(8,128)(2,1)}), bf16[16,16,768]{2,1,0:T(8,128)(2,1)S(1)}, u32[]{:S(2)}, u32[]{:S(2)}) async-start(bf16[16,16,768]{2,1,0:T(8,128)(2,1)} %project.4), calls=%async_computation | async-start | bytes 786432 | tf_op jit(solution)/shard_map/all_to_all | solution.py:260
  60.6 26.1 %collective-permute-start.8 = (bf16[48,6272]{1,0:T(8,128)(2,1)}, bf16[48,6272]{1,0:T(8,128)(2,1)}, u32[]{:S(2)}, u32[]{:S(2)}) collective-permute-start(bf16[48,6272]{1,0:T(8,128)(2,1)} %collective-permute-done.4.refs_0_), channel_id=1, source_target_pairs={{1,0},{2,1},{3,2},{0,3},{5,4},{6,5},{7,6},{4,7},{9,8},{10,9},{11,1... | collective-permute-start | bytes 1806344 | tf_op jit(solution)/shard_map/ppermute | solution.py:235
  63.2 26.4 %collective-permute-start.9 = (bf16[48,6272]{1,0:T(8,128)(2,1)S(1)}, bf16[48,6272]{1,0:T(8,128)(2,1)}, u32[]{:S(2)}, u32[]{:S(2)}) collective-permute-start(bf16[48,6272]{1,0:T(8,128)(2,1)S(1)} %collective-permute-done.6.refs_2_), channel_id=1, source_target_pairs={{3,0},{0,1},{1,2},{2,3},{7,4},{4,5},{5,6},{6,7},{11,8},{8,9},{9,10... | collective-permute-start | bytes 1806344 | tf_op jit(solution)/shard_map/ppermute | solution.py:235
  63.2 26.4 %collective-permute-start.10 = (bf16[48,6272]{1,0:T(8,128)(2,1)S(1)}, bf16[48,6272]{1,0:T(8,128)(2,1)}, u32[]{:S(2)}, u32[]{:S(2)}) collective-permute-start(bf16[48,6272]{1,0:T(8,128)(2,1)S(1)} %collective-permute-done.5.refs_1_), channel_id=1, source_target_pairs={{4,0},{5,1},{6,2},{7,3},{8,4},{9,5},{10,6},{11,7},{12,8},{13,9},{1... | collective-permute-start | bytes 1806344 | tf_op jit(solution)/shard_map/ppermute | solution.py:235
  66.2 23.4 %collective-permute-start.11 = (bf16[48,6272]{1,0:T(8,128)(2,1)}, bf16[48,6272]{1,0:T(8,128)(2,1)}, u32[]{:S(2)}, u32[]{:S(2)}) collective-permute-start(bf16[48,6272]{1,0:T(8,128)(2,1)} %collective-permute-done.7.refs_3_), channel_id=1, source_target_pairs={{12,0},{13,1},{14,2},{15,3},{0,4},{1,5},{2,6},{3,7},{4,8},{5,9},{6... | collective-permute-start | bytes 1806344 | tf_op jit(solution)/shard_map/ppermute | solution.py:235
  66.2 3.7 %copy-start.1 = (bf16[6144,768]{1,0:T(8,128)(2,1)S(1)}, bf16[6144,768]{1,0:T(8,128)(2,1)}, u32[]{:S(2)}) copy-start(bf16[6144,768]{1,0:T(8,128)(2,1)} %copy.12.refs_4_) | copy-start | bytes 28311556
  75.8 31.7 %copy-start.4 = (bf16[48,6272]{1,0:T(8,128)(2,1)S(1)}, bf16[48,6272]{1,0:T(8,128)(2,1)}, u32[]{:S(2)}) copy-start(bf16[48,6272]{1,0:T(8,128)(2,1)} %mark_rows.1.refs_3_) | copy-start | bytes 1806340
  75.9 23.8 %all-to-all-start.1 = ((bf16[16,16,768]{2,1,0:T(8,128)(2,1)}), bf16[16,16,768]{2,1,0:T(8,128)(2,1)}, u32[]{:S(2)}, u32[]{:S(2)}) async-start(bf16[16,16,768]{2,1,0:T(8,128)(2,1)} %project.5), calls=%async_computation.1 | async-start | bytes 786432 | tf_op jit(solution)/shard_map/all_to_all | solution.py:260
  83.7 23.8 %collective-permute-start.12 = (bf16[48,6272]{1,0:T(8,128)(2,1)S(1)}, bf16[48,6272]{1,0:T(8,128)(2,1)}, u32[]{:S(2)}, u32[]{:S(2)}) collective-permute-start(bf16[48,6272]{1,0:T(8,128)(2,1)S(1)} %collective-permute-done.refs_0_), channel_id=1, source_target_pairs={{1,0},{2,1},{3,2},{0,3},{5,4},{6,5},{7,6},{4,7},{9,8},{10,9},{11,1... | collective-permute-start | bytes 1806344 | tf_op jit(solution)/shard_map/ppermute | solution.py:235
  86.6 20.9 %collective-permute-start.13 = (bf16[48,6272]{1,0:T(8,128)(2,1)S(1)}, bf16[48,6272]{1,0:T(8,128)(2,1)}, u32[]{:S(2)}, u32[]{:S(2)}) collective-permute-start(bf16[48,6272]{1,0:T(8,128)(2,1)S(1)} %collective-permute-done.2.refs_2_), channel_id=1, source_target_pairs={{4,0},{5,1},{6,2},{7,3},{8,4},{9,5},{10,6},{11,7},{12,8},{13,9},{1... | collective-permute-start | bytes 1806344 | tf_op jit(solution)/shard_map/ppermute | solution.py:235
  89.6 18.0 %collective-permute-start.14 = (bf16[48,6272]{1,0:T(8,128)(2,1)}, bf16[48,6272]{1,0:T(8,128)(2,1)S(1)}, u32[]{:S(2)}, u32[]{:S(2)}) collective-permute-start(bf16[48,6272]{1,0:T(8,128)(2,1)} %collective-permute-done.10.refs_2_), channel_id=1, source_target_pairs={{3,0},{0,1},{1,2},{2,3},{7,4},{4,5},{5,6},{6,7},{11,8},{8,9},{9,10... | collective-permute-start | bytes 1806344 | tf_op jit(solution)/shard_map/ppermute | solution.py:235
  89.6 3.7 %copy-start.2 = (bf16[6144,768]{1,0:T(8,128)(2,1)S(1)}, bf16[6144,768]{1,0:T(8,128)(2,1)}, u32[]{:S(2)}) copy-start(bf16[6144,768]{1,0:T(8,128)(2,1)} %copy.12.refs_4_) | copy-start | bytes 28311556
  99.6 26.1 %copy-start.5 = (s32[1,1024]{1,0:T(1,128)S(1)}, s32[1,1024]{1,0:T(1,128)}, u32[]{:S(2)}) copy-start(s32[1,1024]{1,0:T(1,128)} %refs_5_.1) | copy-start | bytes 12292
  99.6 22.5 %all-to-all-start.2 = ((bf16[16,16,768]{2,1,0:T(8,128)(2,1)}), bf16[16,16,768]{2,1,0:T(8,128)(2,1)S(1)}, u32[]{:S(2)}, u32[]{:S(2)}) async-start(bf16[16,16,768]{2,1,0:T(8,128)(2,1)} %project.6), calls=%async_computation.2 | async-start | bytes 786432 | tf_op jit(solution)/shard_map/all_to_all | solution.py:260
  107.6 3.7 %copy-start.3 = (bf16[6144,768]{1,0:T(8,128)(2,1)S(1)}, bf16[6144,768]{1,0:T(8,128)(2,1)}, u32[]{:S(2)}) copy-start(bf16[6144,768]{1,0:T(8,128)(2,1)} %copy.12.refs_4_) | copy-start | bytes 28311556
  111.3 28.3 %copy-start.6 = (bf16[1,1024,256]{2,1,0:T(8,128)(2,1)S(1)}, bf16[1,1024,256]{2,1,0:T(8,128)(2,1)}, u32[]{:S(2)}) copy-start(bf16[1,1024,256]{2,1,0:T(8,128)(2,1)} %param.9) | copy-start | bytes 1572868
  122.1 17.4 %all-to-all-start.3 = ((bf16[16,16,768]{2,1,0:T(8,128)(2,1)}), bf16[16,16,768]{2,1,0:T(8,128)(2,1)S(1)}, u32[]{:S(2)}, u32[]{:S(2)}) async-start(bf16[16,16,768]{2,1,0:T(8,128)(2,1)} %project.7), calls=%async_computation.3 | async-start | bytes 786432 | tf_op jit(solution)/shard_map/all_to_all | solution.py:260

commit v2 on v1

--- a/solution.py
+++ b/solution.py
@@ -11,6 +11,7 @@
 FILL = -1000000000.0
 EMPTY = 1.0e15
 EDGE = 128
+STEPS = 2
 
 ROUNDS = (
     (((1, 0), (1, 0)), ((3, 0), (3, 0)), ((0, 1), (0, 1)), ((0, 3), (0, 3))),
@@ -25,79 +26,77 @@
 
     def body(x_ref, t_ref, o_ref):
         o_ref[:, :width] = x_ref[...]
-        target = t_ref[...]
-        owner = lax.broadcasted_iota(jnp.int32, (rows, EDGE), 1)
-        onehot = (target == owner).astype(jnp.float32)
+        owner = lax.broadcasted_iota(jnp.int32, (EDGE, rows), 0)
+        onehot = (t_ref[...] == owner).astype(jnp.bfloat16)
         r = lax.broadcasted_iota(jnp.int32, (rows, rows), 0)
         c = lax.broadcasted_iota(jnp.int32, (rows, rows), 1)
-        lower = (c < r).astype(jnp.bfloat16)
-        before = jnp.dot(lower, onehot.astype(jnp.bfloat16), preferred_element_type=jnp.float32)
-        rank = jnp.sum(before * onehot, axis=1, keepdims=True)
-        slot = target.astype(jnp.float32) * CAP + rank
-        o_ref[:, width:] = jnp.broadcast_to(slot, (rows, EDGE)).astype(jnp.bfloat16)
+        earlier = (r < c).astype(jnp.bfloat16)
+        before = jnp.dot(onehot, earlier, preferred_element_type=jnp.float32)
+        rank = (before * onehot.astype(jnp.float32)).astype(jnp.bfloat16)
+        number = (lax.broadcasted_iota(jnp.int32, (EDGE, EDGE), 0) * CAP).astype(jnp.float32).astype(jnp.bfloat16)
+        tn = (((0,), (0,)), ((), ()))
+        slot = lax.dot_general(onehot, number, tn, preferred_element_type=jnp.float32)
+        slot += lax.dot_general(rank, jnp.ones((EDGE, EDGE), jnp.bfloat16), tn, preferred_element_type=jnp.float32)
+        o_ref[:, width:] = slot.astype(jnp.bfloat16)
 
     return pl.pallas_call(
         body,
         out_shape=jax.ShapeDtypeStruct((rows, width + EDGE), jnp.bfloat16),
         name="mark_rows",
-    )(patches, destination)
+    )(patches, destination.reshape(1, rows))
 
 
 def project(blocks, weight, owners):
     count = len(blocks)
     rows = blocks[0].shape[0]
-    width, cols = weight.shape
-    step = 1024
-    steps = width // step
-    slots = owners * CAP * count
+    kinds, width, third = weight.shape
+    cols = kinds * third
+    each = CAP * count
+    slots = owners * each
+    step = width // STEPS
 
     def body(*refs):
         x_refs = refs[:count]
         w_ref, o_ref, all_x, acc = refs[count:]
-        k = pl.program_id(0)
-
-        @pl.when(k == 0)
+        part = pl.program_id(0)
+
+        @pl.when(part == 0)
         def _():
             for i in range(count):
-                for j in range(steps):
-                    all_x[j, i * rows : (i + 1) * rows, :] = x_refs[i][:, j * step : (j + 1) * step]
-
-        part = jnp.dot(all_x[k], w_ref[...], preferred_element_type=jnp.float32)
-
-        @pl.when(k == 0)
+                for n in range(STEPS):
+                    all_x[n, i * rows : (i + 1) * rows, :] = x_refs[i][:, n * step : (n + 1) * step]
+            acc[...] = jnp.zeros_like(acc)
+
+        for j in range(kinds):
+            lanes = slice(j * third, (j + 1) * third)
+            acc[:, lanes] += jnp.dot(all_x[part], w_ref[j], preferred_element_type=jnp.float32)
+
+        @pl.when(part == STEPS - 1)
         def _():
-            acc[...] = part
-
-        @pl.when(k > 0)
-        def _():
-            acc[...] += part
-
-        @pl.when(k == steps - 1)
-        def _():
-            done = acc[...].astype(jnp.bfloat16)
-            picks = []
-            for i in range(count):
-                code = x_refs[i][:, width:].astype(jnp.float32)[:, :1].astype(jnp.int32)
-                slot = (code // CAP) * (CAP * count) + i * CAP + code % CAP
-                place = lax.broadcasted_iota(jnp.int32, (rows, slots), 1)
-                picks.append((slot == place).astype(jnp.bfloat16))
-            pick = jnp.concatenate(picks, axis=0)
-            down = (((0,), (0,)), ((), ()))
-            placed = lax.dot_general(pick, done, down, preferred_element_type=jnp.float32)
+            nt = (((1,), (1,)), ((), ()))
+            lead = (lax.broadcasted_iota(jnp.int32, (8, EDGE), 1) == 0).astype(jnp.bfloat16)
+            edge = jnp.concatenate([x_refs[i][:, width:] for i in range(count)], axis=0)
+            code = lax.dot_general(lead, edge, nt, preferred_element_type=jnp.float32)[:1].astype(jnp.int32)
+            row = lax.broadcasted_iota(jnp.int32, (1, count * rows), 1)
+            slot = (code // CAP) * each + (row // rows) * CAP + code % CAP
+            pick = (lax.broadcasted_iota(jnp.int32, (slots, count * rows), 0) == slot).astype(jnp.bfloat16)
             ones = jnp.ones((count * rows, EDGE), jnp.bfloat16)
-            filled = lax.dot_general(pick, ones, down, preferred_element_type=jnp.float32)
-            placed = jnp.where(filled[:, :1] > 0, placed, EMPTY)
-            o_ref[...] = placed.astype(jnp.bfloat16).reshape(owners, CAP * count, cols)
-
-    full = pl.BlockSpec((rows, width + EDGE), lambda k: (0, 0))
+            filled = jnp.dot(pick, ones, preferred_element_type=jnp.float32)[:, :1] > 0
+            for j in range(kinds):
+                lanes = slice(j * third, (j + 1) * third)
+                placed = jnp.dot(pick, acc[:, lanes].astype(jnp.bfloat16), preferred_element_type=jnp.float32)
+                placed = jnp.where(filled, placed, EMPTY).astype(jnp.bfloat16)
+                o_ref[:, :, lanes] = placed.reshape(owners, each, third)
+
+    full = pl.BlockSpec((rows, width + EDGE), lambda part: (0, 0))
     return pl.pallas_call(
         body,
-        grid=(steps,),
-        in_specs=[full] * count + [pl.BlockSpec((step, cols), lambda k: (k, 0))],
-        out_specs=pl.BlockSpec((owners, CAP * count, cols), lambda k: (0, 0, 0)),
-        out_shape=jax.ShapeDtypeStruct((owners, CAP * count, cols), jnp.bfloat16),
+        grid=(STEPS,),
+        in_specs=[full] * count + [pl.BlockSpec((kinds, step, third), lambda part: (0, part, 0))],
+        out_specs=pl.BlockSpec((owners, each, cols), lambda part: (0, 0, 0)),
+        out_shape=jax.ShapeDtypeStruct((owners, each, cols), jnp.bfloat16),
         scratch_shapes=[
-            pltpu.VMEM((steps, count * rows, step), jnp.bfloat16),
+            pltpu.VMEM((STEPS, count * rows, step), jnp.bfloat16),
             pltpu.VMEM((count * rows, cols), jnp.float32),
         ],
         compiler_params=pltpu.CompilerParams(vmem_limit_bytes=40 << 20),
@@ -107,12 +106,13 @@
             bytes_accessed=2 * width * cols + 2 * count * rows * width,
         ),
         name="project",
-    )(*blocks, weight)
+    )(*blocks, pltpu.with_memory_space_constraint(weight, pltpu.HBM))
 
 
 def attention(parts, where_to, segments, cotangent):
-    owners, per_owner, cols = parts[0].shape
-    sources = per_owner // CAP
+    owners, _, cols = parts[0].shape
+    sources = SIDE
+    per_owner = sources * CAP
     pack_len = cotangent.shape[0]
     third = cols // 3
     heads = third // HD
@@ -132,8 +132,9 @@
         old = lax.broadcasted_iota(jnp.int32, (chunk, chunk), 1)
         source, rest = new // span, new % span
         move = ((rest // CAP) * per_owner + source * CAP + rest % CAP == old).astype(jnp.bfloat16)
-        for c in range(len(parts)):
-            flat = part_refs[c][...].reshape(chunk, cols)
+        pieces = [(ref, n) for ref in part_refs for n in range(0, ref.shape[1], per_owner)]
+        for c, (ref, n) in enumerate(pieces):
+            flat = ref[:, n : n + per_owner, :].reshape(chunk, cols)
             moved = jnp.dot(move, flat, preferred_element_type=f32).astype(jnp.bfloat16)
             for i in range(sources):
                 at = pl.multiple_of(to_ref[c * sources + i] * span, span)
@@ -178,7 +179,7 @@
                 dp = lax.dot_general(g, v, nt, preferred_element_type=f32)
                 ds = (p * (dp - delta)).astype(jnp.bfloat16)
                 dq = jnp.dot(ds, k, preferred_element_type=f32) * scale
-                grad_ref[rows, lanes] = dq.astype(jnp.bfloat16)
+                grad_ref[0, rows, lanes] = dq.astype(jnp.bfloat16)
                 dk[win, lanes] += lax.dot_general(ds, q, tn, preferred_element_type=f32)
                 dv[win, lanes] += lax.dot_general(p_low, g, tn, preferred_element_type=f32)
                 low[...] = jnp.minimum(low[...], jnp.min(jnp.where(live > 0, top, 0.0), axis=0, keepdims=True))
@@ -198,8 +199,8 @@
 
             lax.fori_loop(0, blocks, again, 0)
 
-        grad_ref[:, third : 2 * third] = (dk[...] * scale).astype(jnp.bfloat16)
-        grad_ref[:, 2 * third :] = dv[...].astype(jnp.bfloat16)
+        grad_ref[1] = (dk[...] * scale).astype(jnp.bfloat16)
+        grad_ref[2] = dv[...].astype(jnp.bfloat16)
 
     vmem = pl.BlockSpec(memory_space=pltpu.VMEM)
     return pl.pallas_call(
@@ -208,7 +209,7 @@
         out_specs=[vmem, vmem],
         out_shape=[
             jax.ShapeDtypeStruct((pack_len, third), jnp.bfloat16),
-            jax.ShapeDtypeStruct((pack_len, cols), jnp.bfloat16),
+            jax.ShapeDtypeStruct((3, pack_len, third), jnp.bfloat16),
         ],
         scratch_shapes=[
             pltpu.VMEM((pack_len, cols), jnp.bfloat16),
@@ -237,29 +238,25 @@
 
 def per_device(patches, destination, segments, qkv_weight, cotangent):
     owners = lax.axis_size("dp")
-    width = patches.shape[1]
-    cols = 3 * qkv_weight.shape[2]
-    pack_len = segments.shape[1]
-    weight = qkv_weight.reshape(width, cols)
+    weight = jnp.transpose(qkv_weight, (1, 0, 2))
 
     held = {(0, 0): mark_rows(patches, destination)}
-    groups = []
     for turn in ROUNDS:
         for (dx, dy), (lx, ly) in turn:
             held[dx, dy] = receive(held[(dx - lx) % SIDE, (dy - ly) % SIDE], (lx, ly))
-        groups.append([offset for offset, _ in turn])
-    groups[-1].append((0, 0))
+    order = [offset for turn in ROUNDS for offset, _ in turn] + [(0, 0)]
+    arrived = [order[:4], order[4:8], order[8:12], order[12:]]
+    parts = []
+    for offsets in arrived:
+        placed = project([held[offset] for offset in offsets], weight, owners)
+        parts.append(lax.all_to_all(placed, "dp", split_axis=0, concat_axis=0, tiled=True))
 
     here = lax.axis_index("seq")
     hx, hy = here % SIDE, here // SIDE
-    where_to = jnp.stack([((hy + dy) % SIDE) * SIDE + (hx + dx) % SIDE for group in groups for dx, dy in group])
-
-    parts = []
-    for group in groups:
-        placed = project([held[offset] for offset in group], weight, owners)
-        parts.append(lax.all_to_all(placed, "dp", split_axis=0, concat_axis=0, tiled=True))
+    where_to = jnp.stack([((hy + dy) % SIDE) * SIDE + (hx + dx) % SIDE for turn in arrived for dx, dy in turn])
+
     attended, grads = attention(parts, where_to, segments, cotangent[0])
-    return attended[None], grads.reshape(1, pack_len, 3, cols // 3)
+    return attended[None], jnp.transpose(grads, (1, 0, 2))[None]
 
 
 def solution(mesh):

time: 156 us -> 126 us (0.81); the launches traced: 154 us -> 126 us
  local copies, waits for them, and re-layouts: 45.1 us -> 0.33 us
  waiting for transfers between devices: 18.4 us -> 36 us
  starting transfers between devices: 52.2 us -> 49.3 us
  Pallas kernels: 37.6 us -> 39.5 us
    unnamed x17 -> x6, local copies, waits for them, and re-layouts: 30.4 us -> 0.01 us
    reshape x1 -> x0, local copies, waits for them, and re-layouts: 12.6 us -> none  [per_device(): weight = qkv_weight.reshape(width, cols)]
    ppermute x15, waiting for transfers between devices: 0.04 us -> 11.5 us  [receive(): return lax.ppermute(block, 'seq', pairs)]
    all_to_all x4, waiting for transfers between devices: 18.3 us -> 24.5 us  [per_device(): lax.all_to_all(placed, 'dp', split_axis=0, concat_axis=0, tiled=True)]
    all_to_all x4, starting transfers between devices: 30.4 us -> 26 us  [per_device(): lax.all_to_all(placed, 'dp', split_axis=0, concat_axis=0, tiled=True)]
    pallas_call x4, Pallas kernels: 24.1 us -> 26 us  [project(): pl.pallas_call(body, grid=(STEPS,), in_specs=[full] * count + [pl.BlockSp...]
    pallas_call x1 -> x0, local copies, waits for them, and re-layouts: 1.71 us -> none  [attention(): pl.pallas_call(body, in_specs=[vmem] * len(parts) + [pl.BlockSpec(memory_...]
  transfers between devices with their start and end apart: 19 -> 19, of which waited for: 2 -> 7; matrix products, arithmetic and copies ran while one was open for 17% -> 0% of each run, Pallas kernels for 16% -> 21%
where the time goes in v2:
time: 126 us
  starting transfers between devices  49.3 us (39%)
  Pallas kernels  39.5 us (31%)
  waiting for transfers between devices  36 us (29%)
    pallas_call x4, Pallas kernels, project(): pl.pallas_call(body, grid=(STEPS,), in_specs=[full] * count + [pl.BlockSp...  26 us
    all_to_all x4, starting transfers between devices, per_device(): lax.all_to_all(placed, 'dp', split_axis=0, concat_axis=0, tiled=True)  26 us
    all_to_all x4, waiting for transfers between devices, per_device(): lax.all_to_all(placed, 'dp', split_axis=0, concat_axis=0, tiled=True)  24.5 us
    ppermute x15, starting transfers between devices, receive(): return lax.ppermute(block, 'seq', pairs)  23.3 us
    ppermute x15, waiting for transfers between devices, receive(): return lax.ppermute(block, 'seq', pairs)  11.5 us
    pallas_call x1, Pallas kernels, attention(): pl.pallas_call(body, in_specs=[vmem] * len(parts) + [pl.BlockSpec(memory_...  11.3 us
  transfers between devices with their start and end apart: 19, of which 7 were waited for; matrix products, arithmetic and copies ran while one was open for 0% of the time, Pallas kernels for 21%

profile of v2, /device:TPU:1, one launch (start us, length us, event | category | flops | bytes accessed | tf_op | source)
XLA Modules:
  0.0 125.9 jit_solution(16754446906444433499)
XLA Ops:
  0.6 2.2 %mark_rows.1.refs_3_ = bf16[48,6272]{1,0:T(8,128)(2,1)} custom-call(bf16[48,6144]{1,0:T(8,128)(2,1)} %x_ref.1, s32[1,48]{1,0:T(1,128)} %bitcast.30), custom_call_target="tpu_custom_call" | custom-call | tf_op jit(solution)/shard_map/mark_rows/pallas_call | solution.py:42
  2.8 3.6 %collective-permute-start.2 = (bf16[48,6272]{1,0:T(8,128)(2,1)}, bf16[48,6272]{1,0:T(8,128)(2,1)S(1)}, u32[]{:S(2)}, u32[]{:S(2)}) collective-permute-start(bf16[48,6272]{1,0:T(8,128)(2,1)} %mark_rows.1.refs_3_), channel_id=1, source_target_pairs={{4,0},{5,1},{6,2},{7,3},{8,4},{9,5},{10,6},{11,7},{12,8},{13,9},{1... | collective-permute-start | bytes 1806344 | tf_op jit(solution)/shard_map/ppermute | solution.py:236
  6.4 1.2 collective-permute-start.1
  7.6 0.0 collective-permute-start.3
  7.6 1.5 %collective-permute-start = (bf16[48,6272]{1,0:T(8,128)(2,1)}, bf16[48,6272]{1,0:T(8,128)(2,1)S(1)}, u32[]{:S(2)}, u32[]{:S(2)}) collective-permute-start(bf16[48,6272]{1,0:T(8,128)(2,1)} %mark_rows.1.refs_3_), channel_id=1, source_target_pairs={{1,0},{2,1},{3,2},{0,3},{5,4},{6,5},{7,6},{4,7},{9,8},{10,9},{11,1... | collective-permute-start | bytes 1806344 | tf_op jit(solution)/shard_map/ppermute | solution.py:236
  9.1 9.9 %collective-permute-done.2.refs_2_ = bf16[48,6272]{1,0:T(8,128)(2,1)S(1)} collective-permute-done((bf16[48,6272]{1,0:T(8,128)(2,1)}, bf16[48,6272]{1,0:T(8,128)(2,1)S(1)}, u32[]{:S(2)}, u32[]{:S(2)}) %collective-permute-start.2) | collective-permute-done | bytes 602144 | tf_op jit(solution)/shard_map/ppermute | solution.py:236
  19.0 2.5 %collective-permute-start.4 = (bf16[48,6272]{1,0:T(8,128)(2,1)S(1)}, bf16[48,6272]{1,0:T(8,128)(2,1)}, u32[]{:S(2)}, u32[]{:S(2)}) collective-permute-start(bf16[48,6272]{1,0:T(8,128)(2,1)S(1)} %collective-permute-done.2.refs_2_), channel_id=1, source_target_pairs={{1,0},{2,1},{3,2},{0,3},{5,4},{6,5},{7,6},{4,7},{9,8},{10,9},{11,1... | collective-permute-start | bytes 1806344 | tf_op jit(solution)/shard_map/ppermute | solution.py:236
  21.4 0.6 collective-permute-done.1.refs_1_
  22.1 2.7 %collective-permute-start.5 = (bf16[48,6272]{1,0:T(8,128)(2,1)S(1)}, bf16[48,6272]{1,0:T(8,128)(2,1)S(1)}, u32[]{:S(2)}, u32[]{:S(2)}) collective-permute-start(bf16[48,6272]{1,0:T(8,128)(2,1)S(1)} %collective-permute-done.1.refs_1_), channel_id=1, source_target_pairs={{4,0},{5,1},{6,2},{7,3},{8,4},{9,5},{10,6},{11,7},{12,8},{13,9},{1... | collective-permute-start | bytes 1806344 | tf_op jit(solution)/shard_map/ppermute | solution.py:236
  24.7 0.0 collective-permute-done.3.refs_3_
  24.8 0.0 collective-permute-start.6
  24.8 0.0 collective-permute-done.refs_0_
  24.8 0.1 collective-permute-start.7
  24.9 6.3 %project.4 = bf16[16,16,768]{2,1,0:T(8,128)(2,1)} custom-call(bf16[48,6272]{1,0:T(8,128)(2,1)S(1)} %collective-permute-done.refs_0_, bf16[48,6272]{1,0:T(8,128)(2,1)S(1)} %collective-permute-done.1.refs_1_, bf16[48,6272]{1,0:T(8,128)(2,1)S(1)} %collective-permute-done.2.refs_2_, bf16[48,6272]{1,0:T(8,128)(2,1)} %collective-permute-done.3.refs_3_, ...), custom_call_target="tpu_custom_call" | custom-call | flops 1811939328 | bytes 11796480 | tf_op jit(solution)/shard_map/project/pallas_call | solution.py:92
  31.1 10.6 %all-to-all-start = ((bf16[16,16,768]{2,1,0:T(8,128)(2,1)}), bf16[16,16,768]{2,1,0:T(8,128)(2,1)S(1)}, u32[]{:S(2)}, u32[]{:S(2)}) async-start(bf16[16,16,768]{2,1,0:T(8,128)(2,1)} %project.4), calls=%async_computation | async-start | bytes 786432 | tf_op jit(solution)/shard_map/all_to_all | solution.py:252
  41.7 0.0 collective-permute-done.4.refs_0_
  41.7 3.0 %collective-permute-start.8 = (bf16[48,6272]{1,0:T(8,128)(2,1)}, bf16[48,6272]{1,0:T(8,128)(2,1)}, u32[]{:S(2)}, u32[]{:S(2)}) collective-permute-start(bf16[48,6272]{1,0:T(8,128)(2,1)} %collective-permute-done.4.refs_0_), channel_id=1, source_target_pairs={{1,0},{2,1},{3,2},{0,3},{5,4},{6,5},{7,6},{4,7},{9,8},{10,9},{11,1... | collective-permute-start | bytes 1806344 | tf_op jit(solution)/shard_map/ppermute | solution.py:236
  44.7 0.0 collective-permute-done.6.refs_2_
  44.7 0.0 collective-permute-start.9
  44.7 0.0 collective-permute-done.5.refs_1_
  44.7 3.0 %collective-permute-start.10 = (bf16[48,6272]{1,0:T(8,128)(2,1)S(1)}, bf16[48,6272]{1,0:T(8,128)(2,1)}, u32[]{:S(2)}, u32[]{:S(2)}) collective-permute-start(bf16[48,6272]{1,0:T(8,128)(2,1)S(1)} %collective-permute-done.5.refs_1_), channel_id=1, source_target_pairs={{4,0},{5,1},{6,2},{7,3},{8,4},{9,5},{10,6},{11,7},{12,8},{13,9},{1... | collective-permute-start | bytes 1806344 | tf_op jit(solution)/shard_map/ppermute | solution.py:236
  47.7 0.0 collective-permute-done.7.refs_3_
  47.7 0.0 collective-permute-start.11
  47.7 6.5 %project.5 = bf16[16,16,768]{2,1,0:T(8,128)(2,1)} custom-call(bf16[48,6272]{1,0:T(8,128)(2,1)} %collective-permute-done.4.refs_0_, bf16[48,6272]{1,0:T(8,128)(2,1)S(1)} %collective-permute-done.5.refs_1_, bf16[48,6272]{1,0:T(8,128)(2,1)S(1)} %collective-permute-done.6.refs_2_, bf16[48,6272]{1,0:T(8,128)(2,1)} %collective-permute-done.7.refs_3_, ...), custom_call_target="tpu_custom_call" | custom-call | flops 1811939328 | bytes 11796480 | tf_op jit(solution)/shard_map/project/pallas_call | solution.py:92
  54.2 0.0 copy-start
  54.2 2.1 %all-to-all-done.refs_0_ = bf16[16,16,768]{2,1,0:T(8,128)(2,1)S(1)} async-done(((bf16[16,16,768]{2,1,0:T(8,128)(2,1)}), bf16[16,16,768]{2,1,0:T(8,128)(2,1)S(1)}, u32[]{:S(2)}, u32[]{:S(2)}) %all-to-all-start) | async-done | bytes 393248 | tf_op jit(solution)/shard_map/all_to_all | solution.py:252
  56.3 5.8 %all-to-all-start.1 = ((bf16[16,16,768]{2,1,0:T(8,128)(2,1)}), bf16[16,16,768]{2,1,0:T(8,128)(2,1)}, u32[]{:S(2)}, u32[]{:S(2)}) async-start(bf16[16,16,768]{2,1,0:T(8,128)(2,1)} %project.5), calls=%async_computation.1 | async-start | bytes 786432 | tf_op jit(solution)/shard_map/all_to_all | solution.py:252
  62.1 2.9 %collective-permute-start.12 = (bf16[48,6272]{1,0:T(8,128)(2,1)S(1)}, bf16[48,6272]{1,0:T(8,128)(2,1)}, u32[]{:S(2)}, u32[]{:S(2)}) collective-permute-start(bf16[48,6272]{1,0:T(8,128)(2,1)S(1)} %collective-permute-done.refs_0_), channel_id=1, source_target_pairs={{1,0},{2,1},{3,2},{0,3},{5,4},{6,5},{7,6},{4,7},{9,8},{10,9},{11,1... | collective-permute-start | bytes 1806344 | tf_op jit(solution)/shard_map/ppermute | solution.py:236
  65.0 0.0 collective-permute-done.8.refs_0_
  65.0 2.9 %collective-permute-start.13 = (bf16[48,6272]{1,0:T(8,128)(2,1)S(1)}, bf16[48,6272]{1,0:T(8,128)(2,1)}, u32[]{:S(2)}, u32[]{:S(2)}) collective-permute-start(bf16[48,6272]{1,0:T(8,128)(2,1)S(1)} %collective-permute-done.2.refs_2_), channel_id=1, source_target_pairs={{4,0},{5,1},{6,2},{7,3},{8,4},{9,5},{10,6},{11,7},{12,8},{13,9},{1... | collective-permute-start | bytes 1806344 | tf_op jit(solution)/shard_map/ppermute | solution.py:236
  67.9 0.0 collective-permute-done.10.refs_2_
  67.9 0.0 collective-permute-start.14
  67.9 0.0 collective-permute-done.9.refs_1_
  67.9 0.0 collective-permute-done.11.refs_3_
  67.9 6.8 %project.6 = bf16[16,16,768]{2,1,0:T(8,128)(2,1)} custom-call(bf16[48,6272]{1,0:T(8,128)(2,1)} %collective-permute-done.8.refs_0_, bf16[48,6272]{1,0:T(8,128)(2,1)} %collective-permute-done.9.refs_1_, bf16[48,6272]{1,0:T(8,128)(2,1)} %collective-permute-done.10.refs_2_, bf16[48,6272]{1,0:T(8,128)(2,1)} %collective-permute-done.11.refs_3_, ...), custom_call_target="tpu_custom_call" | custom-call | flops 1811939328 | bytes 11796480 | tf_op jit(solution)/shard_map/project/pallas_call | solution.py:92
  74.7 0.0 copy-start.1
  74.7 2.0 %all-to-all-done.1.refs_1_ = bf16[16,16,768]{2,1,0:T(8,128)(2,1)} async-done(((bf16[16,16,768]{2,1,0:T(8,128)(2,1)}), bf16[16,16,768]{2,1,0:T(8,128)(2,1)}, u32[]{:S(2)}, u32[]{:S(2)}) %all-to-all-start.1) | async-done | bytes 393248 | tf_op jit(solution)/shard_map/all_to_all | solution.py:252
  76.7 5.9 %all-to-all-start.2 = ((bf16[16,16,768]{2,1,0:T(8,128)(2,1)}), bf16[16,16,768]{2,1,0:T(8,128)(2,1)S(1)}, u32[]{:S(2)}, u32[]{:S(2)}) async-start(bf16[16,16,768]{2,1,0:T(8,128)(2,1)} %project.6), calls=%async_computation.2 | async-start | bytes 786432 | tf_op jit(solution)/shard_map/all_to_all | solution.py:252
  82.7 0.0 collective-permute-done.12.refs_0_
  82.7 0.0 copy-start.2
  82.7 0.0 collective-permute-done.13.refs_1_
  82.7 1.0 collective-permute-done.14.refs_2_
  83.7 0.0 copy-done
  83.7 6.4 %project.7 = bf16[16,16,768]{2,1,0:T(8,128)(2,1)} custom-call(bf16[48,6272]{1,0:T(8,128)(2,1)} %collective-permute-done.12.refs_0_, bf16[48,6272]{1,0:T(8,128)(2,1)} %collective-permute-done.13.refs_1_, bf16[48,6272]{1,0:T(8,128)(2,1)S(1)} %collective-permute-done.14.refs_2_, bf16[48,6272]{1,0:T(8,128)(2,1)S(1)} %copy-done, bf16[3,6144,256]{2,1,0:T(8,128)(2,1)} %bitcast.29), custom_call_target="tpu_custom_call" | custom-call | flops 1811939328 | bytes 11796480 | tf_op jit(solution)/shard_map/project/pallas_call | solution.py:92
  90.1 7.1 %all-to-all-done.2.refs_2_ = bf16[16,16,768]{2,1,0:T(8,128)(2,1)S(1)} async-done(((bf16[16,16,768]{2,1,0:T(8,128)(2,1)}), bf16[16,16,768]{2,1,0:T(8,128)(2,1)S(1)}, u32[]{:S(2)}, u32[]{:S(2)}) %all-to-all-start.2) | async-done | bytes 393248 | tf_op jit(solution)/shard_map/all_to_all | solution.py:252
  97.2 3.7 %all-to-all-start.3 = ((bf16[16,16,768]{2,1,0:T(8,128)(2,1)}), bf16[16,16,768]{2,1,0:T(8,128)(2,1)S(1)}, u32[]{:S(2)}, u32[]{:S(2)}) async-start(bf16[16,16,768]{2,1,0:T(8,128)(2,1)} %project.7), calls=%async_computation.3 | async-start | bytes 786432 | tf_op jit(solution)/shard_map/all_to_all | solution.py:252
  101.0 0.0 copy-done.1
  101.0 0.2 copy.7.refs_6_
  101.3 0.1 stack.67.refs_4_
  101.4 13.3 %all-to-all-done.3.refs_3_ = bf16[16,16,768]{2,1,0:T(8,128)(2,1)S(1)} async-done(((bf16[16,16,768]{2,1,0:T(8,128)(2,1)}), bf16[16,16,768]{2,1,0:T(8,128)(2,1)S(1)}, u32[]{:S(2)}, u32[]{:S(2)}) %all-to-all-start.3) | async-done | bytes 393248 | tf_op jit(solution)/shard_map/all_to_all | solution.py:252
  114.6 0.0 copy-done.2
  114.6 11.3 %attention.1 = (bf16[1024,256]{1,0:T(8,128)(2,1)}, bf16[3,1024,256]{2,1,0:T(8,128)(2,1)}) custom-call(bf16[16,16,768]{2,1,0:T(8,128)(2,1)S(1)} %all-to-all-done.refs_0_, bf16[16,16,768]{2,1,0:T(8,128)(2,1)} %all-to-all-done.1.refs_1_, bf16[16,16,768]{2,1,0:T(8,128)(2,1)S(1)} %all-to-all-done.2.refs_2_, bf16[16,16,768]{2,1,0:T(8,128)(2,1)S(1)} %all-to-all-done.3.refs_3_, ...), custom_call_target="tpu_custom_call" | custom-call | flops 3221225472 | bytes 8388608 | tf_op jit(solution)/shard_map/attention/pallas_call | solution.py:206
Async XLA Ops:
  2.8 16.1 %collective-permute-start.2 = (bf16[48,6272]{1,0:T(8,128)(2,1)}, bf16[48,6272]{1,0:T(8,128)(2,1)S(1)}, u32[]{:S(2)}, u32[]{:S(2)}) collective-permute-start(bf16[48,6272]{1,0:T(8,128)(2,1)} %mark_rows.1.refs_3_), channel_id=1, source_target_pairs={{4,0},{5,1},{6,2},{7,3},{8,4},{9,5},{10,6},{11,7},{12,8},{13,9},{1... | collective-permute-start | bytes 1806344 | tf_op jit(solution)/shard_map/ppermute | solution.py:236
  6.4 15.7 %collective-permute-start.1 = (bf16[48,6272]{1,0:T(8,128)(2,1)}, bf16[48,6272]{1,0:T(8,128)(2,1)S(1)}, u32[]{:S(2)}, u32[]{:S(2)}) collective-permute-start(bf16[48,6272]{1,0:T(8,128)(2,1)} %mark_rows.1.refs_3_), channel_id=1, source_target_pairs={{3,0},{0,1},{1,2},{2,3},{7,4},{4,5},{5,6},{6,7},{11,8},{8,9},{9,10... | collective-permute-start | bytes 1806344 | tf_op jit(solution)/shard_map/ppermute | solution.py:236
  7.6 17.2 %collective-permute-start.3 = (bf16[48,6272]{1,0:T(8,128)(2,1)}, bf16[48,6272]{1,0:T(8,128)(2,1)}, u32[]{:S(2)}, u32[]{:S(2)}) collective-permute-start(bf16[48,6272]{1,0:T(8,128)(2,1)} %mark_rows.1.refs_3_), channel_id=1, source_target_pairs={{12,0},{13,1},{14,2},{15,3},{0,4},{1,5},{2,6},{3,7},{4,8},{5,9},{6... | collective-permute-start | bytes 1806344 | tf_op jit(solution)/shard_map/ppermute | solution.py:236
  7.6 17.2 %collective-permute-start = (bf16[48,6272]{1,0:T(8,128)(2,1)}, bf16[48,6272]{1,0:T(8,128)(2,1)S(1)}, u32[]{:S(2)}, u32[]{:S(2)}) collective-permute-start(bf16[48,6272]{1,0:T(8,128)(2,1)} %mark_rows.1.refs_3_), channel_id=1, source_target_pairs={{1,0},{2,1},{3,2},{0,3},{5,4},{6,5},{7,6},{4,7},{9,8},{10,9},{11,1... | collective-permute-start | bytes 1806344 | tf_op jit(solution)/shard_map/ppermute | solution.py:236
  19.0 22.8 %collective-permute-start.4 = (bf16[48,6272]{1,0:T(8,128)(2,1)S(1)}, bf16[48,6272]{1,0:T(8,128)(2,1)}, u32[]{:S(2)}, u32[]{:S(2)}) collective-permute-start(bf16[48,6272]{1,0:T(8,128)(2,1)S(1)} %collective-permute-done.2.refs_2_), channel_id=1, source_target_pairs={{1,0},{2,1},{3,2},{0,3},{5,4},{6,5},{7,6},{4,7},{9,8},{10,9},{11,1... | collective-permute-start | bytes 1806344 | tf_op jit(solution)/shard_map/ppermute | solution.py:236
  22.1 22.6 %collective-permute-start.5 = (bf16[48,6272]{1,0:T(8,128)(2,1)S(1)}, bf16[48,6272]{1,0:T(8,128)(2,1)S(1)}, u32[]{:S(2)}, u32[]{:S(2)}) collective-permute-start(bf16[48,6272]{1,0:T(8,128)(2,1)S(1)} %collective-permute-done.1.refs_1_), channel_id=1, source_target_pairs={{4,0},{5,1},{6,2},{7,3},{8,4},{9,5},{10,6},{11,7},{12,8},{13,9},{1... | collective-permute-start | bytes 1806344 | tf_op jit(solution)/shard_map/ppermute | solution.py:236
  24.8 19.9 %collective-permute-start.6 = (bf16[48,6272]{1,0:T(8,128)(2,1)}, bf16[48,6272]{1,0:T(8,128)(2,1)S(1)}, u32[]{:S(2)}, u32[]{:S(2)}) collective-permute-start(bf16[48,6272]{1,0:T(8,128)(2,1)} %collective-permute-done.3.refs_3_), channel_id=1, source_target_pairs={{3,0},{0,1},{1,2},{2,3},{7,4},{4,5},{5,6},{6,7},{11,8},{8,9},{9,10... | collective-permute-start | bytes 1806344 | tf_op jit(solution)/shard_map/ppermute | solution.py:236
  24.8 23.0 %collective-permute-start.7 = (bf16[48,6272]{1,0:T(8,128)(2,1)S(1)}, bf16[48,6272]{1,0:T(8,128)(2,1)}, u32[]{:S(2)}, u32[]{:S(2)}) collective-permute-start(bf16[48,6272]{1,0:T(8,128)(2,1)S(1)} %collective-permute-done.refs_0_), channel_id=1, source_target_pairs={{12,0},{13,1},{14,2},{15,3},{0,4},{1,5},{2,6},{3,7},{4,8},{5,9},{6... | collective-permute-start | bytes 1806344 | tf_op jit(solution)/shard_map/ppermute | solution.py:236
  31.1 25.1 %all-to-all-start = ((bf16[16,16,768]{2,1,0:T(8,128)(2,1)}), bf16[16,16,768]{2,1,0:T(8,128)(2,1)S(1)}, u32[]{:S(2)}, u32[]{:S(2)}) async-start(bf16[16,16,768]{2,1,0:T(8,128)(2,1)} %project.4), calls=%async_computation | async-start | bytes 786432 | tf_op jit(solution)/shard_map/all_to_all | solution.py:252
  41.7 23.2 %collective-permute-start.8 = (bf16[48,6272]{1,0:T(8,128)(2,1)}, bf16[48,6272]{1,0:T(8,128)(2,1)}, u32[]{:S(2)}, u32[]{:S(2)}) collective-permute-start(bf16[48,6272]{1,0:T(8,128)(2,1)} %collective-permute-done.4.refs_0_), channel_id=1, source_target_pairs={{1,0},{2,1},{3,2},{0,3},{5,4},{6,5},{7,6},{4,7},{9,8},{10,9},{11,1... | collective-permute-start | bytes 1806344 | tf_op jit(solution)/shard_map/ppermute | solution.py:236
  44.7 23.2 %collective-permute-start.9 = (bf16[48,6272]{1,0:T(8,128)(2,1)S(1)}, bf16[48,6272]{1,0:T(8,128)(2,1)}, u32[]{:S(2)}, u32[]{:S(2)}) collective-permute-start(bf16[48,6272]{1,0:T(8,128)(2,1)S(1)} %collective-permute-done.6.refs_2_), channel_id=1, source_target_pairs={{3,0},{0,1},{1,2},{2,3},{7,4},{4,5},{5,6},{6,7},{11,8},{8,9},{9,10... | collective-permute-start | bytes 1806344 | tf_op jit(solution)/shard_map/ppermute | solution.py:236
  44.7 23.2 %collective-permute-start.10 = (bf16[48,6272]{1,0:T(8,128)(2,1)S(1)}, bf16[48,6272]{1,0:T(8,128)(2,1)}, u32[]{:S(2)}, u32[]{:S(2)}) collective-permute-start(bf16[48,6272]{1,0:T(8,128)(2,1)S(1)} %collective-permute-done.5.refs_1_), channel_id=1, source_target_pairs={{4,0},{5,1},{6,2},{7,3},{8,4},{9,5},{10,6},{11,7},{12,8},{13,9},{1... | collective-permute-start | bytes 1806344 | tf_op jit(solution)/shard_map/ppermute | solution.py:236
  47.7 20.2 %collective-permute-start.11 = (bf16[48,6272]{1,0:T(8,128)(2,1)}, bf16[48,6272]{1,0:T(8,128)(2,1)}, u32[]{:S(2)}, u32[]{:S(2)}) collective-permute-start(bf16[48,6272]{1,0:T(8,128)(2,1)} %collective-permute-done.7.refs_3_), channel_id=1, source_target_pairs={{12,0},{13,1},{14,2},{15,3},{0,4},{1,5},{2,6},{3,7},{4,8},{5,9},{6... | collective-permute-start | bytes 1806344 | tf_op jit(solution)/shard_map/ppermute | solution.py:236
  54.2 29.5 %copy-start = (bf16[48,6272]{1,0:T(8,128)(2,1)S(1)}, bf16[48,6272]{1,0:T(8,128)(2,1)}, u32[]{:S(2)}) copy-start(bf16[48,6272]{1,0:T(8,128)(2,1)} %mark_rows.1.refs_3_) | copy-start | bytes 1806340
  56.3 20.5 %all-to-all-start.1 = ((bf16[16,16,768]{2,1,0:T(8,128)(2,1)}), bf16[16,16,768]{2,1,0:T(8,128)(2,1)}, u32[]{:S(2)}, u32[]{:S(2)}) async-start(bf16[16,16,768]{2,1,0:T(8,128)(2,1)} %project.5), calls=%async_computation.1 | async-start | bytes 786432 | tf_op jit(solution)/shard_map/all_to_all | solution.py:252
  62.1 20.6 %collective-permute-start.12 = (bf16[48,6272]{1,0:T(8,128)(2,1)S(1)}, bf16[48,6272]{1,0:T(8,128)(2,1)}, u32[]{:S(2)}, u32[]{:S(2)}) collective-permute-start(bf16[48,6272]{1,0:T(8,128)(2,1)S(1)} %collective-permute-done.refs_0_), channel_id=1, source_target_pairs={{1,0},{2,1},{3,2},{0,3},{5,4},{6,5},{7,6},{4,7},{9,8},{10,9},{11,1... | collective-permute-start | bytes 1806344 | tf_op jit(solution)/shard_map/ppermute | solution.py:236
  65.0 17.7 %collective-permute-start.13 = (bf16[48,6272]{1,0:T(8,128)(2,1)S(1)}, bf16[48,6272]{1,0:T(8,128)(2,1)}, u32[]{:S(2)}, u32[]{:S(2)}) collective-permute-start(bf16[48,6272]{1,0:T(8,128)(2,1)S(1)} %collective-permute-done.2.refs_2_), channel_id=1, source_target_pairs={{4,0},{5,1},{6,2},{7,3},{8,4},{9,5},{10,6},{11,7},{12,8},{13,9},{1... | collective-permute-start | bytes 1806344 | tf_op jit(solution)/shard_map/ppermute | solution.py:236
  67.9 15.8 %collective-permute-start.14 = (bf16[48,6272]{1,0:T(8,128)(2,1)}, bf16[48,6272]{1,0:T(8,128)(2,1)S(1)}, u32[]{:S(2)}, u32[]{:S(2)}) collective-permute-start(bf16[48,6272]{1,0:T(8,128)(2,1)} %collective-permute-done.10.refs_2_), channel_id=1, source_target_pairs={{3,0},{0,1},{1,2},{2,3},{7,4},{4,5},{5,6},{6,7},{11,8},{8,9},{9,10... | collective-permute-start | bytes 1806344 | tf_op jit(solution)/shard_map/ppermute | solution.py:236
  74.7 26.3 %copy-start.1 = (s32[1,1024]{1,0:T(1,128)S(1)}, s32[1,1024]{1,0:T(1,128)}, u32[]{:S(2)}) copy-start(s32[1,1024]{1,0:T(1,128)} %refs_5_.1) | copy-start | bytes 12292
  76.7 20.5 %all-to-all-start.2 = ((bf16[16,16,768]{2,1,0:T(8,128)(2,1)}), bf16[16,16,768]{2,1,0:T(8,128)(2,1)S(1)}, u32[]{:S(2)}, u32[]{:S(2)}) async-start(bf16[16,16,768]{2,1,0:T(8,128)(2,1)} %project.6), calls=%async_computation.2 | async-start | bytes 786432 | tf_op jit(solution)/shard_map/all_to_all | solution.py:252
  82.7 32.0 %copy-start.2 = (bf16[1,1024,256]{2,1,0:T(8,128)(2,1)S(1)}, bf16[1,1024,256]{2,1,0:T(8,128)(2,1)}, u32[]{:S(2)}) copy-start(bf16[1,1024,256]{2,1,0:T(8,128)(2,1)} %param.9) | copy-start | bytes 1572868
  97.2 17.4 %all-to-all-start.3 = ((bf16[16,16,768]{2,1,0:T(8,128)(2,1)}), bf16[16,16,768]{2,1,0:T(8,128)(2,1)S(1)}, u32[]{:S(2)}, u32[]{:S(2)}) async-start(bf16[16,16,768]{2,1,0:T(8,128)(2,1)} %project.7), calls=%async_computation.3 | async-start | bytes 786432 | tf_op jit(solution)/shard_map/all_to_all | solution.py:252

commit v3 on v2

--- a/solution.py
+++ b/solution.py
@@ -109,14 +109,43 @@
     )(*blocks, pltpu.with_memory_space_constraint(weight, pltpu.HBM))
 
 
-def attention(parts, where_to, segments, cotangent):
-    owners, _, cols = parts[0].shape
-    sources = SIDE
-    per_owner = sources * CAP
+def by_source(part, cols):
+    owners, each, _ = part.shape
+    chunk, span = owners * each, owners * CAP
+    new = lax.broadcasted_iota(jnp.int32, (chunk, chunk), 0)
+    old = lax.broadcasted_iota(jnp.int32, (chunk, chunk), 1)
+    source, rest = new // span, new % span
+    move = ((rest // CAP) * each + source * CAP + rest % CAP == old).astype(jnp.bfloat16)
+    return jnp.dot(move, part.reshape(chunk, cols), preferred_element_type=jnp.float32).astype(jnp.bfloat16)
+
+
+def assemble(parts):
+    owners, each, cols = parts[0].shape
+    chunk = owners * each
+
+    def body(*refs):
+        for c in range(len(parts)):
+            refs[-1][c * chunk : (c + 1) * chunk, :] = by_source(refs[c][...], cols)
+
+    vmem = pl.BlockSpec(memory_space=pltpu.VMEM)
+    return pl.pallas_call(
+        body,
+        in_specs=[vmem] * len(parts),
+        out_specs=vmem,
+        out_shape=jax.ShapeDtypeStruct((len(parts) * chunk, cols), jnp.bfloat16),
+        compiler_params=pltpu.CompilerParams(vmem_limit_bytes=16 << 20),
+        cost_estimate=pl.CostEstimate(
+            flops=2 * len(parts) * chunk * chunk * cols, transcendentals=0, bytes_accessed=4 * len(parts) * chunk * cols
+        ),
+        name="assemble",
+    )(*parts)
+
+
+def attention(early, last, where_to, segments, cotangent):
+    owners, each, cols = last.shape
     pack_len = cotangent.shape[0]
     third = cols // 3
     heads = third // HD
-    chunk = owners * per_owner
     span = owners * CAP
     block = 256
     blocks = pack_len // block
@@ -126,19 +155,16 @@
     f32 = jnp.float32
 
     def body(*refs):
-        part_refs = refs[: len(parts)]
-        to_ref, segk_ref, segq_ref, cot_ref, out_ref, grad_ref, qkv, keep, codes, dk, dv, low = refs[len(parts) :]
-        new = lax.broadcasted_iota(jnp.int32, (chunk, chunk), 0)
-        old = lax.broadcasted_iota(jnp.int32, (chunk, chunk), 1)
-        source, rest = new // span, new % span
-        move = ((rest // CAP) * per_owner + source * CAP + rest % CAP == old).astype(jnp.bfloat16)
-        pieces = [(ref, n) for ref in part_refs for n in range(0, ref.shape[1], per_owner)]
-        for c, (ref, n) in enumerate(pieces):
-            flat = ref[:, n : n + per_owner, :].reshape(chunk, cols)
-            moved = jnp.dot(move, flat, preferred_element_type=f32).astype(jnp.bfloat16)
-            for i in range(sources):
-                at = pl.multiple_of(to_ref[c * sources + i] * span, span)
-                qkv[pl.ds(at, span), :] = moved[i * span : (i + 1) * span, :]
+        early_ref, last_ref = refs[:2]
+        to_ref, segk_ref, segq_ref, cot_ref, out_ref, grad_ref, qkv, keep, codes, dk, dv, low = refs[2:]
+        before = early.shape[0] // span
+        late = by_source(last_ref[...], cols)
+        for i in range(before + each // CAP):
+            at = pl.multiple_of(to_ref[i] * span, span)
+            if i < before:
+                qkv[pl.ds(at, span), :] = early_ref[i * span : (i + 1) * span, :]
+            else:
+                qkv[pl.ds(at, span), :] = late[(i - before) * span : (i - before + 1) * span, :]
         for b in range(blocks):
             at = b * block
             lead = qkv[at : at + block, :HD].astype(f32)
@@ -205,7 +231,7 @@
     vmem = pl.BlockSpec(memory_space=pltpu.VMEM)
     return pl.pallas_call(
         body,
-        in_specs=[vmem] * len(parts) + [pl.BlockSpec(memory_space=pltpu.SMEM)] + [vmem] * 3,
+        in_specs=[vmem] * 2 + [pl.BlockSpec(memory_space=pltpu.SMEM)] + [vmem] * 3,
         out_specs=[vmem, vmem],
         out_shape=[
             jax.ShapeDtypeStruct((pack_len, third), jnp.bfloat16),
@@ -224,7 +250,7 @@
             flops=12 * pack_len * pack_len * third, transcendentals=pack_len * pack_len * heads, bytes_accessed=1 << 23
         ),
         name="attention",
-    )(*parts, where_to, segments, segments.reshape(pack_len, 1), cotangent)
+    )(early, last, where_to, segments, segments.reshape(pack_len, 1), cotangent)
 
 
 def receive(block, link):
@@ -255,7 +281,7 @@
     hx, hy = here % SIDE, here // SIDE
     where_to = jnp.stack([((hy + dy) % SIDE) * SIDE + (hx + dx) % SIDE for turn in arrived for dx, dy in turn])
 
-    attended, grads = attention(parts, where_to, segments, cotangent[0])
+    attended, grads = attention(assemble(parts[:-1]), parts[-1], where_to, segments, cotangent[0])
     return attended[None], jnp.transpose(grads, (1, 0, 2))[None]
 
 

time: 126 us -> 127 us (level)
  waiting for transfers between devices: 36 us -> 34.6 us
    all_to_all x4, waiting for transfers between devices: 24.5 us -> 22.8 us  [per_device(): lax.all_to_all(placed, 'dp', split_axis=0, concat_axis=0, tiled=True)]
    pallas_call x1 -> x2, Pallas kernels: 11.3 us -> 11 us  [the longest x1 10.5 us: attention(): pl.pallas_call(body, in_specs=[vmem] * 2 + [pl.BlockSpec(memory_space=plt...]
where the time goes in v3:
time: 127 us; the launch traced here: 126 us
  starting transfers between devices  49.7 us (39%)
  Pallas kernels  39.5 us (31%)
  waiting for transfers between devices  34.6 us (27%)
  local copies, waits for them, and re-layouts  1.37 us (1%)
    pallas_call x4, Pallas kernels, project(): pl.pallas_call(body, grid=(STEPS,), in_specs=[full] * count + [pl.BlockSp...  26.3 us
    all_to_all x4, starting transfers between devices, per_device(): lax.all_to_all(placed, 'dp', split_axis=0, concat_axis=0, tiled=True)  26.2 us
    ppermute x15, starting transfers between devices, receive(): return lax.ppermute(block, 'seq', pairs)  23.5 us
    all_to_all x4, waiting for transfers between devices, per_device(): lax.all_to_all(placed, 'dp', split_axis=0, concat_axis=0, tiled=True)  22.8 us
    ppermute x15, waiting for transfers between devices, receive(): return lax.ppermute(block, 'seq', pairs)  11.8 us
    pallas_call x1, Pallas kernels, attention(): pl.pallas_call(body, in_specs=[vmem] * 2 + [pl.BlockSpec(memory_space=plt...  10.5 us
  transfers between devices with their start and end apart: 19, of which 7 were waited for; matrix products, arithmetic and copies ran while one was open for 0% of the time, Pallas kernels for 21%

profile of v3, /device:TPU:1, one launch (start us, length us, event | category | flops | bytes accessed | tf_op | source)
XLA Modules:
  0.0 126.2 jit_solution(10767391786745378633)
XLA Ops:
  0.6 2.2 %mark_rows.1.refs_3_ = bf16[48,6272]{1,0:T(8,128)(2,1)} custom-call(bf16[48,6144]{1,0:T(8,128)(2,1)} %x_ref.1, s32[1,48]{1,0:T(1,128)} %bitcast.30), custom_call_target="tpu_custom_call" | custom-call | tf_op jit(solution)/shard_map/mark_rows/pallas_call | solution.py:42
  2.8 3.6 %collective-permute-start.2 = (bf16[48,6272]{1,0:T(8,128)(2,1)}, bf16[48,6272]{1,0:T(8,128)(2,1)S(1)}, u32[]{:S(2)}, u32[]{:S(2)}) collective-permute-start(bf16[48,6272]{1,0:T(8,128)(2,1)} %mark_rows.1.refs_3_), channel_id=1, source_target_pairs={{4,0},{5,1},{6,2},{7,3},{8,4},{9,5},{10,6},{11,7},{12,8},{13,9},{1... | collective-permute-start | bytes 1806344 | tf_op jit(solution)/shard_map/ppermute | solution.py:262
  6.4 1.2 collective-permute-start.1
  7.6 0.0 collective-permute-start.3
  7.6 1.5 %collective-permute-start = (bf16[48,6272]{1,0:T(8,128)(2,1)}, bf16[48,6272]{1,0:T(8,128)(2,1)S(1)}, u32[]{:S(2)}, u32[]{:S(2)}) collective-permute-start(bf16[48,6272]{1,0:T(8,128)(2,1)} %mark_rows.1.refs_3_), channel_id=1, source_target_pairs={{1,0},{2,1},{3,2},{0,3},{5,4},{6,5},{7,6},{4,7},{9,8},{10,9},{11,1... | collective-permute-start | bytes 1806344 | tf_op jit(solution)/shard_map/ppermute | solution.py:262
  9.1 9.9 %collective-permute-done.2.refs_2_ = bf16[48,6272]{1,0:T(8,128)(2,1)S(1)} collective-permute-done((bf16[48,6272]{1,0:T(8,128)(2,1)}, bf16[48,6272]{1,0:T(8,128)(2,1)S(1)}, u32[]{:S(2)}, u32[]{:S(2)}) %collective-permute-start.2) | collective-permute-done | bytes 602144 | tf_op jit(solution)/shard_map/ppermute | solution.py:262
  19.0 2.5 %collective-permute-start.4 = (bf16[48,6272]{1,0:T(8,128)(2,1)S(1)}, bf16[48,6272]{1,0:T(8,128)(2,1)}, u32[]{:S(2)}, u32[]{:S(2)}) collective-permute-start(bf16[48,6272]{1,0:T(8,128)(2,1)S(1)} %collective-permute-done.2.refs_2_), channel_id=1, source_target_pairs={{1,0},{2,1},{3,2},{0,3},{5,4},{6,5},{7,6},{4,7},{9,8},{10,9},{11,1... | collective-permute-start | bytes 1806344 | tf_op jit(solution)/shard_map/ppermute | solution.py:262
  21.4 0.5 collective-permute-done.1.refs_1_
  21.9 2.8 %collective-permute-start.5 = (bf16[48,6272]{1,0:T(8,128)(2,1)S(1)}, bf16[48,6272]{1,0:T(8,128)(2,1)}, u32[]{:S(2)}, u32[]{:S(2)}) collective-permute-start(bf16[48,6272]{1,0:T(8,128)(2,1)S(1)} %collective-permute-done.1.refs_1_), channel_id=1, source_target_pairs={{4,0},{5,1},{6,2},{7,3},{8,4},{9,5},{10,6},{11,7},{12,8},{13,9},{1... | collective-permute-start | bytes 1806344 | tf_op jit(solution)/shard_map/ppermute | solution.py:262
  24.7 0.0 collective-permute-done.3.refs_3_
  24.8 0.0 collective-permute-start.6
  24.8 0.0 collective-permute-done.refs_0_
  24.8 0.1 collective-permute-start.7
  24.9 6.1 %project.4 = bf16[16,16,768]{2,1,0:T(8,128)(2,1)} custom-call(bf16[48,6272]{1,0:T(8,128)(2,1)S(1)} %collective-permute-done.refs_0_, bf16[48,6272]{1,0:T(8,128)(2,1)S(1)} %collective-permute-done.1.refs_1_, bf16[48,6272]{1,0:T(8,128)(2,1)S(1)} %collective-permute-done.2.refs_2_, bf16[48,6272]{1,0:T(8,128)(2,1)S(1)} %collective-permute-done.3.refs_3_, ...), custom_call_target="tpu_custom_call" | custom-call | flops 1811939328 | bytes 11796480 | tf_op jit(solution)/shard_map/project/pallas_call | solution.py:92
  31.0 10.6 %all-to-all-start = ((bf16[16,16,768]{2,1,0:T(8,128)(2,1)}), bf16[16,16,768]{2,1,0:T(8,128)(2,1)S(1)}, u32[]{:S(2)}, u32[]{:S(2)}) async-start(bf16[16,16,768]{2,1,0:T(8,128)(2,1)} %project.4), calls=%async_computation | async-start | bytes 786432 | tf_op jit(solution)/shard_map/all_to_all | solution.py:278
  41.5 0.0 collective-permute-done.4.refs_0_
  41.5 3.0 %collective-permute-start.8 = (bf16[48,6272]{1,0:T(8,128)(2,1)}, bf16[48,6272]{1,0:T(8,128)(2,1)}, u32[]{:S(2)}, u32[]{:S(2)}) collective-permute-start(bf16[48,6272]{1,0:T(8,128)(2,1)} %collective-permute-done.4.refs_0_), channel_id=1, source_target_pairs={{1,0},{2,1},{3,2},{0,3},{5,4},{6,5},{7,6},{4,7},{9,8},{10,9},{11,1... | collective-permute-start | bytes 1806344 | tf_op jit(solution)/shard_map/ppermute | solution.py:262
  44.5 0.0 collective-permute-done.6.refs_2_
  44.5 0.0 collective-permute-start.9
  44.5 0.0 collective-permute-done.5.refs_1_
  44.5 3.0 %collective-permute-start.10 = (bf16[48,6272]{1,0:T(8,128)(2,1)}, bf16[48,6272]{1,0:T(8,128)(2,1)}, u32[]{:S(2)}, u32[]{:S(2)}) collective-permute-start(bf16[48,6272]{1,0:T(8,128)(2,1)} %collective-permute-done.5.refs_1_), channel_id=1, source_target_pairs={{4,0},{5,1},{6,2},{7,3},{8,4},{9,5},{10,6},{11,7},{12,8},{13,9},{1... | collective-permute-start | bytes 1806344 | tf_op jit(solution)/shard_map/ppermute | solution.py:262
  47.5 0.0 collective-permute-done.7.refs_3_
  47.5 0.0 collective-permute-start.11
  47.5 6.8 %project.5 = bf16[16,16,768]{2,1,0:T(8,128)(2,1)} custom-call(bf16[48,6272]{1,0:T(8,128)(2,1)} %collective-permute-done.4.refs_0_, bf16[48,6272]{1,0:T(8,128)(2,1)} %collective-permute-done.5.refs_1_, bf16[48,6272]{1,0:T(8,128)(2,1)} %collective-permute-done.6.refs_2_, bf16[48,6272]{1,0:T(8,128)(2,1)} %collective-permute-done.7.refs_3_, ...), custom_call_target="tpu_custom_call" | custom-call | flops 1811939328 | bytes 11796480 | tf_op jit(solution)/shard_map/project/pallas_call | solution.py:92
  54.4 1.7 %all-to-all-done.refs_0_ = bf16[16,16,768]{2,1,0:T(8,128)(2,1)S(1)} async-done(((bf16[16,16,768]{2,1,0:T(8,128)(2,1)}), bf16[16,16,768]{2,1,0:T(8,128)(2,1)S(1)}, u32[]{:S(2)}, u32[]{:S(2)}) %all-to-all-start) | async-done | bytes 393248 | tf_op jit(solution)/shard_map/all_to_all | solution.py:278
  56.1 6.0 %all-to-all-start.1 = ((bf16[16,16,768]{2,1,0:T(8,128)(2,1)}), bf16[16,16,768]{2,1,0:T(8,128)(2,1)S(1)}, u32[]{:S(2)}, u32[]{:S(2)}) async-start(bf16[16,16,768]{2,1,0:T(8,128)(2,1)} %project.5), calls=%async_computation.1 | async-start | bytes 786432 | tf_op jit(solution)/shard_map/all_to_all | solution.py:278
  62.1 0.0 copy-start
  62.1 3.0 %collective-permute-start.12 = (bf16[48,6272]{1,0:T(8,128)(2,1)S(1)}, bf16[48,6272]{1,0:T(8,128)(2,1)}, u32[]{:S(2)}, u32[]{:S(2)}) collective-permute-start(bf16[48,6272]{1,0:T(8,128)(2,1)S(1)} %collective-permute-done.refs_0_), channel_id=1, source_target_pairs={{1,0},{2,1},{3,2},{0,3},{5,4},{6,5},{7,6},{4,7},{9,8},{10,9},{11,1... | collective-permute-start | bytes 1806344 | tf_op jit(solution)/shard_map/ppermute | solution.py:262
  65.1 0.0 collective-permute-done.8.refs_0_
  65.1 2.9 %collective-permute-start.13 = (bf16[48,6272]{1,0:T(8,128)(2,1)S(1)}, bf16[48,6272]{1,0:T(8,128)(2,1)}, u32[]{:S(2)}, u32[]{:S(2)}) collective-permute-start(bf16[48,6272]{1,0:T(8,128)(2,1)S(1)} %collective-permute-done.2.refs_2_), channel_id=1, source_target_pairs={{4,0},{5,1},{6,2},{7,3},{8,4},{9,5},{10,6},{11,7},{12,8},{13,9},{1... | collective-permute-start | bytes 1806344 | tf_op jit(solution)/shard_map/ppermute | solution.py:262
  68.0 0.0 collective-permute-done.10.refs_2_
  68.0 0.0 collective-permute-start.14
  68.0 0.0 collective-permute-done.9.refs_1_
  68.0 0.0 collective-permute-done.11.refs_3_
  68.1 6.8 %project.6 = bf16[16,16,768]{2,1,0:T(8,128)(2,1)} custom-call(bf16[48,6272]{1,0:T(8,128)(2,1)} %collective-permute-done.8.refs_0_, bf16[48,6272]{1,0:T(8,128)(2,1)} %collective-permute-done.9.refs_1_, bf16[48,6272]{1,0:T(8,128)(2,1)} %collective-permute-done.10.refs_2_, bf16[48,6272]{1,0:T(8,128)(2,1)} %collective-permute-done.11.refs_3_, ...), custom_call_target="tpu_custom_call" | custom-call | flops 1811939328 | bytes 11796480 | tf_op jit(solution)/shard_map/project/pallas_call | solution.py:92
  74.9 1.8 %all-to-all-done.1.refs_1_ = bf16[16,16,768]{2,1,0:T(8,128)(2,1)S(1)} async-done(((bf16[16,16,768]{2,1,0:T(8,128)(2,1)}), bf16[16,16,768]{2,1,0:T(8,128)(2,1)S(1)}, u32[]{:S(2)}, u32[]{:S(2)}) %all-to-all-start.1) | async-done | bytes 393248 | tf_op jit(solution)/shard_map/all_to_all | solution.py:278
  76.7 6.0 %all-to-all-start.2 = ((bf16[16,16,768]{2,1,0:T(8,128)(2,1)}), bf16[16,16,768]{2,1,0:T(8,128)(2,1)S(1)}, u32[]{:S(2)}, u32[]{:S(2)}) async-start(bf16[16,16,768]{2,1,0:T(8,128)(2,1)} %project.6), calls=%async_computation.2 | async-start | bytes 786432 | tf_op jit(solution)/shard_map/all_to_all | solution.py:278
  82.6 0.0 copy-start.1
  82.6 0.0 collective-permute-done.12.refs_0_
  82.7 0.0 collective-permute-done.13.refs_1_
  82.7 1.4 %collective-permute-done.14.refs_2_ = bf16[48,6272]{1,0:T(8,128)(2,1)} collective-permute-done((bf16[48,6272]{1,0:T(8,128)(2,1)}, bf16[48,6272]{1,0:T(8,128)(2,1)}, u32[]{:S(2)}, u32[]{:S(2)}) %collective-permute-start.14) | collective-permute-done | bytes 602144 | tf_op jit(solution)/shard_map/ppermute | solution.py:262
  84.1 0.0 copy-done
  84.1 6.6 %project.7 = bf16[16,16,768]{2,1,0:T(8,128)(2,1)} custom-call(bf16[48,6272]{1,0:T(8,128)(2,1)} %collective-permute-done.12.refs_0_, bf16[48,6272]{1,0:T(8,128)(2,1)} %collective-permute-done.13.refs_1_, bf16[48,6272]{1,0:T(8,128)(2,1)} %collective-permute-done.14.refs_2_, bf16[48,6272]{1,0:T(8,128)(2,1)S(1)} %copy-done, bf16[3,6144,256]{2,1,0:T(8,128)(2,1)} %bitcast.29), custom_call_target="tpu_custom_call" | custom-call | flops 1811939328 | bytes 11796480 | tf_op jit(solution)/shard_map/project/pallas_call | solution.py:92
  90.7 6.5 %all-to-all-done.2.refs_2_ = bf16[16,16,768]{2,1,0:T(8,128)(2,1)S(1)} async-done(((bf16[16,16,768]{2,1,0:T(8,128)(2,1)}), bf16[16,16,768]{2,1,0:T(8,128)(2,1)S(1)}, u32[]{:S(2)}, u32[]{:S(2)}) %all-to-all-start.2) | async-done | bytes 393248 | tf_op jit(solution)/shard_map/all_to_all | solution.py:278
  97.2 3.7 %all-to-all-start.3 = ((bf16[16,16,768]{2,1,0:T(8,128)(2,1)}), bf16[16,16,768]{2,1,0:T(8,128)(2,1)S(1)}, u32[]{:S(2)}, u32[]{:S(2)}) async-start(bf16[16,16,768]{2,1,0:T(8,128)(2,1)} %project.7), calls=%async_computation.3 | async-start | bytes 786432 | tf_op jit(solution)/shard_map/all_to_all | solution.py:278
  101.0 0.0 copy-done.1
  101.0 0.2 copy.7.refs_4_
  101.2 0.1 stack.67.refs_2_
  101.3 0.5 assemble.1.refs_0_
  101.8 12.8 %all-to-all-done.3.refs_1_ = bf16[16,16,768]{2,1,0:T(8,128)(2,1)S(1)} async-done(((bf16[16,16,768]{2,1,0:T(8,128)(2,1)}), bf16[16,16,768]{2,1,0:T(8,128)(2,1)S(1)}, u32[]{:S(2)}, u32[]{:S(2)}) %all-to-all-start.3) | async-done | bytes 393248 | tf_op jit(solution)/shard_map/all_to_all | solution.py:278
  114.6 0.0 copy-start.2
  114.6 1.0 copy-done.2
  115.6 10.5 %attention.1 = (bf16[1024,256]{1,0:T(8,128)(2,1)}, bf16[3,1024,256]{2,1,0:T(8,128)(2,1)}) custom-call(bf16[768,768]{1,0:T(8,128)(2,1)S(1)} %assemble.1.refs_0_, bf16[16,16,768]{2,1,0:T(8,128)(2,1)S(1)} %all-to-all-done.3.refs_1_, s32[16]{0:T(128)S(1)} %stack.67.refs_2_, s32[1,1024]{1,0:T(1,128)S(1)} %copy-done.1, s32[1024,1]{1,0:T(8,128)S(1)} %copy.7.refs_4_, ...), custom_call_target="tpu_custom_call" | custom-call | flops 3221225472 | bytes 8388608 | tf_op jit(solution)/shard_map/attention/pallas_call | solution.py:232
Async XLA Ops:
  2.8 16.1 %collective-permute-start.2 = (bf16[48,6272]{1,0:T(8,128)(2,1)}, bf16[48,6272]{1,0:T(8,128)(2,1)S(1)}, u32[]{:S(2)}, u32[]{:S(2)}) collective-permute-start(bf16[48,6272]{1,0:T(8,128)(2,1)} %mark_rows.1.refs_3_), channel_id=1, source_target_pairs={{4,0},{5,1},{6,2},{7,3},{8,4},{9,5},{10,6},{11,7},{12,8},{13,9},{1... | collective-permute-start | bytes 1806344 | tf_op jit(solution)/shard_map/ppermute | solution.py:262
  6.4 15.6 %collective-permute-start.1 = (bf16[48,6272]{1,0:T(8,128)(2,1)}, bf16[48,6272]{1,0:T(8,128)(2,1)S(1)}, u32[]{:S(2)}, u32[]{:S(2)}) collective-permute-start(bf16[48,6272]{1,0:T(8,128)(2,1)} %mark_rows.1.refs_3_), channel_id=1, source_target_pairs={{3,0},{0,1},{1,2},{2,3},{7,4},{4,5},{5,6},{6,7},{11,8},{8,9},{9,10... | collective-permute-start | bytes 1806344 | tf_op jit(solution)/shard_map/ppermute | solution.py:262
  7.6 17.2 %collective-permute-start.3 = (bf16[48,6272]{1,0:T(8,128)(2,1)}, bf16[48,6272]{1,0:T(8,128)(2,1)S(1)}, u32[]{:S(2)}, u32[]{:S(2)}) collective-permute-start(bf16[48,6272]{1,0:T(8,128)(2,1)} %mark_rows.1.refs_3_), channel_id=1, source_target_pairs={{12,0},{13,1},{14,2},{15,3},{0,4},{1,5},{2,6},{3,7},{4,8},{5,9},{6... | collective-permute-start | bytes 1806344 | tf_op jit(solution)/shard_map/ppermute | solution.py:262
  7.6 17.2 %collective-permute-start = (bf16[48,6272]{1,0:T(8,128)(2,1)}, bf16[48,6272]{1,0:T(8,128)(2,1)S(1)}, u32[]{:S(2)}, u32[]{:S(2)}) collective-permute-start(bf16[48,6272]{1,0:T(8,128)(2,1)} %mark_rows.1.refs_3_), channel_id=1, source_target_pairs={{1,0},{2,1},{3,2},{0,3},{5,4},{6,5},{7,6},{4,7},{9,8},{10,9},{11,1... | collective-permute-start | bytes 1806344 | tf_op jit(solution)/shard_map/ppermute | solution.py:262
  19.0 22.6 %collective-permute-start.4 = (bf16[48,6272]{1,0:T(8,128)(2,1)S(1)}, bf16[48,6272]{1,0:T(8,128)(2,1)}, u32[]{:S(2)}, u32[]{:S(2)}) collective-permute-start(bf16[48,6272]{1,0:T(8,128)(2,1)S(1)} %collective-permute-done.2.refs_2_), channel_id=1, source_target_pairs={{1,0},{2,1},{3,2},{0,3},{5,4},{6,5},{7,6},{4,7},{9,8},{10,9},{11,1... | collective-permute-start | bytes 1806344 | tf_op jit(solution)/shard_map/ppermute | solution.py:262
  21.9 22.6 %collective-permute-start.5 = (bf16[48,6272]{1,0:T(8,128)(2,1)S(1)}, bf16[48,6272]{1,0:T(8,128)(2,1)}, u32[]{:S(2)}, u32[]{:S(2)}) collective-permute-start(bf16[48,6272]{1,0:T(8,128)(2,1)S(1)} %collective-permute-done.1.refs_1_), channel_id=1, source_target_pairs={{4,0},{5,1},{6,2},{7,3},{8,4},{9,5},{10,6},{11,7},{12,8},{13,9},{1... | collective-permute-start | bytes 1806344 | tf_op jit(solution)/shard_map/ppermute | solution.py:262
  24.8 19.8 %collective-permute-start.6 = (bf16[48,6272]{1,0:T(8,128)(2,1)S(1)}, bf16[48,6272]{1,0:T(8,128)(2,1)}, u32[]{:S(2)}, u32[]{:S(2)}) collective-permute-start(bf16[48,6272]{1,0:T(8,128)(2,1)S(1)} %collective-permute-done.3.refs_3_), channel_id=1, source_target_pairs={{3,0},{0,1},{1,2},{2,3},{7,4},{4,5},{5,6},{6,7},{11,8},{8,9},{9,10... | collective-permute-start | bytes 1806344 | tf_op jit(solution)/shard_map/ppermute | solution.py:262
  24.8 22.8 %collective-permute-start.7 = (bf16[48,6272]{1,0:T(8,128)(2,1)S(1)}, bf16[48,6272]{1,0:T(8,128)(2,1)}, u32[]{:S(2)}, u32[]{:S(2)}) collective-permute-start(bf16[48,6272]{1,0:T(8,128)(2,1)S(1)} %collective-permute-done.refs_0_), channel_id=1, source_target_pairs={{12,0},{13,1},{14,2},{15,3},{0,4},{1,5},{2,6},{3,7},{4,8},{5,9},{6... | collective-permute-start | bytes 1806344 | tf_op jit(solution)/shard_map/ppermute | solution.py:262
  31.0 25.1 %all-to-all-start = ((bf16[16,16,768]{2,1,0:T(8,128)(2,1)}), bf16[16,16,768]{2,1,0:T(8,128)(2,1)S(1)}, u32[]{:S(2)}, u32[]{:S(2)}) async-start(bf16[16,16,768]{2,1,0:T(8,128)(2,1)} %project.4), calls=%async_computation | async-start | bytes 786432 | tf_op jit(solution)/shard_map/all_to_all | solution.py:278
  41.5 23.6 %collective-permute-start.8 = (bf16[48,6272]{1,0:T(8,128)(2,1)}, bf16[48,6272]{1,0:T(8,128)(2,1)}, u32[]{:S(2)}, u32[]{:S(2)}) collective-permute-start(bf16[48,6272]{1,0:T(8,128)(2,1)} %collective-permute-done.4.refs_0_), channel_id=1, source_target_pairs={{1,0},{2,1},{3,2},{0,3},{5,4},{6,5},{7,6},{4,7},{9,8},{10,9},{11,1... | collective-permute-start | bytes 1806344 | tf_op jit(solution)/shard_map/ppermute | solution.py:262
  44.5 23.5 %collective-permute-start.9 = (bf16[48,6272]{1,0:T(8,128)(2,1)}, bf16[48,6272]{1,0:T(8,128)(2,1)}, u32[]{:S(2)}, u32[]{:S(2)}) collective-permute-start(bf16[48,6272]{1,0:T(8,128)(2,1)} %collective-permute-done.6.refs_2_), channel_id=1, source_target_pairs={{3,0},{0,1},{1,2},{2,3},{7,4},{4,5},{5,6},{6,7},{11,8},{8,9},{9,10... | collective-permute-start | bytes 1806344 | tf_op jit(solution)/shard_map/ppermute | solution.py:262
  44.5 23.5 %collective-permute-start.10 = (bf16[48,6272]{1,0:T(8,128)(2,1)}, bf16[48,6272]{1,0:T(8,128)(2,1)}, u32[]{:S(2)}, u32[]{:S(2)}) collective-permute-start(bf16[48,6272]{1,0:T(8,128)(2,1)} %collective-permute-done.5.refs_1_), channel_id=1, source_target_pairs={{4,0},{5,1},{6,2},{7,3},{8,4},{9,5},{10,6},{11,7},{12,8},{13,9},{1... | collective-permute-start | bytes 1806344 | tf_op jit(solution)/shard_map/ppermute | solution.py:262
  47.5 20.5 %collective-permute-start.11 = (bf16[48,6272]{1,0:T(8,128)(2,1)}, bf16[48,6272]{1,0:T(8,128)(2,1)}, u32[]{:S(2)}, u32[]{:S(2)}) collective-permute-start(bf16[48,6272]{1,0:T(8,128)(2,1)} %collective-permute-done.7.refs_3_), channel_id=1, source_target_pairs={{12,0},{13,1},{14,2},{15,3},{0,4},{1,5},{2,6},{3,7},{4,8},{5,9},{6... | collective-permute-start | bytes 1806344 | tf_op jit(solution)/shard_map/ppermute | solution.py:262
  56.1 20.6 %all-to-all-start.1 = ((bf16[16,16,768]{2,1,0:T(8,128)(2,1)}), bf16[16,16,768]{2,1,0:T(8,128)(2,1)S(1)}, u32[]{:S(2)}, u32[]{:S(2)}) async-start(bf16[16,16,768]{2,1,0:T(8,128)(2,1)} %project.5), calls=%async_computation.1 | async-start | bytes 786432 | tf_op jit(solution)/shard_map/all_to_all | solution.py:278
  62.1 21.9 %copy-start = (bf16[48,6272]{1,0:T(8,128)(2,1)S(1)}, bf16[48,6272]{1,0:T(8,128)(2,1)}, u32[]{:S(2)}) copy-start(bf16[48,6272]{1,0:T(8,128)(2,1)} %mark_rows.1.refs_3_) | copy-start | bytes 1806340
  62.1 20.5 %collective-permute-start.12 = (bf16[48,6272]{1,0:T(8,128)(2,1)S(1)}, bf16[48,6272]{1,0:T(8,128)(2,1)}, u32[]{:S(2)}, u32[]{:S(2)}) collective-permute-start(bf16[48,6272]{1,0:T(8,128)(2,1)S(1)} %collective-permute-done.refs_0_), channel_id=1, source_target_pairs={{1,0},{2,1},{3,2},{0,3},{5,4},{6,5},{7,6},{4,7},{9,8},{10,9},{11,1... | collective-permute-start | bytes 1806344 | tf_op jit(solution)/shard_map/ppermute | solution.py:262
  65.1 17.5 %collective-permute-start.13 = (bf16[48,6272]{1,0:T(8,128)(2,1)S(1)}, bf16[48,6272]{1,0:T(8,128)(2,1)}, u32[]{:S(2)}, u32[]{:S(2)}) collective-permute-start(bf16[48,6272]{1,0:T(8,128)(2,1)S(1)} %collective-permute-done.2.refs_2_), channel_id=1, source_target_pairs={{4,0},{5,1},{6,2},{7,3},{8,4},{9,5},{10,6},{11,7},{12,8},{13,9},{1... | collective-permute-start | bytes 1806344 | tf_op jit(solution)/shard_map/ppermute | solution.py:262
  68.0 16.0 %collective-permute-start.14 = (bf16[48,6272]{1,0:T(8,128)(2,1)}, bf16[48,6272]{1,0:T(8,128)(2,1)}, u32[]{:S(2)}, u32[]{:S(2)}) collective-permute-start(bf16[48,6272]{1,0:T(8,128)(2,1)} %collective-permute-done.10.refs_2_), channel_id=1, source_target_pairs={{3,0},{0,1},{1,2},{2,3},{7,4},{4,5},{5,6},{6,7},{11,8},{8,9},{9,10... | collective-permute-start | bytes 1806344 | tf_op jit(solution)/shard_map/ppermute | solution.py:262
  76.7 20.5 %all-to-all-start.2 = ((bf16[16,16,768]{2,1,0:T(8,128)(2,1)}), bf16[16,16,768]{2,1,0:T(8,128)(2,1)S(1)}, u32[]{:S(2)}, u32[]{:S(2)}) async-start(bf16[16,16,768]{2,1,0:T(8,128)(2,1)} %project.6), calls=%async_computation.2 | async-start | bytes 786432 | tf_op jit(solution)/shard_map/all_to_all | solution.py:278
  82.6 18.4 %copy-start.1 = (s32[1,1024]{1,0:T(1,128)S(1)}, s32[1,1024]{1,0:T(1,128)}, u32[]{:S(2)}) copy-start(s32[1,1024]{1,0:T(1,128)} %refs_3_.1) | copy-start | bytes 12292
  97.2 17.4 %all-to-all-start.3 = ((bf16[16,16,768]{2,1,0:T(8,128)(2,1)}), bf16[16,16,768]{2,1,0:T(8,128)(2,1)S(1)}, u32[]{:S(2)}, u32[]{:S(2)}) async-start(bf16[16,16,768]{2,1,0:T(8,128)(2,1)} %project.7), calls=%async_computation.3 | async-start | bytes 786432 | tf_op jit(solution)/shard_map/all_to_all | solution.py:278
  114.6 1.0 copy-start.2

commit v4 on v3

--- a/solution.py
+++ b/solution.py
@@ -156,7 +156,9 @@
 
     def body(*refs):
         early_ref, last_ref = refs[:2]
-        to_ref, segk_ref, segq_ref, cot_ref, out_ref, grad_ref, qkv, keep, codes, dk, dv, low = refs[2:]
+        to_ref, segk_ref, segq_ref, cot_hbm, out_ref, grad_ref, cot_ref, cot_here, qkv, keep, codes, dk, dv, low = refs[2:]
+        load = pltpu.make_async_copy(cot_hbm, cot_ref, cot_here)
+        load.start()
         before = early.shape[0] // span
         late = by_source(last_ref[...], cols)
         for i in range(before + each // CAP):
@@ -211,6 +213,7 @@
                 low[...] = jnp.minimum(low[...], jnp.min(jnp.where(live > 0, top, 0.0), axis=0, keepdims=True))
 
         clear()
+        load.wait()
         for b in range(blocks):
             first, last = max(b - 1, 0), min(b + 2, blocks)
             work(b * block, first * block, (last - first) * block)
@@ -231,13 +234,15 @@
     vmem = pl.BlockSpec(memory_space=pltpu.VMEM)
     return pl.pallas_call(
         body,
-        in_specs=[vmem] * 2 + [pl.BlockSpec(memory_space=pltpu.SMEM)] + [vmem] * 3,
+        in_specs=[vmem] * 2 + [pl.BlockSpec(memory_space=pltpu.SMEM)] + [vmem] * 2 + [pl.BlockSpec(memory_space=pltpu.HBM)],
         out_specs=[vmem, vmem],
         out_shape=[
             jax.ShapeDtypeStruct((pack_len, third), jnp.bfloat16),
             jax.ShapeDtypeStruct((3, pack_len, third), jnp.bfloat16),
         ],
         scratch_shapes=[
+            pltpu.VMEM(cotangent.shape, jnp.bfloat16),
+            pltpu.SemaphoreType.DMA,
             pltpu.VMEM((pack_len, cols), jnp.bfloat16),
             pltpu.VMEM((pack_len, HD), f32),
             pltpu.VMEM((1, pack_len), jnp.int32),
@@ -250,7 +255,7 @@
             flops=12 * pack_len * pack_len * third, transcendentals=pack_len * pack_len * heads, bytes_accessed=1 << 23
         ),
         name="attention",
-    )(early, last, where_to, segments, segments.reshape(pack_len, 1), cotangent)
+    )(early, last, where_to, segments, segments.reshape(pack_len, 1), pltpu.with_memory_space_constraint(cotangent, pltpu.HBM))
 
 
 def receive(block, link):

time: 127 us -> 127 us (level)
  no operation moved by 1% of the time
where the time goes in v4:
time: 127 us; the launch traced here: 126 us
  starting transfers between devices  49.7 us (39%)
  Pallas kernels  40.3 us (32%)
  waiting for transfers between devices  34.6 us (27%)
    pallas_call x4, Pallas kernels, project(): pl.pallas_call(body, grid=(STEPS,), in_specs=[full] * count + [pl.BlockSp...  26.3 us
    all_to_all x4, starting transfers between devices, per_device(): lax.all_to_all(placed, 'dp', split_axis=0, concat_axis=0, tiled=True)  26.2 us
    ppermute x15, starting transfers between devices, receive(): return lax.ppermute(block, 'seq', pairs)  23.5 us
    all_to_all x4, waiting for transfers between devices, per_device(): lax.all_to_all(placed, 'dp', split_axis=0, concat_axis=0, tiled=True)  22.8 us
    ppermute x15, waiting for transfers between devices, receive(): return lax.ppermute(block, 'seq', pairs)  11.8 us
    pallas_call x1, Pallas kernels, attention(): pl.pallas_call(body, in_specs=[vmem] * 2 + [pl.BlockSpec(memory_space=plt...  11.3 us
  transfers between devices with their start and end apart: 19, of which 7 were waited for; matrix products, arithmetic and copies ran while one was open for 0% of the time, Pallas kernels for 21%

profile of v4, /device:TPU:1, one launch (start us, length us, event | category | flops | bytes accessed | tf_op | source)
XLA Modules:
  0.0 126.1 jit_solution(2859287201191879709)
XLA Ops:
  0.6 2.2 %mark_rows.1.refs_3_ = bf16[48,6272]{1,0:T(8,128)(2,1)} custom-call(bf16[48,6144]{1,0:T(8,128)(2,1)} %x_ref.1, s32[1,48]{1,0:T(1,128)} %bitcast.29), custom_call_target="tpu_custom_call" | custom-call | tf_op jit(solution)/shard_map/mark_rows/pallas_call | solution.py:42
  2.8 3.6 %collective-permute-start.2 = (bf16[48,6272]{1,0:T(8,128)(2,1)}, bf16[48,6272]{1,0:T(8,128)(2,1)S(1)}, u32[]{:S(2)}, u32[]{:S(2)}) collective-permute-start(bf16[48,6272]{1,0:T(8,128)(2,1)} %mark_rows.1.refs_3_), channel_id=1, source_target_pairs={{4,0},{5,1},{6,2},{7,3},{8,4},{9,5},{10,6},{11,7},{12,8},{13,9},{1... | collective-permute-start | bytes 1806344 | tf_op jit(solution)/shard_map/ppermute | solution.py:267
  6.4 1.2 collective-permute-start.1
  7.6 0.0 collective-permute-start.3
  7.6 1.5 %collective-permute-start = (bf16[48,6272]{1,0:T(8,128)(2,1)}, bf16[48,6272]{1,0:T(8,128)(2,1)S(1)}, u32[]{:S(2)}, u32[]{:S(2)}) collective-permute-start(bf16[48,6272]{1,0:T(8,128)(2,1)} %mark_rows.1.refs_3_), channel_id=1, source_target_pairs={{1,0},{2,1},{3,2},{0,3},{5,4},{6,5},{7,6},{4,7},{9,8},{10,9},{11,1... | collective-permute-start | bytes 1806344 | tf_op jit(solution)/shard_map/ppermute | solution.py:267
  9.1 9.9 %collective-permute-done.2.refs_2_ = bf16[48,6272]{1,0:T(8,128)(2,1)S(1)} collective-permute-done((bf16[48,6272]{1,0:T(8,128)(2,1)}, bf16[48,6272]{1,0:T(8,128)(2,1)S(1)}, u32[]{:S(2)}, u32[]{:S(2)}) %collective-permute-start.2) | collective-permute-done | bytes 602144 | tf_op jit(solution)/shard_map/ppermute | solution.py:267
  19.0 2.5 %collective-permute-start.4 = (bf16[48,6272]{1,0:T(8,128)(2,1)S(1)}, bf16[48,6272]{1,0:T(8,128)(2,1)}, u32[]{:S(2)}, u32[]{:S(2)}) collective-permute-start(bf16[48,6272]{1,0:T(8,128)(2,1)S(1)} %collective-permute-done.2.refs_2_), channel_id=1, source_target_pairs={{1,0},{2,1},{3,2},{0,3},{5,4},{6,5},{7,6},{4,7},{9,8},{10,9},{11,1... | collective-permute-start | bytes 1806344 | tf_op jit(solution)/shard_map/ppermute | solution.py:267
  21.4 0.5 collective-permute-done.1.refs_1_
  21.9 2.8 %collective-permute-start.5 = (bf16[48,6272]{1,0:T(8,128)(2,1)S(1)}, bf16[48,6272]{1,0:T(8,128)(2,1)}, u32[]{:S(2)}, u32[]{:S(2)}) collective-permute-start(bf16[48,6272]{1,0:T(8,128)(2,1)S(1)} %collective-permute-done.1.refs_1_), channel_id=1, source_target_pairs={{4,0},{5,1},{6,2},{7,3},{8,4},{9,5},{10,6},{11,7},{12,8},{13,9},{1... | collective-permute-start | bytes 1806344 | tf_op jit(solution)/shard_map/ppermute | solution.py:267
  24.7 0.0 collective-permute-done.3.refs_3_
  24.8 0.0 collective-permute-start.6
  24.8 0.0 collective-permute-done.refs_0_
  24.8 0.1 collective-permute-start.7
  24.9 6.1 %project.4 = bf16[16,16,768]{2,1,0:T(8,128)(2,1)} custom-call(bf16[48,6272]{1,0:T(8,128)(2,1)S(1)} %collective-permute-done.refs_0_, bf16[48,6272]{1,0:T(8,128)(2,1)S(1)} %collective-permute-done.1.refs_1_, bf16[48,6272]{1,0:T(8,128)(2,1)S(1)} %collective-permute-done.2.refs_2_, bf16[48,6272]{1,0:T(8,128)(2,1)S(1)} %collective-permute-done.3.refs_3_, ...), custom_call_target="tpu_custom_call" | custom-call | flops 1811939328 | bytes 11796480 | tf_op jit(solution)/shard_map/project/pallas_call | solution.py:92
  31.0 10.6 %all-to-all-start = ((bf16[16,16,768]{2,1,0:T(8,128)(2,1)}), bf16[16,16,768]{2,1,0:T(8,128)(2,1)S(1)}, u32[]{:S(2)}, u32[]{:S(2)}) async-start(bf16[16,16,768]{2,1,0:T(8,128)(2,1)} %project.4), calls=%async_computation | async-start | bytes 786432 | tf_op jit(solution)/shard_map/all_to_all | solution.py:283
  41.5 0.0 collective-permute-done.4.refs_0_
  41.5 3.0 %collective-permute-start.8 = (bf16[48,6272]{1,0:T(8,128)(2,1)}, bf16[48,6272]{1,0:T(8,128)(2,1)}, u32[]{:S(2)}, u32[]{:S(2)}) collective-permute-start(bf16[48,6272]{1,0:T(8,128)(2,1)} %collective-permute-done.4.refs_0_), channel_id=1, source_target_pairs={{1,0},{2,1},{3,2},{0,3},{5,4},{6,5},{7,6},{4,7},{9,8},{10,9},{11,1... | collective-permute-start | bytes 1806344 | tf_op jit(solution)/shard_map/ppermute | solution.py:267
  44.5 0.0 collective-permute-done.6.refs_2_
  44.5 0.0 collective-permute-start.9
  44.5 0.0 collective-permute-done.5.refs_1_
  44.5 3.0 %collective-permute-start.10 = (bf16[48,6272]{1,0:T(8,128)(2,1)}, bf16[48,6272]{1,0:T(8,128)(2,1)}, u32[]{:S(2)}, u32[]{:S(2)}) collective-permute-start(bf16[48,6272]{1,0:T(8,128)(2,1)} %collective-permute-done.5.refs_1_), channel_id=1, source_target_pairs={{4,0},{5,1},{6,2},{7,3},{8,4},{9,5},{10,6},{11,7},{12,8},{13,9},{1... | collective-permute-start | bytes 1806344 | tf_op jit(solution)/shard_map/ppermute | solution.py:267
  47.5 0.0 collective-permute-done.7.refs_3_
  47.5 0.0 collective-permute-start.11
  47.5 6.8 %project.5 = bf16[16,16,768]{2,1,0:T(8,128)(2,1)} custom-call(bf16[48,6272]{1,0:T(8,128)(2,1)} %collective-permute-done.4.refs_0_, bf16[48,6272]{1,0:T(8,128)(2,1)} %collective-permute-done.5.refs_1_, bf16[48,6272]{1,0:T(8,128)(2,1)} %collective-permute-done.6.refs_2_, bf16[48,6272]{1,0:T(8,128)(2,1)} %collective-permute-done.7.refs_3_, ...), custom_call_target="tpu_custom_call" | custom-call | flops 1811939328 | bytes 11796480 | tf_op jit(solution)/shard_map/project/pallas_call | solution.py:92
  54.4 1.7 %all-to-all-done.refs_0_ = bf16[16,16,768]{2,1,0:T(8,128)(2,1)S(1)} async-done(((bf16[16,16,768]{2,1,0:T(8,128)(2,1)}), bf16[16,16,768]{2,1,0:T(8,128)(2,1)S(1)}, u32[]{:S(2)}, u32[]{:S(2)}) %all-to-all-start) | async-done | bytes 393248 | tf_op jit(solution)/shard_map/all_to_all | solution.py:283
  56.1 6.0 %all-to-all-start.1 = ((bf16[16,16,768]{2,1,0:T(8,128)(2,1)}), bf16[16,16,768]{2,1,0:T(8,128)(2,1)S(1)}, u32[]{:S(2)}, u32[]{:S(2)}) async-start(bf16[16,16,768]{2,1,0:T(8,128)(2,1)} %project.5), calls=%async_computation.1 | async-start | bytes 786432 | tf_op jit(solution)/shard_map/all_to_all | solution.py:283
  62.1 0.0 copy-start
  62.1 3.0 %collective-permute-start.12 = (bf16[48,6272]{1,0:T(8,128)(2,1)S(1)}, bf16[48,6272]{1,0:T(8,128)(2,1)}, u32[]{:S(2)}, u32[]{:S(2)}) collective-permute-start(bf16[48,6272]{1,0:T(8,128)(2,1)S(1)} %collective-permute-done.refs_0_), channel_id=1, source_target_pairs={{1,0},{2,1},{3,2},{0,3},{5,4},{6,5},{7,6},{4,7},{9,8},{10,9},{11,1... | collective-permute-start | bytes 1806344 | tf_op jit(solution)/shard_map/ppermute | solution.py:267
  65.1 0.0 collective-permute-done.8.refs_0_
  65.1 2.9 %collective-permute-start.13 = (bf16[48,6272]{1,0:T(8,128)(2,1)S(1)}, bf16[48,6272]{1,0:T(8,128)(2,1)}, u32[]{:S(2)}, u32[]{:S(2)}) collective-permute-start(bf16[48,6272]{1,0:T(8,128)(2,1)S(1)} %collective-permute-done.2.refs_2_), channel_id=1, source_target_pairs={{4,0},{5,1},{6,2},{7,3},{8,4},{9,5},{10,6},{11,7},{12,8},{13,9},{1... | collective-permute-start | bytes 1806344 | tf_op jit(solution)/shard_map/ppermute | solution.py:267
  68.0 0.0 collective-permute-done.10.refs_2_
  68.0 0.0 collective-permute-start.14
  68.0 0.0 collective-permute-done.9.refs_1_
  68.0 0.0 collective-permute-done.11.refs_3_
  68.1 6.8 %project.6 = bf16[16,16,768]{2,1,0:T(8,128)(2,1)} custom-call(bf16[48,6272]{1,0:T(8,128)(2,1)} %collective-permute-done.8.refs_0_, bf16[48,6272]{1,0:T(8,128)(2,1)} %collective-permute-done.9.refs_1_, bf16[48,6272]{1,0:T(8,128)(2,1)} %collective-permute-done.10.refs_2_, bf16[48,6272]{1,0:T(8,128)(2,1)} %collective-permute-done.11.refs_3_, ...), custom_call_target="tpu_custom_call" | custom-call | flops 1811939328 | bytes 11796480 | tf_op jit(solution)/shard_map/project/pallas_call | solution.py:92
  74.9 1.8 %all-to-all-done.1.refs_1_ = bf16[16,16,768]{2,1,0:T(8,128)(2,1)S(1)} async-done(((bf16[16,16,768]{2,1,0:T(8,128)(2,1)}), bf16[16,16,768]{2,1,0:T(8,128)(2,1)S(1)}, u32[]{:S(2)}, u32[]{:S(2)}) %all-to-all-start.1) | async-done | bytes 393248 | tf_op jit(solution)/shard_map/all_to_all | solution.py:283
  76.7 6.0 %all-to-all-start.2 = ((bf16[16,16,768]{2,1,0:T(8,128)(2,1)}), bf16[16,16,768]{2,1,0:T(8,128)(2,1)S(1)}, u32[]{:S(2)}, u32[]{:S(2)}) async-start(bf16[16,16,768]{2,1,0:T(8,128)(2,1)} %project.6), calls=%async_computation.2 | async-start | bytes 786432 | tf_op jit(solution)/shard_map/all_to_all | solution.py:283
  82.6 0.0 copy-start.1
  82.6 0.0 collective-permute-done.12.refs_0_
  82.7 0.0 collective-permute-done.13.refs_1_
  82.7 1.4 %collective-permute-done.14.refs_2_ = bf16[48,6272]{1,0:T(8,128)(2,1)} collective-permute-done((bf16[48,6272]{1,0:T(8,128)(2,1)}, bf16[48,6272]{1,0:T(8,128)(2,1)}, u32[]{:S(2)}, u32[]{:S(2)}) %collective-permute-start.14) | collective-permute-done | bytes 602144 | tf_op jit(solution)/shard_map/ppermute | solution.py:267
  84.1 0.0 copy-done
  84.1 6.6 %project.7 = bf16[16,16,768]{2,1,0:T(8,128)(2,1)} custom-call(bf16[48,6272]{1,0:T(8,128)(2,1)} %collective-permute-done.12.refs_0_, bf16[48,6272]{1,0:T(8,128)(2,1)} %collective-permute-done.13.refs_1_, bf16[48,6272]{1,0:T(8,128)(2,1)} %collective-permute-done.14.refs_2_, bf16[48,6272]{1,0:T(8,128)(2,1)S(1)} %copy-done, bf16[3,6144,256]{2,1,0:T(8,128)(2,1)} %bitcast.28), custom_call_target="tpu_custom_call" | custom-call | flops 1811939328 | bytes 11796480 | tf_op jit(solution)/shard_map/project/pallas_call | solution.py:92
  90.7 6.5 %all-to-all-done.2.refs_2_ = bf16[16,16,768]{2,1,0:T(8,128)(2,1)S(1)} async-done(((bf16[16,16,768]{2,1,0:T(8,128)(2,1)}), bf16[16,16,768]{2,1,0:T(8,128)(2,1)S(1)}, u32[]{:S(2)}, u32[]{:S(2)}) %all-to-all-start.2) | async-done | bytes 393248 | tf_op jit(solution)/shard_map/all_to_all | solution.py:283
  97.2 3.7 %all-to-all-start.3 = ((bf16[16,16,768]{2,1,0:T(8,128)(2,1)}), bf16[16,16,768]{2,1,0:T(8,128)(2,1)S(1)}, u32[]{:S(2)}, u32[]{:S(2)}) async-start(bf16[16,16,768]{2,1,0:T(8,128)(2,1)} %project.7), calls=%async_computation.3 | async-start | bytes 786432 | tf_op jit(solution)/shard_map/all_to_all | solution.py:283
  101.0 0.0 copy-done.1
  101.0 0.2 copy.7.refs_4_
  101.2 0.1 stack.67.refs_2_
  101.3 0.5 assemble.1.refs_0_
  101.8 12.8 %all-to-all-done.3.refs_1_ = bf16[16,16,768]{2,1,0:T(8,128)(2,1)S(1)} async-done(((bf16[16,16,768]{2,1,0:T(8,128)(2,1)}), bf16[16,16,768]{2,1,0:T(8,128)(2,1)S(1)}, u32[]{:S(2)}, u32[]{:S(2)}) %all-to-all-start.3) | async-done | bytes 393248 | tf_op jit(solution)/shard_map/all_to_all | solution.py:283
  114.6 11.3 %attention.1 = (bf16[1024,256]{1,0:T(8,128)(2,1)}, bf16[3,1024,256]{2,1,0:T(8,128)(2,1)}) custom-call(bf16[768,768]{1,0:T(8,128)(2,1)S(1)} %assemble.1.refs_0_, bf16[16,16,768]{2,1,0:T(8,128)(2,1)S(1)} %all-to-all-done.3.refs_1_, s32[16]{0:T(128)S(1)} %stack.67.refs_2_, s32[1,1024]{1,0:T(1,128)S(1)} %copy-done.1, s32[1024,1]{1,0:T(8,128)S(1)} %copy.7.refs_4_, ...), custom_call_target="tpu_custom_call" | custom-call | flops 3221225472 | bytes 8388608 | tf_op jit(solution)/shard_map/attention/pallas_call | solution.py:235
Async XLA Ops:
  2.8 16.1 %collective-permute-start.2 = (bf16[48,6272]{1,0:T(8,128)(2,1)}, bf16[48,6272]{1,0:T(8,128)(2,1)S(1)}, u32[]{:S(2)}, u32[]{:S(2)}) collective-permute-start(bf16[48,6272]{1,0:T(8,128)(2,1)} %mark_rows.1.refs_3_), channel_id=1, source_target_pairs={{4,0},{5,1},{6,2},{7,3},{8,4},{9,5},{10,6},{11,7},{12,8},{13,9},{1... | collective-permute-start | bytes 1806344 | tf_op jit(solution)/shard_map/ppermute | solution.py:267
  6.4 15.6 %collective-permute-start.1 = (bf16[48,6272]{1,0:T(8,128)(2,1)}, bf16[48,6272]{1,0:T(8,128)(2,1)S(1)}, u32[]{:S(2)}, u32[]{:S(2)}) collective-permute-start(bf16[48,6272]{1,0:T(8,128)(2,1)} %mark_rows.1.refs_3_), channel_id=1, source_target_pairs={{3,0},{0,1},{1,2},{2,3},{7,4},{4,5},{5,6},{6,7},{11,8},{8,9},{9,10... | collective-permute-start | bytes 1806344 | tf_op jit(solution)/shard_map/ppermute | solution.py:267
  7.6 17.2 %collective-permute-start.3 = (bf16[48,6272]{1,0:T(8,128)(2,1)}, bf16[48,6272]{1,0:T(8,128)(2,1)S(1)}, u32[]{:S(2)}, u32[]{:S(2)}) collective-permute-start(bf16[48,6272]{1,0:T(8,128)(2,1)} %mark_rows.1.refs_3_), channel_id=1, source_target_pairs={{12,0},{13,1},{14,2},{15,3},{0,4},{1,5},{2,6},{3,7},{4,8},{5,9},{6... | collective-permute-start | bytes 1806344 | tf_op jit(solution)/shard_map/ppermute | solution.py:267
  7.6 17.2 %collective-permute-start = (bf16[48,6272]{1,0:T(8,128)(2,1)}, bf16[48,6272]{1,0:T(8,128)(2,1)S(1)}, u32[]{:S(2)}, u32[]{:S(2)}) collective-permute-start(bf16[48,6272]{1,0:T(8,128)(2,1)} %mark_rows.1.refs_3_), channel_id=1, source_target_pairs={{1,0},{2,1},{3,2},{0,3},{5,4},{6,5},{7,6},{4,7},{9,8},{10,9},{11,1... | collective-permute-start | bytes 1806344 | tf_op jit(solution)/shard_map/ppermute | solution.py:267
  19.0 22.6 %collective-permute-start.4 = (bf16[48,6272]{1,0:T(8,128)(2,1)S(1)}, bf16[48,6272]{1,0:T(8,128)(2,1)}, u32[]{:S(2)}, u32[]{:S(2)}) collective-permute-start(bf16[48,6272]{1,0:T(8,128)(2,1)S(1)} %collective-permute-done.2.refs_2_), channel_id=1, source_target_pairs={{1,0},{2,1},{3,2},{0,3},{5,4},{6,5},{7,6},{4,7},{9,8},{10,9},{11,1... | collective-permute-start | bytes 1806344 | tf_op jit(solution)/shard_map/ppermute | solution.py:267
  21.9 22.6 %collective-permute-start.5 = (bf16[48,6272]{1,0:T(8,128)(2,1)S(1)}, bf16[48,6272]{1,0:T(8,128)(2,1)}, u32[]{:S(2)}, u32[]{:S(2)}) collective-permute-start(bf16[48,6272]{1,0:T(8,128)(2,1)S(1)} %collective-permute-done.1.refs_1_), channel_id=1, source_target_pairs={{4,0},{5,1},{6,2},{7,3},{8,4},{9,5},{10,6},{11,7},{12,8},{13,9},{1... | collective-permute-start | bytes 1806344 | tf_op jit(solution)/shard_map/ppermute | solution.py:267
  24.8 19.8 %collective-permute-start.6 = (bf16[48,6272]{1,0:T(8,128)(2,1)S(1)}, bf16[48,6272]{1,0:T(8,128)(2,1)}, u32[]{:S(2)}, u32[]{:S(2)}) collective-permute-start(bf16[48,6272]{1,0:T(8,128)(2,1)S(1)} %collective-permute-done.3.refs_3_), channel_id=1, source_target_pairs={{3,0},{0,1},{1,2},{2,3},{7,4},{4,5},{5,6},{6,7},{11,8},{8,9},{9,10... | collective-permute-start | bytes 1806344 | tf_op jit(solution)/shard_map/ppermute | solution.py:267
  24.8 22.8 %collective-permute-start.7 = (bf16[48,6272]{1,0:T(8,128)(2,1)S(1)}, bf16[48,6272]{1,0:T(8,128)(2,1)}, u32[]{:S(2)}, u32[]{:S(2)}) collective-permute-start(bf16[48,6272]{1,0:T(8,128)(2,1)S(1)} %collective-permute-done.refs_0_), channel_id=1, source_target_pairs={{12,0},{13,1},{14,2},{15,3},{0,4},{1,5},{2,6},{3,7},{4,8},{5,9},{6... | collective-permute-start | bytes 1806344 | tf_op jit(solution)/shard_map/ppermute | solution.py:267
  31.0 25.1 %all-to-all-start = ((bf16[16,16,768]{2,1,0:T(8,128)(2,1)}), bf16[16,16,768]{2,1,0:T(8,128)(2,1)S(1)}, u32[]{:S(2)}, u32[]{:S(2)}) async-start(bf16[16,16,768]{2,1,0:T(8,128)(2,1)} %project.4), calls=%async_computation | async-start | bytes 786432 | tf_op jit(solution)/shard_map/all_to_all | solution.py:283
  41.5 23.6 %collective-permute-start.8 = (bf16[48,6272]{1,0:T(8,128)(2,1)}, bf16[48,6272]{1,0:T(8,128)(2,1)}, u32[]{:S(2)}, u32[]{:S(2)}) collective-permute-start(bf16[48,6272]{1,0:T(8,128)(2,1)} %collective-permute-done.4.refs_0_), channel_id=1, source_target_pairs={{1,0},{2,1},{3,2},{0,3},{5,4},{6,5},{7,6},{4,7},{9,8},{10,9},{11,1... | collective-permute-start | bytes 1806344 | tf_op jit(solution)/shard_map/ppermute | solution.py:267
  44.5 23.5 %collective-permute-start.9 = (bf16[48,6272]{1,0:T(8,128)(2,1)}, bf16[48,6272]{1,0:T(8,128)(2,1)}, u32[]{:S(2)}, u32[]{:S(2)}) collective-permute-start(bf16[48,6272]{1,0:T(8,128)(2,1)} %collective-permute-done.6.refs_2_), channel_id=1, source_target_pairs={{3,0},{0,1},{1,2},{2,3},{7,4},{4,5},{5,6},{6,7},{11,8},{8,9},{9,10... | collective-permute-start | bytes 1806344 | tf_op jit(solution)/shard_map/ppermute | solution.py:267
  44.5 23.5 %collective-permute-start.10 = (bf16[48,6272]{1,0:T(8,128)(2,1)}, bf16[48,6272]{1,0:T(8,128)(2,1)}, u32[]{:S(2)}, u32[]{:S(2)}) collective-permute-start(bf16[48,6272]{1,0:T(8,128)(2,1)} %collective-permute-done.5.refs_1_), channel_id=1, source_target_pairs={{4,0},{5,1},{6,2},{7,3},{8,4},{9,5},{10,6},{11,7},{12,8},{13,9},{1... | collective-permute-start | bytes 1806344 | tf_op jit(solution)/shard_map/ppermute | solution.py:267
  47.5 20.5 %collective-permute-start.11 = (bf16[48,6272]{1,0:T(8,128)(2,1)}, bf16[48,6272]{1,0:T(8,128)(2,1)}, u32[]{:S(2)}, u32[]{:S(2)}) collective-permute-start(bf16[48,6272]{1,0:T(8,128)(2,1)} %collective-permute-done.7.refs_3_), channel_id=1, source_target_pairs={{12,0},{13,1},{14,2},{15,3},{0,4},{1,5},{2,6},{3,7},{4,8},{5,9},{6... | collective-permute-start | bytes 1806344 | tf_op jit(solution)/shard_map/ppermute | solution.py:267
  56.1 20.6 %all-to-all-start.1 = ((bf16[16,16,768]{2,1,0:T(8,128)(2,1)}), bf16[16,16,768]{2,1,0:T(8,128)(2,1)S(1)}, u32[]{:S(2)}, u32[]{:S(2)}) async-start(bf16[16,16,768]{2,1,0:T(8,128)(2,1)} %project.5), calls=%async_computation.1 | async-start | bytes 786432 | tf_op jit(solution)/shard_map/all_to_all | solution.py:283
  62.1 21.9 %copy-start = (bf16[48,6272]{1,0:T(8,128)(2,1)S(1)}, bf16[48,6272]{1,0:T(8,128)(2,1)}, u32[]{:S(2)}) copy-start(bf16[48,6272]{1,0:T(8,128)(2,1)} %mark_rows.1.refs_3_) | copy-start | bytes 1806340
  62.1 20.5 %collective-permute-start.12 = (bf16[48,6272]{1,0:T(8,128)(2,1)S(1)}, bf16[48,6272]{1,0:T(8,128)(2,1)}, u32[]{:S(2)}, u32[]{:S(2)}) collective-permute-start(bf16[48,6272]{1,0:T(8,128)(2,1)S(1)} %collective-permute-done.refs_0_), channel_id=1, source_target_pairs={{1,0},{2,1},{3,2},{0,3},{5,4},{6,5},{7,6},{4,7},{9,8},{10,9},{11,1... | collective-permute-start | bytes 1806344 | tf_op jit(solution)/shard_map/ppermute | solution.py:267
  65.1 17.5 %collective-permute-start.13 = (bf16[48,6272]{1,0:T(8,128)(2,1)S(1)}, bf16[48,6272]{1,0:T(8,128)(2,1)}, u32[]{:S(2)}, u32[]{:S(2)}) collective-permute-start(bf16[48,6272]{1,0:T(8,128)(2,1)S(1)} %collective-permute-done.2.refs_2_), channel_id=1, source_target_pairs={{4,0},{5,1},{6,2},{7,3},{8,4},{9,5},{10,6},{11,7},{12,8},{13,9},{1... | collective-permute-start | bytes 1806344 | tf_op jit(solution)/shard_map/ppermute | solution.py:267
  68.0 16.0 %collective-permute-start.14 = (bf16[48,6272]{1,0:T(8,128)(2,1)}, bf16[48,6272]{1,0:T(8,128)(2,1)}, u32[]{:S(2)}, u32[]{:S(2)}) collective-permute-start(bf16[48,6272]{1,0:T(8,128)(2,1)} %collective-permute-done.10.refs_2_), channel_id=1, source_target_pairs={{3,0},{0,1},{1,2},{2,3},{7,4},{4,5},{5,6},{6,7},{11,8},{8,9},{9,10... | collective-permute-start | bytes 1806344 | tf_op jit(solution)/shard_map/ppermute | solution.py:267
  76.7 20.5 %all-to-all-start.2 = ((bf16[16,16,768]{2,1,0:T(8,128)(2,1)}), bf16[16,16,768]{2,1,0:T(8,128)(2,1)S(1)}, u32[]{:S(2)}, u32[]{:S(2)}) async-start(bf16[16,16,768]{2,1,0:T(8,128)(2,1)} %project.6), calls=%async_computation.2 | async-start | bytes 786432 | tf_op jit(solution)/shard_map/all_to_all | solution.py:283
  82.6 18.4 %copy-start.1 = (s32[1,1024]{1,0:T(1,128)S(1)}, s32[1,1024]{1,0:T(1,128)}, u32[]{:S(2)}) copy-start(s32[1,1024]{1,0:T(1,128)} %refs_3_.1) | copy-start | bytes 12292
  97.2 17.4 %all-to-all-start.3 = ((bf16[16,16,768]{2,1,0:T(8,128)(2,1)}), bf16[16,16,768]{2,1,0:T(8,128)(2,1)S(1)}, u32[]{:S(2)}, u32[]{:S(2)}) async-start(bf16[16,16,768]{2,1,0:T(8,128)(2,1)} %project.7), calls=%async_computation.3 | async-start | bytes 786432 | tf_op jit(solution)/shard_map/all_to_all | solution.py:283

commit v5 on v4

--- a/solution.py
+++ b/solution.py
@@ -9,6 +9,7 @@
 SIDE = 4
 CAP = 4
 FILL = -1000000000.0
+LOG2E = 1.4426950408889634
 EMPTY = 1.0e15
 EDGE = 128
 STEPS = 2
@@ -193,10 +194,10 @@
                 q = qkv[rows, h * HD : (h + 1) * HD]
                 k = qkv[win, third + h * HD : third + (h + 1) * HD]
                 v = qkv[win, 2 * third + h * HD : 2 * third + (h + 1) * HD]
-                s = lax.dot_general(q, k, nt, preferred_element_type=f32) * scale
-                s = jnp.where(allowed, s, FILL)
+                s = lax.dot_general(q, k, nt, preferred_element_type=f32) * (scale * LOG2E)
+                s = jnp.where(allowed, s, FILL * LOG2E)
                 top = jnp.max(s, axis=1, keepdims=True)
-                e = jnp.exp(s - top)
+                e = jnp.exp2(s - top)
                 p = e * (1.0 / jnp.sum(e, axis=1, keepdims=True))
                 p_low = p.astype(jnp.bfloat16)
                 context = jnp.dot(p_low, v, preferred_element_type=f32)
@@ -218,7 +219,7 @@
             first, last = max(b - 1, 0), min(b + 2, blocks)
             work(b * block, first * block, (last - first) * block)
 
-        @pl.when(jnp.min(low[...]) < 0.5 * FILL)
+        @pl.when(jnp.min(low[...]) < 0.5 * FILL * LOG2E)
         def _():
             clear()
 

time: 127 us -> 127 us (level)
  no operation moved by 1% of the time
where the time goes in v5:
time: 127 us; the launch traced here: 126 us
  starting transfers between devices  49.7 us (39%)
  Pallas kernels  40.2 us (32%)
  waiting for transfers between devices  34.6 us (27%)
    pallas_call x4, Pallas kernels, project(): pl.pallas_call(body, grid=(STEPS,), in_specs=[full] * count + [pl.BlockSp...  26.3 us
    all_to_all x4, starting transfers between devices, per_device(): lax.all_to_all(placed, 'dp', split_axis=0, concat_axis=0, tiled=True)  26.2 us
    ppermute x15, starting transfers between devices, receive(): return lax.ppermute(block, 'seq', pairs)  23.5 us
    all_to_all x4, waiting for transfers between devices, per_device(): lax.all_to_all(placed, 'dp', split_axis=0, concat_axis=0, tiled=True)  22.8 us
    ppermute x15, waiting for transfers between devices, receive(): return lax.ppermute(block, 'seq', pairs)  11.8 us
    pallas_call x1, Pallas kernels, attention(): pl.pallas_call(body, in_specs=[vmem] * 2 + [pl.BlockSpec(memory_space=plt...  11.2 us
  transfers between devices with their start and end apart: 19, of which 7 were waited for; matrix products, arithmetic and copies ran while one was open for 0% of the time, Pallas kernels for 21%

profile of v5, /device:TPU:1, one launch (start us, length us, event | category | flops | bytes accessed | tf_op | source)
XLA Modules:
  0.0 126.0 jit_solution(10390260579482912323)
XLA Ops:
  0.6 2.2 %mark_rows.1.refs_3_ = bf16[48,6272]{1,0:T(8,128)(2,1)} custom-call(bf16[48,6144]{1,0:T(8,128)(2,1)} %x_ref.1, s32[1,48]{1,0:T(1,128)} %bitcast.29), custom_call_target="tpu_custom_call" | custom-call | tf_op jit(solution)/shard_map/mark_rows/pallas_call | solution.py:43
  2.8 3.6 %collective-permute-start.2 = (bf16[48,6272]{1,0:T(8,128)(2,1)}, bf16[48,6272]{1,0:T(8,128)(2,1)S(1)}, u32[]{:S(2)}, u32[]{:S(2)}) collective-permute-start(bf16[48,6272]{1,0:T(8,128)(2,1)} %mark_rows.1.refs_3_), channel_id=1, source_target_pairs={{4,0},{5,1},{6,2},{7,3},{8,4},{9,5},{10,6},{11,7},{12,8},{13,9},{1... | collective-permute-start | bytes 1806344 | tf_op jit(solution)/shard_map/ppermute | solution.py:268
  6.4 1.2 collective-permute-start.1
  7.6 0.0 collective-permute-start.3
  7.6 1.5 %collective-permute-start = (bf16[48,6272]{1,0:T(8,128)(2,1)}, bf16[48,6272]{1,0:T(8,128)(2,1)S(1)}, u32[]{:S(2)}, u32[]{:S(2)}) collective-permute-start(bf16[48,6272]{1,0:T(8,128)(2,1)} %mark_rows.1.refs_3_), channel_id=1, source_target_pairs={{1,0},{2,1},{3,2},{0,3},{5,4},{6,5},{7,6},{4,7},{9,8},{10,9},{11,1... | collective-permute-start | bytes 1806344 | tf_op jit(solution)/shard_map/ppermute | solution.py:268
  9.1 9.9 %collective-permute-done.2.refs_2_ = bf16[48,6272]{1,0:T(8,128)(2,1)S(1)} collective-permute-done((bf16[48,6272]{1,0:T(8,128)(2,1)}, bf16[48,6272]{1,0:T(8,128)(2,1)S(1)}, u32[]{:S(2)}, u32[]{:S(2)}) %collective-permute-start.2) | collective-permute-done | bytes 602144 | tf_op jit(solution)/shard_map/ppermute | solution.py:268
  19.0 2.5 %collective-permute-start.4 = (bf16[48,6272]{1,0:T(8,128)(2,1)S(1)}, bf16[48,6272]{1,0:T(8,128)(2,1)}, u32[]{:S(2)}, u32[]{:S(2)}) collective-permute-start(bf16[48,6272]{1,0:T(8,128)(2,1)S(1)} %collective-permute-done.2.refs_2_), channel_id=1, source_target_pairs={{1,0},{2,1},{3,2},{0,3},{5,4},{6,5},{7,6},{4,7},{9,8},{10,9},{11,1... | collective-permute-start | bytes 1806344 | tf_op jit(solution)/shard_map/ppermute | solution.py:268
  21.4 0.5 collective-permute-done.1.refs_1_
  21.9 2.8 %collective-permute-start.5 = (bf16[48,6272]{1,0:T(8,128)(2,1)S(1)}, bf16[48,6272]{1,0:T(8,128)(2,1)}, u32[]{:S(2)}, u32[]{:S(2)}) collective-permute-start(bf16[48,6272]{1,0:T(8,128)(2,1)S(1)} %collective-permute-done.1.refs_1_), channel_id=1, source_target_pairs={{4,0},{5,1},{6,2},{7,3},{8,4},{9,5},{10,6},{11,7},{12,8},{13,9},{1... | collective-permute-start | bytes 1806344 | tf_op jit(solution)/shard_map/ppermute | solution.py:268
  24.7 0.0 collective-permute-done.3.refs_3_
  24.8 0.0 collective-permute-start.6
  24.8 0.0 collective-permute-done.refs_0_
  24.8 0.1 collective-permute-start.7
  24.9 6.1 %project.4 = bf16[16,16,768]{2,1,0:T(8,128)(2,1)} custom-call(bf16[48,6272]{1,0:T(8,128)(2,1)S(1)} %collective-permute-done.refs_0_, bf16[48,6272]{1,0:T(8,128)(2,1)S(1)} %collective-permute-done.1.refs_1_, bf16[48,6272]{1,0:T(8,128)(2,1)S(1)} %collective-permute-done.2.refs_2_, bf16[48,6272]{1,0:T(8,128)(2,1)S(1)} %collective-permute-done.3.refs_3_, ...), custom_call_target="tpu_custom_call" | custom-call | flops 1811939328 | bytes 11796480 | tf_op jit(solution)/shard_map/project/pallas_call | solution.py:93
  31.0 10.6 %all-to-all-start = ((bf16[16,16,768]{2,1,0:T(8,128)(2,1)}), bf16[16,16,768]{2,1,0:T(8,128)(2,1)S(1)}, u32[]{:S(2)}, u32[]{:S(2)}) async-start(bf16[16,16,768]{2,1,0:T(8,128)(2,1)} %project.4), calls=%async_computation | async-start | bytes 786432 | tf_op jit(solution)/shard_map/all_to_all | solution.py:284
  41.5 0.0 collective-permute-done.4.refs_0_
  41.5 3.0 %collective-permute-start.8 = (bf16[48,6272]{1,0:T(8,128)(2,1)}, bf16[48,6272]{1,0:T(8,128)(2,1)}, u32[]{:S(2)}, u32[]{:S(2)}) collective-permute-start(bf16[48,6272]{1,0:T(8,128)(2,1)} %collective-permute-done.4.refs_0_), channel_id=1, source_target_pairs={{1,0},{2,1},{3,2},{0,3},{5,4},{6,5},{7,6},{4,7},{9,8},{10,9},{11,1... | collective-permute-start | bytes 1806344 | tf_op jit(solution)/shard_map/ppermute | solution.py:268
  44.5 0.0 collective-permute-done.6.refs_2_
  44.5 0.0 collective-permute-start.9
  44.5 0.0 collective-permute-done.5.refs_1_
  44.5 3.0 %collective-permute-start.10 = (bf16[48,6272]{1,0:T(8,128)(2,1)}, bf16[48,6272]{1,0:T(8,128)(2,1)}, u32[]{:S(2)}, u32[]{:S(2)}) collective-permute-start(bf16[48,6272]{1,0:T(8,128)(2,1)} %collective-permute-done.5.refs_1_), channel_id=1, source_target_pairs={{4,0},{5,1},{6,2},{7,3},{8,4},{9,5},{10,6},{11,7},{12,8},{13,9},{1... | collective-permute-start | bytes 1806344 | tf_op jit(solution)/shard_map/ppermute | solution.py:268
  47.5 0.0 collective-permute-done.7.refs_3_
  47.5 0.0 collective-permute-start.11
  47.5 6.8 %project.5 = bf16[16,16,768]{2,1,0:T(8,128)(2,1)} custom-call(bf16[48,6272]{1,0:T(8,128)(2,1)} %collective-permute-done.4.refs_0_, bf16[48,6272]{1,0:T(8,128)(2,1)} %collective-permute-done.5.refs_1_, bf16[48,6272]{1,0:T(8,128)(2,1)} %collective-permute-done.6.refs_2_, bf16[48,6272]{1,0:T(8,128)(2,1)} %collective-permute-done.7.refs_3_, ...), custom_call_target="tpu_custom_call" | custom-call | flops 1811939328 | bytes 11796480 | tf_op jit(solution)/shard_map/project/pallas_call | solution.py:93
  54.4 1.7 %all-to-all-done.refs_0_ = bf16[16,16,768]{2,1,0:T(8,128)(2,1)S(1)} async-done(((bf16[16,16,768]{2,1,0:T(8,128)(2,1)}), bf16[16,16,768]{2,1,0:T(8,128)(2,1)S(1)}, u32[]{:S(2)}, u32[]{:S(2)}) %all-to-all-start) | async-done | bytes 393248 | tf_op jit(solution)/shard_map/all_to_all | solution.py:284
  56.1 6.0 %all-to-all-start.1 = ((bf16[16,16,768]{2,1,0:T(8,128)(2,1)}), bf16[16,16,768]{2,1,0:T(8,128)(2,1)S(1)}, u32[]{:S(2)}, u32[]{:S(2)}) async-start(bf16[16,16,768]{2,1,0:T(8,128)(2,1)} %project.5), calls=%async_computation.1 | async-start | bytes 786432 | tf_op jit(solution)/shard_map/all_to_all | solution.py:284
  62.1 0.0 copy-start
  62.1 3.0 %collective-permute-start.12 = (bf16[48,6272]{1,0:T(8,128)(2,1)S(1)}, bf16[48,6272]{1,0:T(8,128)(2,1)}, u32[]{:S(2)}, u32[]{:S(2)}) collective-permute-start(bf16[48,6272]{1,0:T(8,128)(2,1)S(1)} %collective-permute-done.refs_0_), channel_id=1, source_target_pairs={{1,0},{2,1},{3,2},{0,3},{5,4},{6,5},{7,6},{4,7},{9,8},{10,9},{11,1... | collective-permute-start | bytes 1806344 | tf_op jit(solution)/shard_map/ppermute | solution.py:268
  65.1 0.0 collective-permute-done.8.refs_0_
  65.1 2.9 %collective-permute-start.13 = (bf16[48,6272]{1,0:T(8,128)(2,1)S(1)}, bf16[48,6272]{1,0:T(8,128)(2,1)}, u32[]{:S(2)}, u32[]{:S(2)}) collective-permute-start(bf16[48,6272]{1,0:T(8,128)(2,1)S(1)} %collective-permute-done.2.refs_2_), channel_id=1, source_target_pairs={{4,0},{5,1},{6,2},{7,3},{8,4},{9,5},{10,6},{11,7},{12,8},{13,9},{1... | collective-permute-start | bytes 1806344 | tf_op jit(solution)/shard_map/ppermute | solution.py:268
  68.0 0.0 collective-permute-done.10.refs_2_
  68.0 0.0 collective-permute-start.14
  68.0 0.0 collective-permute-done.9.refs_1_
  68.0 0.0 collective-permute-done.11.refs_3_
  68.1 6.8 %project.6 = bf16[16,16,768]{2,1,0:T(8,128)(2,1)} custom-call(bf16[48,6272]{1,0:T(8,128)(2,1)} %collective-permute-done.8.refs_0_, bf16[48,6272]{1,0:T(8,128)(2,1)} %collective-permute-done.9.refs_1_, bf16[48,6272]{1,0:T(8,128)(2,1)} %collective-permute-done.10.refs_2_, bf16[48,6272]{1,0:T(8,128)(2,1)} %collective-permute-done.11.refs_3_, ...), custom_call_target="tpu_custom_call" | custom-call | flops 1811939328 | bytes 11796480 | tf_op jit(solution)/shard_map/project/pallas_call | solution.py:93
  74.9 1.8 %all-to-all-done.1.refs_1_ = bf16[16,16,768]{2,1,0:T(8,128)(2,1)S(1)} async-done(((bf16[16,16,768]{2,1,0:T(8,128)(2,1)}), bf16[16,16,768]{2,1,0:T(8,128)(2,1)S(1)}, u32[]{:S(2)}, u32[]{:S(2)}) %all-to-all-start.1) | async-done | bytes 393248 | tf_op jit(solution)/shard_map/all_to_all | solution.py:284
  76.7 6.0 %all-to-all-start.2 = ((bf16[16,16,768]{2,1,0:T(8,128)(2,1)}), bf16[16,16,768]{2,1,0:T(8,128)(2,1)S(1)}, u32[]{:S(2)}, u32[]{:S(2)}) async-start(bf16[16,16,768]{2,1,0:T(8,128)(2,1)} %project.6), calls=%async_computation.2 | async-start | bytes 786432 | tf_op jit(solution)/shard_map/all_to_all | solution.py:284
  82.6 0.0 copy-start.1
  82.6 0.0 collective-permute-done.12.refs_0_
  82.7 0.0 collective-permute-done.13.refs_1_
  82.7 1.4 %collective-permute-done.14.refs_2_ = bf16[48,6272]{1,0:T(8,128)(2,1)} collective-permute-done((bf16[48,6272]{1,0:T(8,128)(2,1)}, bf16[48,6272]{1,0:T(8,128)(2,1)}, u32[]{:S(2)}, u32[]{:S(2)}) %collective-permute-start.14) | collective-permute-done | bytes 602144 | tf_op jit(solution)/shard_map/ppermute | solution.py:268
  84.1 0.0 copy-done
  84.1 6.6 %project.7 = bf16[16,16,768]{2,1,0:T(8,128)(2,1)} custom-call(bf16[48,6272]{1,0:T(8,128)(2,1)} %collective-permute-done.12.refs_0_, bf16[48,6272]{1,0:T(8,128)(2,1)} %collective-permute-done.13.refs_1_, bf16[48,6272]{1,0:T(8,128)(2,1)} %collective-permute-done.14.refs_2_, bf16[48,6272]{1,0:T(8,128)(2,1)S(1)} %copy-done, bf16[3,6144,256]{2,1,0:T(8,128)(2,1)} %bitcast.28), custom_call_target="tpu_custom_call" | custom-call | flops 1811939328 | bytes 11796480 | tf_op jit(solution)/shard_map/project/pallas_call | solution.py:93
  90.7 6.5 %all-to-all-done.2.refs_2_ = bf16[16,16,768]{2,1,0:T(8,128)(2,1)S(1)} async-done(((bf16[16,16,768]{2,1,0:T(8,128)(2,1)}), bf16[16,16,768]{2,1,0:T(8,128)(2,1)S(1)}, u32[]{:S(2)}, u32[]{:S(2)}) %all-to-all-start.2) | async-done | bytes 393248 | tf_op jit(solution)/shard_map/all_to_all | solution.py:284
  97.2 3.7 %all-to-all-start.3 = ((bf16[16,16,768]{2,1,0:T(8,128)(2,1)}), bf16[16,16,768]{2,1,0:T(8,128)(2,1)S(1)}, u32[]{:S(2)}, u32[]{:S(2)}) async-start(bf16[16,16,768]{2,1,0:T(8,128)(2,1)} %project.7), calls=%async_computation.3 | async-start | bytes 786432 | tf_op jit(solution)/shard_map/all_to_all | solution.py:284
  101.0 0.0 copy-done.1
  101.0 0.2 copy.7.refs_4_
  101.2 0.1 stack.67.refs_2_
  101.3 0.5 assemble.1.refs_0_
  101.8 12.8 %all-to-all-done.3.refs_1_ = bf16[16,16,768]{2,1,0:T(8,128)(2,1)S(1)} async-done(((bf16[16,16,768]{2,1,0:T(8,128)(2,1)}), bf16[16,16,768]{2,1,0:T(8,128)(2,1)S(1)}, u32[]{:S(2)}, u32[]{:S(2)}) %all-to-all-start.3) | async-done | bytes 393248 | tf_op jit(solution)/shard_map/all_to_all | solution.py:284
  114.6 11.2 %attention.1 = (bf16[1024,256]{1,0:T(8,128)(2,1)}, bf16[3,1024,256]{2,1,0:T(8,128)(2,1)}) custom-call(bf16[768,768]{1,0:T(8,128)(2,1)S(1)} %assemble.1.refs_0_, bf16[16,16,768]{2,1,0:T(8,128)(2,1)S(1)} %all-to-all-done.3.refs_1_, s32[16]{0:T(128)S(1)} %stack.67.refs_2_, s32[1,1024]{1,0:T(1,128)S(1)} %copy-done.1, s32[1024,1]{1,0:T(8,128)S(1)} %copy.7.refs_4_, ...), custom_call_target="tpu_custom_call" | custom-call | flops 3221225472 | bytes 8388608 | tf_op jit(solution)/shard_map/attention/pallas_call | solution.py:236
Async XLA Ops:
  2.8 16.1 %collective-permute-start.2 = (bf16[48,6272]{1,0:T(8,128)(2,1)}, bf16[48,6272]{1,0:T(8,128)(2,1)S(1)}, u32[]{:S(2)}, u32[]{:S(2)}) collective-permute-start(bf16[48,6272]{1,0:T(8,128)(2,1)} %mark_rows.1.refs_3_), channel_id=1, source_target_pairs={{4,0},{5,1},{6,2},{7,3},{8,4},{9,5},{10,6},{11,7},{12,8},{13,9},{1... | collective-permute-start | bytes 1806344 | tf_op jit(solution)/shard_map/ppermute | solution.py:268
  6.4 15.6 %collective-permute-start.1 = (bf16[48,6272]{1,0:T(8,128)(2,1)}, bf16[48,6272]{1,0:T(8,128)(2,1)S(1)}, u32[]{:S(2)}, u32[]{:S(2)}) collective-permute-start(bf16[48,6272]{1,0:T(8,128)(2,1)} %mark_rows.1.refs_3_), channel_id=1, source_target_pairs={{3,0},{0,1},{1,2},{2,3},{7,4},{4,5},{5,6},{6,7},{11,8},{8,9},{9,10... | collective-permute-start | bytes 1806344 | tf_op jit(solution)/shard_map/ppermute | solution.py:268
  7.6 17.2 %collective-permute-start.3 = (bf16[48,6272]{1,0:T(8,128)(2,1)}, bf16[48,6272]{1,0:T(8,128)(2,1)S(1)}, u32[]{:S(2)}, u32[]{:S(2)}) collective-permute-start(bf16[48,6272]{1,0:T(8,128)(2,1)} %mark_rows.1.refs_3_), channel_id=1, source_target_pairs={{12,0},{13,1},{14,2},{15,3},{0,4},{1,5},{2,6},{3,7},{4,8},{5,9},{6... | collective-permute-start | bytes 1806344 | tf_op jit(solution)/shard_map/ppermute | solution.py:268
  7.6 17.2 %collective-permute-start = (bf16[48,6272]{1,0:T(8,128)(2,1)}, bf16[48,6272]{1,0:T(8,128)(2,1)S(1)}, u32[]{:S(2)}, u32[]{:S(2)}) collective-permute-start(bf16[48,6272]{1,0:T(8,128)(2,1)} %mark_rows.1.refs_3_), channel_id=1, source_target_pairs={{1,0},{2,1},{3,2},{0,3},{5,4},{6,5},{7,6},{4,7},{9,8},{10,9},{11,1... | collective-permute-start | bytes 1806344 | tf_op jit(solution)/shard_map/ppermute | solution.py:268
  19.0 22.6 %collective-permute-start.4 = (bf16[48,6272]{1,0:T(8,128)(2,1)S(1)}, bf16[48,6272]{1,0:T(8,128)(2,1)}, u32[]{:S(2)}, u32[]{:S(2)}) collective-permute-start(bf16[48,6272]{1,0:T(8,128)(2,1)S(1)} %collective-permute-done.2.refs_2_), channel_id=1, source_target_pairs={{1,0},{2,1},{3,2},{0,3},{5,4},{6,5},{7,6},{4,7},{9,8},{10,9},{11,1... | collective-permute-start | bytes 1806344 | tf_op jit(solution)/shard_map/ppermute | solution.py:268
  21.9 22.6 %collective-permute-start.5 = (bf16[48,6272]{1,0:T(8,128)(2,1)S(1)}, bf16[48,6272]{1,0:T(8,128)(2,1)}, u32[]{:S(2)}, u32[]{:S(2)}) collective-permute-start(bf16[48,6272]{1,0:T(8,128)(2,1)S(1)} %collective-permute-done.1.refs_1_), channel_id=1, source_target_pairs={{4,0},{5,1},{6,2},{7,3},{8,4},{9,5},{10,6},{11,7},{12,8},{13,9},{1... | collective-permute-start | bytes 1806344 | tf_op jit(solution)/shard_map/ppermute | solution.py:268
  24.8 19.8 %collective-permute-start.6 = (bf16[48,6272]{1,0:T(8,128)(2,1)S(1)}, bf16[48,6272]{1,0:T(8,128)(2,1)}, u32[]{:S(2)}, u32[]{:S(2)}) collective-permute-start(bf16[48,6272]{1,0:T(8,128)(2,1)S(1)} %collective-permute-done.3.refs_3_), channel_id=1, source_target_pairs={{3,0},{0,1},{1,2},{2,3},{7,4},{4,5},{5,6},{6,7},{11,8},{8,9},{9,10... | collective-permute-start | bytes 1806344 | tf_op jit(solution)/shard_map/ppermute | solution.py:268
  24.8 22.8 %collective-permute-start.7 = (bf16[48,6272]{1,0:T(8,128)(2,1)S(1)}, bf16[48,6272]{1,0:T(8,128)(2,1)}, u32[]{:S(2)}, u32[]{:S(2)}) collective-permute-start(bf16[48,6272]{1,0:T(8,128)(2,1)S(1)} %collective-permute-done.refs_0_), channel_id=1, source_target_pairs={{12,0},{13,1},{14,2},{15,3},{0,4},{1,5},{2,6},{3,7},{4,8},{5,9},{6... | collective-permute-start | bytes 1806344 | tf_op jit(solution)/shard_map/ppermute | solution.py:268
  31.0 25.1 %all-to-all-start = ((bf16[16,16,768]{2,1,0:T(8,128)(2,1)}), bf16[16,16,768]{2,1,0:T(8,128)(2,1)S(1)}, u32[]{:S(2)}, u32[]{:S(2)}) async-start(bf16[16,16,768]{2,1,0:T(8,128)(2,1)} %project.4), calls=%async_computation | async-start | bytes 786432 | tf_op jit(solution)/shard_map/all_to_all | solution.py:284
  41.5 23.6 %collective-permute-start.8 = (bf16[48,6272]{1,0:T(8,128)(2,1)}, bf16[48,6272]{1,0:T(8,128)(2,1)}, u32[]{:S(2)}, u32[]{:S(2)}) collective-permute-start(bf16[48,6272]{1,0:T(8,128)(2,1)} %collective-permute-done.4.refs_0_), channel_id=1, source_target_pairs={{1,0},{2,1},{3,2},{0,3},{5,4},{6,5},{7,6},{4,7},{9,8},{10,9},{11,1... | collective-permute-start | bytes 1806344 | tf_op jit(solution)/shard_map/ppermute | solution.py:268
  44.5 23.5 %collective-permute-start.9 = (bf16[48,6272]{1,0:T(8,128)(2,1)}, bf16[48,6272]{1,0:T(8,128)(2,1)}, u32[]{:S(2)}, u32[]{:S(2)}) collective-permute-start(bf16[48,6272]{1,0:T(8,128)(2,1)} %collective-permute-done.6.refs_2_), channel_id=1, source_target_pairs={{3,0},{0,1},{1,2},{2,3},{7,4},{4,5},{5,6},{6,7},{11,8},{8,9},{9,10... | collective-permute-start | bytes 1806344 | tf_op jit(solution)/shard_map/ppermute | solution.py:268
  44.5 23.5 %collective-permute-start.10 = (bf16[48,6272]{1,0:T(8,128)(2,1)}, bf16[48,6272]{1,0:T(8,128)(2,1)}, u32[]{:S(2)}, u32[]{:S(2)}) collective-permute-start(bf16[48,6272]{1,0:T(8,128)(2,1)} %collective-permute-done.5.refs_1_), channel_id=1, source_target_pairs={{4,0},{5,1},{6,2},{7,3},{8,4},{9,5},{10,6},{11,7},{12,8},{13,9},{1... | collective-permute-start | bytes 1806344 | tf_op jit(solution)/shard_map/ppermute | solution.py:268
  47.5 20.5 %collective-permute-start.11 = (bf16[48,6272]{1,0:T(8,128)(2,1)}, bf16[48,6272]{1,0:T(8,128)(2,1)}, u32[]{:S(2)}, u32[]{:S(2)}) collective-permute-start(bf16[48,6272]{1,0:T(8,128)(2,1)} %collective-permute-done.7.refs_3_), channel_id=1, source_target_pairs={{12,0},{13,1},{14,2},{15,3},{0,4},{1,5},{2,6},{3,7},{4,8},{5,9},{6... | collective-permute-start | bytes 1806344 | tf_op jit(solution)/shard_map/ppermute | solution.py:268
  56.1 20.6 %all-to-all-start.1 = ((bf16[16,16,768]{2,1,0:T(8,128)(2,1)}), bf16[16,16,768]{2,1,0:T(8,128)(2,1)S(1)}, u32[]{:S(2)}, u32[]{:S(2)}) async-start(bf16[16,16,768]{2,1,0:T(8,128)(2,1)} %project.5), calls=%async_computation.1 | async-start | bytes 786432 | tf_op jit(solution)/shard_map/all_to_all | solution.py:284
  62.1 21.9 %copy-start = (bf16[48,6272]{1,0:T(8,128)(2,1)S(1)}, bf16[48,6272]{1,0:T(8,128)(2,1)}, u32[]{:S(2)}) copy-start(bf16[48,6272]{1,0:T(8,128)(2,1)} %mark_rows.1.refs_3_) | copy-start | bytes 1806340
  62.1 20.5 %collective-permute-start.12 = (bf16[48,6272]{1,0:T(8,128)(2,1)S(1)}, bf16[48,6272]{1,0:T(8,128)(2,1)}, u32[]{:S(2)}, u32[]{:S(2)}) collective-permute-start(bf16[48,6272]{1,0:T(8,128)(2,1)S(1)} %collective-permute-done.refs_0_), channel_id=1, source_target_pairs={{1,0},{2,1},{3,2},{0,3},{5,4},{6,5},{7,6},{4,7},{9,8},{10,9},{11,1... | collective-permute-start | bytes 1806344 | tf_op jit(solution)/shard_map/ppermute | solution.py:268
  65.1 17.5 %collective-permute-start.13 = (bf16[48,6272]{1,0:T(8,128)(2,1)S(1)}, bf16[48,6272]{1,0:T(8,128)(2,1)}, u32[]{:S(2)}, u32[]{:S(2)}) collective-permute-start(bf16[48,6272]{1,0:T(8,128)(2,1)S(1)} %collective-permute-done.2.refs_2_), channel_id=1, source_target_pairs={{4,0},{5,1},{6,2},{7,3},{8,4},{9,5},{10,6},{11,7},{12,8},{13,9},{1... | collective-permute-start | bytes 1806344 | tf_op jit(solution)/shard_map/ppermute | solution.py:268
  68.0 16.0 %collective-permute-start.14 = (bf16[48,6272]{1,0:T(8,128)(2,1)}, bf16[48,6272]{1,0:T(8,128)(2,1)}, u32[]{:S(2)}, u32[]{:S(2)}) collective-permute-start(bf16[48,6272]{1,0:T(8,128)(2,1)} %collective-permute-done.10.refs_2_), channel_id=1, source_target_pairs={{3,0},{0,1},{1,2},{2,3},{7,4},{4,5},{5,6},{6,7},{11,8},{8,9},{9,10... | collective-permute-start | bytes 1806344 | tf_op jit(solution)/shard_map/ppermute | solution.py:268
  76.7 20.5 %all-to-all-start.2 = ((bf16[16,16,768]{2,1,0:T(8,128)(2,1)}), bf16[16,16,768]{2,1,0:T(8,128)(2,1)S(1)}, u32[]{:S(2)}, u32[]{:S(2)}) async-start(bf16[16,16,768]{2,1,0:T(8,128)(2,1)} %project.6), calls=%async_computation.2 | async-start | bytes 786432 | tf_op jit(solution)/shard_map/all_to_all | solution.py:284
  82.6 18.4 %copy-start.1 = (s32[1,1024]{1,0:T(1,128)S(1)}, s32[1,1024]{1,0:T(1,128)}, u32[]{:S(2)}) copy-start(s32[1,1024]{1,0:T(1,128)} %refs_3_.1) | copy-start | bytes 12292
  97.2 17.4 %all-to-all-start.3 = ((bf16[16,16,768]{2,1,0:T(8,128)(2,1)}), bf16[16,16,768]{2,1,0:T(8,128)(2,1)S(1)}, u32[]{:S(2)}, u32[]{:S(2)}) async-start(bf16[16,16,768]{2,1,0:T(8,128)(2,1)} %project.7), calls=%async_computation.3 | async-start | bytes 786432 | tf_op jit(solution)/shard_map/all_to_all | solution.py:284
